TPU v7x, 128 devices: a whole 4x4x4 slice. The times are simulated.
128 devices in a mesh: seq: 16 (over x_hi, y, core), chan: 8 (over z, x_lo).
Axes of the slice: x: 4 (x_hi: 2, x_lo: 2; x = x_hi * 2 + x_lo), y: 4, z: 4, core: 2. Of those that a mesh axis runs over, the one named last changes fastest.
Arguments:
- out_grad: bfloat16 [8192, 8192], P('seq', 'chan'), may hold values from -6 to 6
- out_weight: bfloat16 [1024, 8192], P(None, 'chan'), may hold values from -0.0625 to 0.0625
- conv_input: bfloat16 [1024, 8192], P('chan', 'seq'), may hold values from -6 to 6
- gate_values: bfloat16 [1024, 8192], P('chan', 'seq'), may hold values from -6 to 6
- conv_output: bfloat16 [1024, 8192], P('chan', 'seq'), may hold values from -6 to 6
- filters: bfloat16 [2, 1024, 512], P(None, 'chan'), may hold values from -0.29882812 to 0.29882812
- filter_reach: int32 [16], replicated, may hold values from 128 to 512, as said below
Outputs:
- grad_input: float32 [1024, 8192], P('chan', 'seq')
- grad_gate: float32 [1024, 8192], P('chan', 'seq')
- grad_weight: float32 [1024, 8192], P('seq', 'chan')
- grad_filters: float32 [2, 1024, 512], P(None, 'chan', 'seq')
Inputs may be any that keep to these rules, and one draw needn't show every extreme that they name: `filter_reach`: group g holds channels g * 64 to (g + 1) * 64 - 1. Every reach is a multiple of 128, and at least one group has reach 512.
All inputs are finite; a program needn't handle non-finite values.
Results may differ from a plain program's by a relative error of at most 0.014.
Values may be sent and summed in bfloat16 or wider, within the bound.
No kernel may reach another device: no remote copies, remote signals or barrier semaphores. Data moves between devices by JAX's collectives and lax.ppermute only.
A program may use at most 128 MiB of HBM per device.

v0:
```python
import functools

import jax
import jax.numpy as jnp
from jax import lax
from jax.experimental import pallas as pl
from jax.experimental.pallas import tpu as pltpu
from jax.sharding import PartitionSpec as P


GROUP = 64
VN = 32
F32 = jnp.float32
BF16 = jnp.bfloat16


def iota(shape, dim):
    return lax.broadcasted_iota(jnp.int32, shape, dim)


def dot(a, b, dims=(((1,), (0,)), ((), ()))):
    return lax.dot_general(a, b, dims, preferred_element_type=F32)


NT = (((1,), (1,)), ((), ()))


RELS = (0, 1, 3, 2)


def gate_rows(pos_ref, v_ref, g_ref, mine, other):
    half = mine.shape[0]
    core = pos_ref[4] % 2
    for ref, part in ((mine, core), (other, 1 - core)):
        band = pl.ds(pl.multiple_of(part * half, half), half)
        ref[...] = (v_ref[band, :].astype(F32) * g_ref[band, :].astype(F32)).astype(BF16)


def first_product(pos_ref, w_ref, og_ref, *outs):
    z = pos_ref[0]
    x = pos_ref[1]
    og = og_ref[...]
    for ref, rel in zip(outs, RELS):
        for a in range(2):
            row = ((z ^ rel) * 2 + (x ^ a)) * 128
            ref[128 * a : 128 * (a + 1), :] = dot(w_ref[pl.ds(row, 128), :], og, NT).astype(BF16)


def second_product(pos_ref, b0, b1, b3, b2, bx, og_ref, ogs_ref, *refs):
    outs, g_ref = refs[:4], refs[4]
    for i, ref in enumerate((b0, b1, b2, b3)):
        g_ref[i] = ref[...]
        g_ref[4 + i] = bx[i]
    z = pos_ref[0]
    x = pos_ref[1]
    xh = pos_ref[2]
    y = pos_ref[3]
    tok = og_ref.shape[0]
    for ref, rel in zip(outs, RELS):
        for a in range(2):
            j = (xh ^ a) * 4 + (y ^ rel)
            g = g_ref[((j % 2) ^ x) * 4 + ((j // 2) ^ z)]
            ref[a] = (dot(g[:, :tok], og_ref[...]) + dot(g[:, tok:], ogs_ref[...])).astype(BF16)


def conv_grads(pos_ref, reach_ref, gm_ref, gs_ref, gp_ref, f_ref, x_ref, o_ref, t_ref, h_ref, u_ref):
    rows, n = gm_ref.shape
    width = 3 * n
    chan = pos_ref[0] * 2 + pos_ref[1]
    place = pos_ref[4]
    core0 = place % 2 == 0
    own_rows = iota((128, 256), 0) % 8 == iota((128, 256), 1) % 8
    own_cols = iota((16, 8, 256), 1) == iota((16, 8, 256), 2) % 8
    ef = (iota((128, 256), 0) == iota((128, 256), 1) // 8).astype(BF16)
    eb = (iota((128, 256), 0) == (VN - 1) - iota((128, 256), 1) // 8).astype(BF16)
    taps = f_ref.shape[2]
    lag = iota((8, taps), 1)

    def step(i, carry):
        base = pl.multiple_of(i * 16, 16)
        band = pl.ds(base, 16)
        gm = gm_ref[band, :].astype(F32)
        gs = gs_ref[band, :].astype(F32)
        gp = gp_ref[band, :].astype(F32)
        gl = jnp.where(core0, gp, gs)
        gr = jnp.where(core0, gs, gp)
        ext16 = jnp.concatenate([gl, gm, gr], axis=1)
        own16 = x_ref[band, :].astype(F32)
        filt16 = [f_ref[d, band, :].astype(F32) for d in range(2)]
        inside = lag < reach_ref[(chan * rows + base) // GROUP]
        zero = jnp.zeros((8, n), F32)
        outs = []
        for h in range(2):
            ext = ext16[8 * h : 8 * h + 8]
            for k in range(VN // 2):
                pair = [ext if v == 0 else pltpu.roll(ext, width - v, 1) for v in (2 * k, 2 * k + 1)]
                h_ref[h, 16 * k : 16 * k + 16, :] = jnp.concatenate(pair, axis=0).astype(BF16)
            lhs = []
            for d, e in ((0, ef), (1, eb)):
                f8 = jnp.where(inside, filt16[d][8 * h : 8 * h + 8], 0.0)
                rolled = [f8 if b == 0 else pltpu.roll(f8, taps - 32 * b, 1) for b in range(4)]
                cut = [rolled[u % 4][:, 128 * (u // 4) : 128 * (u // 4) + 128] for u in range(16)]
                spread = dot(jnp.concatenate(cut, axis=0).astype(BF16), e)
                lhs.append(jnp.where(own_rows, spread, 0.0).astype(BF16))
            pf = dot(lhs[0], h_ref[h, :, n : 3 * n])
            pb = dot(lhs[1], h_ref[h, :, 0 : 2 * n])
            total = None
            for b in range(4):
                acc = None
                for a in range(4):
                    u = 4 * a + b
                    part = pf[8 * u : 8 * u + 8, 128 * a : 128 * a + n + 128]
                    acc = part if acc is None else acc + part
                if b:
                    acc = pltpu.roll(acc, n + 128 - 32 * b, 1)
                acc = acc[:, :n]
                total = acc if total is None else total + acc
            for b in range(4):
                acc = None
                for a in range(1, 5) if b == 0 else range(4):
                    u = 4 * a + b - 1
                    start = n - 128 - 128 * a
                    if b == 0:
                        part = pb[8 * u : 8 * u + 8, start + 128 : start + 128 + n]
                    else:
                        part = pb[8 * u : 8 * u + 8, start : start + n + 128]
                    acc = part if acc is None else acc + part
                if b:
                    acc = pltpu.roll(acc, 32 * b, 1)[:, 128:]
                total = total + acc
            outs.append(total)
            own = jnp.concatenate([zero, own16[8 * h : 8 * h + 8], zero], axis=1)
            later = [own if b == 0 else pltpu.roll(own, 32 * b, 1) for b in range(4)]
            sooner = [own if b == 0 else pltpu.roll(own, width - 32 * b, 1) for b in range(4)]
            for d in range(2):
                for k in range(8):
                    pair = []
                    for u in (2 * k, 2 * k + 1):
                        if d == 0:
                            start = n - 128 * (u // 4)
                            pair.append(later[u % 4][:, start : start + 2 * n])
                        else:
                            start = 128 * ((u + 1) // 4)
                            pair.append(sooner[(u + 1) % 4][:, start : start + 2 * n])
                    u_ref[h, d, 16 * k : 16 * k + 16, :] = jnp.concatenate(pair, axis=0).astype(BF16)
            for d in range(2):
                start = n * (1 - d)
                cross = dot(u_ref[h, d], h_ref[h, :, start : start + 2 * n], NT)
                sums = jnp.sum(jnp.where(own_cols, cross.reshape(16, 8, 256), 0.0), axis=1)
                row = d * (rows // 8) + 2 * i + h
                for u in range(16):
                    r = u ^ place
                    slot = (r % 2) * 8 + ((r // 2) % 4) * 2 + r // 8
                    t_ref[slot, pl.ds(row, 1), :] = sums[u : u + 1]
        o_ref[band, :] = jnp.concatenate(outs, axis=0)
        return carry

    lax.fori_loop(0, rows // 16, step, 0)


def split_taps(t_ref, got_ref, k, s1, s3, s2):
    for rel, ref in ((0, k), (1, s1), (3, s3), (2, s2)):
        both = t_ref[2 * rel : 2 * rel + 2] + got_ref[2 * rel : 2 * rel + 2].astype(F32)
        ref[...] = both.astype(ref.dtype)


def last_send(ek, e1, e3, e2, fk, f1, f3, f2, o_ref):
    e = ek[1].astype(F32)
    for ref in (e1, e3, e2):
        e = e + ref[1].astype(F32)
    f = fk[1]
    for ref in (f1, f3, f2):
        f = f + ref[1].astype(F32)
    n = f.shape[0] // 4
    o_ref[0 : e.shape[0], :] = e.astype(BF16)
    tail = jnp.concatenate([f[n * i : n * i + n] for i in range(4)], axis=1)
    o_ref[e.shape[0] :, :] = jnp.concatenate([tail, tail], axis=0).astype(BF16)


def finish(pos_ref, reach_ref, ek, e1, e3, e2, fk, f1, f3, f2, got, w_ref, t_ref, *, scale):
    e = ek[0].astype(F32)
    for ref in (e1, e3, e2):
        e = e + ref[0].astype(F32)
    m = e.shape[0]
    w_ref[...] = (e + got[0:m, :].astype(F32)) * scale
    f = fk[0]
    for ref in (f1, f3, f2):
        f = f + ref[0].astype(F32)
    n = f.shape[0] // 4
    tail = got[m:, :].astype(F32)[0:n]
    wide = f.shape[1]
    f = f + jnp.concatenate([tail[:, wide * i : wide * i + wide] for i in range(4)], axis=0)
    chan = pos_ref[0] * 2 + pos_ref[1]
    place = pos_ref[4]
    own_cols = iota((16, 8, 256), 1) == iota((16, 8, 256), 2) % 8
    row = iota((128, VN), 0)
    first = chan * 128 // GROUP
    limit = jnp.where(row < GROUP, reach_ref[first], reach_ref[first + 1])
    keep = place * VN + iota((128, VN), 1) < limit
    for d in range(2):
        v = iota((256, VN), 0) // 8
        e = (iota((256, VN), 1) == (v if d == 0 else (VN - 1) - v)).astype(F32)
        s = f[16 * d : 16 * d + 16, :]
        spread = jnp.broadcast_to(s[:, None, :], (16, 8, 256))
        spread = jnp.where(own_cols, spread, 0.0).reshape(128, 256)
        taps = lax.dot_general(
            spread, e, (((1,), (0,)), ((), ())),
            precision=lax.Precision.HIGHEST, preferred_element_type=F32,
        )
        t_ref[d] = jnp.where(keep, taps * scale, 0.0)


def swap(v, axis, mask):
    return lax.ppermute(v, axis, [(i, i ^ mask) for i in range(lax.axis_size(axis))])


def smem():
    return pl.BlockSpec(memory_space=pltpu.SMEM)


def call(body, out_shape, args, scalars=1, scratch=()):
    vmem = pl.BlockSpec(memory_space=pltpu.VMEM)
    return pl.pallas_call(
        body,
        out_shape=out_shape,
        in_specs=[smem()] * scalars + [vmem] * (len(args) - scalars),
        out_specs=jax.tree.map(lambda _: vmem, out_shape),
        scratch_shapes=list(scratch),
    )(*args)


def on_device_0(out_grad, out_weight, conv_input, gate_values, conv_output, filters, filter_reach):
    shape = jax.ShapeDtypeStruct
    rows, tok = conv_input.shape
    feats = out_grad.shape[1]
    seq_count = lax.axis_size("seq")
    place = lax.axis_index("seq").astype(jnp.int32)
    chan = lax.axis_index("chan").astype(jnp.int32)
    pos = jnp.stack([chan >> 1, chan & 1, place >> 3, (place >> 1) & 3, place])
    half = rows // 2
    scale = 1.0 / float(tok * seq_count) ** 0.5

    mine, other = call(gate_rows, [shape((half, tok), BF16)] * 2, (pos, conv_output, gate_values))
    own = jnp.concatenate([mine, swap(other, "seq", 1)], axis=1)
    og_core = swap(out_grad, "seq", 1)
    b1 = swap(own, "chan", 2)
    b3 = swap(own, "chan", 6)
    b2 = swap(own, "chan", 4)
    bx = swap(jnp.stack([own, b1, b2, b3]), "chan", 1)

    k, s1, s3, s2 = call(first_product, [shape((256, tok), BF16)] * 4, (pos, out_weight, out_grad))
    parts = [k, swap(s1, "chan", 2), swap(s3, "chan", 6), swap(s2, "chan", 4)]
    away = sum(p[128:].astype(F32) for p in parts).astype(BF16)
    got = swap(away, "chan", 1)
    grad_gated = sum(p[:128].astype(F32) for p in parts) + got.astype(F32)
    grad_gate = grad_gated * conv_output.astype(F32)
    grad_conv = (grad_gated * gate_values.astype(F32)).astype(BF16)

    halo_core = swap(grad_conv, "seq", 1)
    pairs = [(i, i + 1) for i in range(1, seq_count - 1, 2)]
    halo_out = lax.ppermute(grad_conv, "seq", pairs + [(b, a) for a, b in pairs])

    e = call(
        second_product,
        [shape((2, half, feats), BF16)] * 4,
        (pos, own, b1, b3, b2, bx, out_grad, og_core),
        scratch=[pltpu.VMEM((8, half, 2 * tok), BF16)],
    )
    e = [e[0], swap(e[1], "seq", 2), swap(e[2], "seq", 6), swap(e[3], "seq", 4)]

    grad_input, tap_sums = call(
        conv_grads,
        [shape((rows, tok), F32), shape((16, rows // 4, 256), F32)],
        (pos, filter_reach, grad_conv, halo_core, halo_out, filters, conv_input),
        scalars=2,
        scratch=[pltpu.VMEM((2, 256, 3 * tok), BF16), pltpu.VMEM((2, 2, 128, 2 * tok), BF16)],
    )
    f_got = swap(tap_sums[8:].astype(BF16), "seq", 1)
    piece = (2, rows // 4, 256)
    f = call(
        split_taps, [shape(piece, F32)] + [shape(piece, BF16)] * 3,
        (tap_sums, f_got), scalars=0,
    )
    f = [f[0], swap(f[1], "seq", 2), swap(f[2], "seq", 6), swap(f[3], "seq", 4)]
    last = call(last_send, shape((half + 16, feats), BF16), (*e, *f), scalars=0)
    got = swap(last, "seq", 8)
    grad_weight, grad_filters = call(
        functools.partial(finish, scale=scale),
        [shape((half, feats), F32), shape((2, rows, VN), F32)],
        (pos, filter_reach, *e, *f, got),
        scalars=2,
    )
    return (grad_input, grad_gate, grad_weight, grad_filters)


def solution(mesh):
    return jax.shard_map(
        on_device_0,
        mesh=mesh,
        in_specs=(
            P("seq", "chan"),
            P(None, "chan"),
            P("chan", "seq"),
            P("chan", "seq"),
            P("chan", "seq"),
            P(None, "chan", None),
            P(),
        ),
        out_specs=(P("chan", "seq"), P("chan", "seq"), P("seq", "chan"), P(None, "chan", "seq")),
        check_vma=False,
    )
```

profile of v0, /device:TPU:0, one launch (start us, length us, event | category | flops | bytes accessed | tf_op | source)
XLA Modules:
  0.0 113.5 jit_solution(11692091550350454660)
XLA Ops:
  1.2 1.7 %shard_map.104 = (bf16[64,512]{1,0:T(8,128)(2,1)}, bf16[64,512]{1,0:T(8,128)(2,1)}) custom-call(s32[5]{0:T(128)} %stack.38.pos_ref, bf16[128,512]{1,0:T(8,128)(2,1)} %v_ref.1, bf16[128,512]{1,0:T(8,128)(2,1)} %g_ref.1), custom_call_target="tpu_custom_call" | custom-call | tf_op jit(solution)/shard_map/pallas_call | solution.py:223
  4.4 2.1 %collective-permute-start.7 = (bf16[64,1024]{1,0:T(8,128)(2,1)S(1)}, bf16[64,1024]{1,0:T(8,128)(2,1)S(1)}, u32[]{:S(2)}, u32[]{:S(2)}) collective-permute-start(bf16[64,1024]{1,0:T(8,128)(2,1)S(1)} %constant_dynamic-update-slice_fusion.b0), channel_id=1, source_target_pairs={{0,2},{1,3},{2,0},{3,1},{4,6},{5,7},{6,4},{7,5},{8,10},{9,11},{10,... | collective-permute-start | bytes 393224 | tf_op jit(solution)/shard_map/ppermute | solution.py:214
  6.5 3.6 %collective-permute-start.9 = (bf16[64,1024]{1,0:T(8,128)(2,1)S(1)}, bf16[64,1024]{1,0:T(8,128)(2,1)S(1)}, u32[]{:S(2)}, u32[]{:S(2)}) collective-permute-start(bf16[64,1024]{1,0:T(8,128)(2,1)S(1)} %constant_dynamic-update-slice_fusion.b0), channel_id=1, source_target_pairs={{0,4},{1,5},{2,6},{3,7},{4,0},{5,1},{6,2},{7,3},{8,12},{9,13},{10,... | collective-permute-start | bytes 393224 | tf_op jit(solution)/shard_map/ppermute | solution.py:214
  10.1 5.4 %shard_map.102 = (bf16[256,512]{1,0:T(8,128)(2,1)}, bf16[256,512]{1,0:T(8,128)(2,1)}, bf16[256,512]{1,0:T(8,128)(2,1)}, bf16[256,512]{1,0:T(8,128)(2,1)}) custom-call(s32[5]{0:T(128)} %stack.38.pos_ref, bf16[1024,1024]{1,0:T(8,128)(2,1)} %w_ref.1, bf16[512,1024]{1,0:T(8,128)(2,1)} %og_ref.3), custom_call_target="tpu_custom_call" | custom-call | tf_op jit(solution)/shard_map/pallas_call | solution.py:223
  16.0 3.5 %collective-permute-start.2 = (bf16[256,512]{1,0:T(8,128)(2,1)}, bf16[256,512]{1,0:T(8,128)(2,1)S(1)}, u32[]{:S(2)}, u32[]{:S(2)}) collective-permute-start(bf16[256,512]{1,0:T(8,128)(2,1)} %get-tuple-element.25), channel_id=1, source_target_pairs={{0,4},{1,5},{2,6},{3,7},{4,0},{5,1},{6,2},{7,3},{8,12},{9,13},{10,... | collective-permute-start | bytes 786440 | tf_op jit(solution)/shard_map/ppermute | solution.py:214
  20.2 13.8 %collective-permute-done.8.b3 = bf16[64,1024]{1,0:T(8,128)(2,1)S(1)} collective-permute-done((bf16[64,1024]{1,0:T(8,128)(2,1)S(1)}, bf16[64,1024]{1,0:T(8,128)(2,1)S(1)}, u32[]{:S(2)}, u32[]{:S(2)}) %collective-permute-start.8) | collective-permute-done | bytes 131104 | tf_op jit(solution)/shard_map/ppermute | solution.py:214
  34.1 1.6 %collective-permute-start.10 = (bf16[4,64,1024]{2,1,0:T(8,128)(2,1)S(1)}, bf16[4,64,1024]{2,1,0:T(8,128)(2,1)S(1)}, u32[]{:S(2)}, u32[]{:S(2)}) collective-permute-start(bf16[4,64,1024]{2,1,0:T(8,128)(2,1)S(1)} %pad_maximum_fusion), channel_id=1, source_target_pairs={{0,1},{1,0},{2,3},{3,2},{4,5},{5,4},{6,7},{7,6},{8,9},{9,8},{10,11... | collective-permute-start | bytes 1572872 | tf_op jit(solution)/shard_map/ppermute | solution.py:214
  37.3 13.2 %collective-permute-done.3 = bf16[128,512]{1,0:T(8,128)(2,1)S(1)} collective-permute-done((bf16[128,512]{1,0:T(8,128)(2,1)S(1)}, bf16[128,512]{1,0:T(8,128)(2,1)S(1)}, u32[]{:S(2)}, u32[]{:S(2)}) %collective-permute-start.3) | collective-permute-done | bytes 131104 | tf_op jit(solution)/shard_map/ppermute | solution.py:214
  50.4 1.7 %convert_multiply_fusion = (f32[128,512]{1,0:T(8,128)}, bf16[128,512]{1,0:T(8,128)(2,1)S(1)}) fusion(bf16[128,512]{1,0:T(8,128)(2,1)S(1)} %copy-done.5, bf16[128,512]{1,0:T(8,128)(2,1)S(1)} %collective-permute-done.3, bf16[256,512]{1,0:T(8,128)(2,1)S(1)} %collective-permute-done.2, bf16[256,512]{1,0:T(8,128)(2,1)S(1)} %collective-permute-done.1, ...), kind=kLoop, calls=%fused_computation.2 | loop fusion | flops 917504 | bytes 1310720 | tf_op jit(solution)/shard_map/mul | solution.py:256
  54.7 5.7 %shard_map.105 = (bf16[2,64,1024]{2,1,0:T(8,128)(2,1)}, bf16[2,64,1024]{2,1,0:T(8,128)(2,1)}, bf16[2,64,1024]{2,1,0:T(8,128)(2,1)}, bf16[2,64,1024]{2,1,0:T(8,128)(2,1)}) custom-call(s32[5]{0:T(128)} %stack.38.pos_ref, bf16[64,1024]{1,0:T(8,128)(2,1)} %copy-done.4, bf16[64,1024]{1,0:T(8,128)(2,1)} %copy-done.9, bf16[64,1024]{1,0:T(8,128)(2,1)} %copy-done.11, ...), custom_call_target="tpu_custom_call" | custom-call | tf_op jit(solution)/shard_map/pallas_call | solution.py:223
  60.4 3.4 %collective-permute-start.12 = (bf16[2,64,1024]{2,1,0:T(8,128)(2,1)}, bf16[2,64,1024]{2,1,0:T(8,128)(2,1)S(1)}, u32[]{:S(2)}, u32[]{:S(2)}) collective-permute-start(bf16[2,64,1024]{2,1,0:T(8,128)(2,1)} %get-tuple-element.30), channel_id=1, source_target_pairs={{0,16},{8,24},{16,0},{24,8},{32,48},{40,56},{48,32},{56,40},{64,80... | collective-permute-start | bytes 786440 | tf_op jit(solution)/shard_map/ppermute | solution.py:214
  63.7 2.2 %collective-permute-start.13 = (bf16[2,64,1024]{2,1,0:T(8,128)(2,1)}, bf16[2,64,1024]{2,1,0:T(8,128)(2,1)S(1)}, u32[]{:S(2)}, u32[]{:S(2)}) collective-permute-start(bf16[2,64,1024]{2,1,0:T(8,128)(2,1)} %get-tuple-element.31), channel_id=1, source_target_pairs={{0,48},{8,56},{16,32},{24,40},{32,16},{40,24},{48,0},{56,8},{64,11... | collective-permute-start | bytes 786440 | tf_op jit(solution)/shard_map/ppermute | solution.py:214
  68.2 14.8 %shard_map.103 = (f32[128,512]{1,0:T(8,128)}, f32[16,32,256]{2,1,0:T(8,128)}) custom-call(s32[5]{0:T(128)} %stack.38.pos_ref, s32[16]{0:T(128)} %reach_ref.3, bf16[128,512]{1,0:T(8,128)(2,1)} %copy-done.7, bf16[128,512]{1,0:T(8,128)(2,1)} %copy-done.17, bf16[128,512]{1,0:T(8,128)(2,1)} %copy-done.18, bf16[2,128,512]{2,1,0:T(8,128)(2,1)} %f_ref.1, ...), custom_call_target="tpu_custom_call" | custom-call | tf_op jit(solution)/shard_map/pallas_call | solution.py:223
  84.0 1.5 %collective-permute-start.15 = (bf16[8,32,256]{2,1,0:T(8,128)(2,1)S(1)}, bf16[8,32,256]{2,1,0:T(8,128)(2,1)S(1)}, u32[]{:S(2)}, u32[]{:S(2)}) collective-permute-start(bf16[8,32,256]{2,1,0:T(8,128)(2,1)S(1)} %slice.69), channel_id=1, source_target_pairs={{0,8},{8,0},{16,24},{24,16},{32,40},{40,32},{48,56},{56,48},{64,72... | collective-permute-start | bytes 393224 | tf_op jit(solution)/shard_map/ppermute | solution.py:214
  87.1 1.7 %shard_map.106 = (f32[2,32,256]{2,1,0:T(8,128)}, bf16[2,32,256]{2,1,0:T(8,128)(2,1)}, bf16[2,32,256]{2,1,0:T(8,128)(2,1)}, bf16[2,32,256]{2,1,0:T(8,128)(2,1)}) custom-call(f32[16,32,256]{2,1,0:T(8,128)} %get-tuple-element.33.t_ref, bf16[8,32,256]{2,1,0:T(8,128)(2,1)} %copy-done.13), custom_call_target="tpu_custom_call" | custom-call | tf_op jit(solution)/shard_map/pallas_call | solution.py:223
  88.8 2.6 %collective-permute-start.17 = (bf16[2,32,256]{2,1,0:T(8,128)(2,1)}, bf16[2,32,256]{2,1,0:T(8,128)(2,1)S(1)}, u32[]{:S(2)}, u32[]{:S(2)}) collective-permute-start(bf16[2,32,256]{2,1,0:T(8,128)(2,1)} %get-tuple-element.36), channel_id=1, source_target_pairs={{0,48},{8,56},{16,32},{24,40},{32,16},{40,24},{48,0},{56,8},{64,11... | collective-permute-start | bytes 98312 | tf_op jit(solution)/shard_map/ppermute | solution.py:214
  91.4 1.5 %collective-permute-done.16.f1 = bf16[2,32,256]{2,1,0:T(8,128)(2,1)S(1)} collective-permute-done((bf16[2,32,256]{2,1,0:T(8,128)(2,1)}, bf16[2,32,256]{2,1,0:T(8,128)(2,1)S(1)}, u32[]{:S(2)}, u32[]{:S(2)}) %collective-permute-start.16) | collective-permute-done | bytes 32800 | tf_op jit(solution)/shard_map/ppermute | solution.py:214
  92.9 2.1 %collective-permute-start.18 = (bf16[2,32,256]{2,1,0:T(8,128)(2,1)}, bf16[2,32,256]{2,1,0:T(8,128)(2,1)S(1)}, u32[]{:S(2)}, u32[]{:S(2)}) collective-permute-start(bf16[2,32,256]{2,1,0:T(8,128)(2,1)} %get-tuple-element.37), channel_id=1, source_target_pairs={{0,32},{8,40},{16,48},{24,56},{32,0},{40,8},{48,16},{56,24},{64,96... | collective-permute-start | bytes 98312 | tf_op jit(solution)/shard_map/ppermute | solution.py:214
  95.0 3.6 %collective-permute-done.18.f2 = bf16[2,32,256]{2,1,0:T(8,128)(2,1)S(1)} collective-permute-done((bf16[2,32,256]{2,1,0:T(8,128)(2,1)}, bf16[2,32,256]{2,1,0:T(8,128)(2,1)S(1)}, u32[]{:S(2)}, u32[]{:S(2)}) %collective-permute-start.18) | collective-permute-done | bytes 32800 | tf_op jit(solution)/shard_map/ppermute | solution.py:214
  99.5 1.9 %shard_map.107 = bf16[80,1024]{1,0:T(8,128)(2,1)} custom-call(bf16[2,64,1024]{2,1,0:T(8,128)(2,1)} %get-tuple-element.29.ek, bf16[2,64,1024]{2,1,0:T(8,128)(2,1)} %copy-done.1, bf16[2,64,1024]{2,1,0:T(8,128)(2,1)} %copy-done.2, bf16[2,64,1024]{2,1,0:T(8,128)(2,1)} %copy-done.3, f32[2,32,256]{2,1,0:T(8,128)} %get-tuple-element.34.fk, ...), custom_call_target="tpu_custom_call" | custom-call | tf_op jit(solution)/shard_map/pallas_call | solution.py:223
  101.4 3.8 %collective-permute-start.19 = (bf16[80,1024]{1,0:T(8,128)(2,1)}, bf16[80,1024]{1,0:T(8,128)(2,1)S(1)}, u32[]{:S(2)}, u32[]{:S(2)}) collective-permute-start(bf16[80,1024]{1,0:T(8,128)(2,1)} %shard_map.107), channel_id=1, source_target_pairs={{0,64},{8,72},{16,80},{24,88},{32,96},{40,104},{48,112},{56,120},{... | collective-permute-start | bytes 491528 | tf_op jit(solution)/shard_map/ppermute | solution.py:214
  105.2 3.5 %collective-permute-done.19.got = bf16[80,1024]{1,0:T(8,128)(2,1)S(1)} collective-permute-done((bf16[80,1024]{1,0:T(8,128)(2,1)}, bf16[80,1024]{1,0:T(8,128)(2,1)S(1)}, u32[]{:S(2)}, u32[]{:S(2)}) %collective-permute-start.19) | collective-permute-done | bytes 163872 | tf_op jit(solution)/shard_map/ppermute | solution.py:214
  109.4 2.5 %shard_map.108 = (f32[64,1024]{1,0:T(8,128)}, f32[2,128,32]{2,1,0:T(8,128)}) custom-call(s32[5]{0:T(128)} %stack.38.pos_ref, s32[16]{0:T(128)} %reach_ref.3, bf16[2,64,1024]{2,1,0:T(8,128)(2,1)} %get-tuple-element.29.ek, bf16[2,64,1024]{2,1,0:T(8,128)(2,1)} %copy-done.1, bf16[2,64,1024]{2,1,0:T(8,128)(2,1)} %copy-done.2, bf16[2,64,1024]{2,1,0:T(8,128)(2,1)} %copy-done.3, ...), custom_call_target="tpu_custom_call" | custom-call | tf_op jit(solution)/shard_map/pallas_call | solution.py:223
  111.9 1.6 %copy.11 = f32[2,128,32]{1,2,0:T(8,128)} copy(f32[2,128,32]{2,1,0:T(8,128)} %get-tuple-element.43) | data formatting | bytes 65536
  (69 shorter events, 13.8 us)
Async XLA Ops:
  2.9 1.5 %collective-permute-start.6 = (bf16[64,512]{1,0:T(8,128)(2,1)}, bf16[64,512]{1,0:T(8,128)(2,1)S(1)}, u32[]{:S(2)}, u32[]{:S(2)}) collective-permute-start(bf16[64,512]{1,0:T(8,128)(2,1)} %get-tuple-element.28), channel_id=1, source_target_pairs={{0,8},{8,0},{16,24},{24,16},{32,40},{40,32},{48,56},{56,48},{64,72... | collective-permute-start | bytes 196616 | tf_op jit(solution)/shard_map/ppermute | solution.py:214
  4.3 46.1 %copy-start.5 = (bf16[128,512]{1,0:T(8,128)(2,1)S(1)}, bf16[128,512]{1,0:T(8,128)(2,1)}, u32[]{:S(2)}) copy-start(bf16[128,512]{1,0:T(8,128)(2,1)} %v_ref.1) | copy-start | bytes 393220
  4.3 46.1 %copy-start.6 = (bf16[128,512]{1,0:T(8,128)(2,1)S(1)}, bf16[128,512]{1,0:T(8,128)(2,1)}, u32[]{:S(2)}) copy-start(bf16[128,512]{1,0:T(8,128)(2,1)} %g_ref.1) | copy-start | bytes 393220
  4.4 11.6 %collective-permute-start.7 = (bf16[64,1024]{1,0:T(8,128)(2,1)S(1)}, bf16[64,1024]{1,0:T(8,128)(2,1)S(1)}, u32[]{:S(2)}, u32[]{:S(2)}) collective-permute-start(bf16[64,1024]{1,0:T(8,128)(2,1)S(1)} %constant_dynamic-update-slice_fusion.b0), channel_id=1, source_target_pairs={{0,2},{1,3},{2,0},{3,1},{4,6},{5,7},{6,4},{7,5},{8,10},{9,11},{10,... | collective-permute-start | bytes 393224 | tf_op jit(solution)/shard_map/ppermute | solution.py:214
  6.5 13.1 %collective-permute-start.9 = (bf16[64,1024]{1,0:T(8,128)(2,1)S(1)}, bf16[64,1024]{1,0:T(8,128)(2,1)S(1)}, u32[]{:S(2)}, u32[]{:S(2)}) collective-permute-start(bf16[64,1024]{1,0:T(8,128)(2,1)S(1)} %constant_dynamic-update-slice_fusion.b0), channel_id=1, source_target_pairs={{0,4},{1,5},{2,6},{3,7},{4,0},{5,1},{6,2},{7,3},{8,12},{9,13},{10,... | collective-permute-start | bytes 393224 | tf_op jit(solution)/shard_map/ppermute | solution.py:214
  10.1 42.8 %collective-permute-start.11 = (bf16[512,1024]{1,0:T(8,128)(2,1)}, bf16[512,1024]{1,0:T(8,128)(2,1)S(1)}, u32[]{:S(2)}, u32[]{:S(2)}) collective-permute-start(bf16[512,1024]{1,0:T(8,128)(2,1)} %og_ref.3), channel_id=1, source_target_pairs={{0,8},{8,0},{16,24},{24,16},{32,40},{40,32},{48,56},{56,48},{64,72... | collective-permute-start | bytes 3145736 | tf_op jit(solution)/shard_map/ppermute | solution.py:214
  15.4 20.2 %collective-permute-start = (bf16[256,512]{1,0:T(8,128)(2,1)}, bf16[256,512]{1,0:T(8,128)(2,1)S(1)}, u32[]{:S(2)}, u32[]{:S(2)}) collective-permute-start(bf16[256,512]{1,0:T(8,128)(2,1)} %get-tuple-element.23), channel_id=1, source_target_pairs={{0,2},{1,3},{2,0},{3,1},{4,6},{5,7},{6,4},{7,5},{8,10},{9,11},{10,... | collective-permute-start | bytes 786440 | tf_op jit(solution)/shard_map/ppermute | solution.py:214
  15.4 20.2 %collective-permute-start.1 = (bf16[256,512]{1,0:T(8,128)(2,1)}, bf16[256,512]{1,0:T(8,128)(2,1)S(1)}, u32[]{:S(2)}, u32[]{:S(2)}) collective-permute-start(bf16[256,512]{1,0:T(8,128)(2,1)} %get-tuple-element.24), channel_id=1, source_target_pairs={{0,6},{1,7},{2,4},{3,5},{4,2},{5,3},{6,0},{7,1},{8,14},{9,15},{10,... | collective-permute-start | bytes 786440 | tf_op jit(solution)/shard_map/ppermute | solution.py:214
  16.0 36.9 %copy-start.9 = (bf16[64,1024]{1,0:T(8,128)(2,1)}, bf16[64,1024]{1,0:T(8,128)(2,1)S(1)}, u32[]{:S(2)}) copy-start(bf16[64,1024]{1,0:T(8,128)(2,1)S(1)} %collective-permute-done.7.b1) | copy-start | bytes 393220
  16.0 19.7 %collective-permute-start.2 = (bf16[256,512]{1,0:T(8,128)(2,1)}, bf16[256,512]{1,0:T(8,128)(2,1)S(1)}, u32[]{:S(2)}, u32[]{:S(2)}) collective-permute-start(bf16[256,512]{1,0:T(8,128)(2,1)} %get-tuple-element.25), channel_id=1, source_target_pairs={{0,4},{1,5},{2,6},{3,7},{4,0},{5,1},{6,2},{7,3},{8,12},{9,13},{10,... | collective-permute-start | bytes 786440 | tf_op jit(solution)/shard_map/ppermute | solution.py:214
  19.5 33.4 %copy-start.10 = (bf16[64,1024]{1,0:T(8,128)(2,1)}, bf16[64,1024]{1,0:T(8,128)(2,1)S(1)}, u32[]{:S(2)}) copy-start(bf16[64,1024]{1,0:T(8,128)(2,1)S(1)} %collective-permute-done.9.b2) | copy-start | bytes 393220
  19.5 14.5 %collective-permute-start.8 = (bf16[64,1024]{1,0:T(8,128)(2,1)S(1)}, bf16[64,1024]{1,0:T(8,128)(2,1)S(1)}, u32[]{:S(2)}, u32[]{:S(2)}) collective-permute-start(bf16[64,1024]{1,0:T(8,128)(2,1)S(1)} %constant_dynamic-update-slice_fusion.b0), channel_id=1, source_target_pairs={{0,6},{1,7},{2,4},{3,5},{4,2},{5,3},{6,0},{7,1},{8,14},{9,15},{10,... | collective-permute-start | bytes 393224 | tf_op jit(solution)/shard_map/ppermute | solution.py:214
  34.1 18.8 %collective-permute-start.10 = (bf16[4,64,1024]{2,1,0:T(8,128)(2,1)S(1)}, bf16[4,64,1024]{2,1,0:T(8,128)(2,1)S(1)}, u32[]{:S(2)}, u32[]{:S(2)}) collective-permute-start(bf16[4,64,1024]{2,1,0:T(8,128)(2,1)S(1)} %pad_maximum_fusion), channel_id=1, source_target_pairs={{0,1},{1,0},{2,3},{3,2},{4,5},{5,4},{6,7},{7,6},{8,9},{9,8},{10,11... | collective-permute-start | bytes 1572872 | tf_op jit(solution)/shard_map/ppermute | solution.py:214
  36.6 13.8 %collective-permute-start.3 = (bf16[128,512]{1,0:T(8,128)(2,1)S(1)}, bf16[128,512]{1,0:T(8,128)(2,1)S(1)}, u32[]{:S(2)}, u32[]{:S(2)}) collective-permute-start(bf16[128,512]{1,0:T(8,128)(2,1)S(1)} %add_convert_fusion), channel_id=1, source_target_pairs={{0,1},{1,0},{2,3},{3,2},{4,5},{5,4},{6,7},{7,6},{8,9},{9,8},{10,11... | collective-permute-start | bytes 393224 | tf_op jit(solution)/shard_map/ppermute | solution.py:214
  52.2 14.7 %collective-permute-start.4 = (bf16[128,512]{1,0:T(8,128)(2,1)S(1)}, bf16[128,512]{1,0:T(8,128)(2,1)S(1)}, u32[]{:S(2)}, u32[]{:S(2)}) collective-permute-start(bf16[128,512]{1,0:T(8,128)(2,1)S(1)} %get-tuple-element.45.gm_ref), channel_id=1, source_target_pairs={{0,8},{8,0},{16,24},{24,16},{32,40},{40,32},{48,56},{56,48},{64,72... | collective-permute-start | bytes 393224 | tf_op jit(solution)/shard_map/ppermute | solution.py:214
  52.2 14.7 %collective-permute-start.5 = (bf16[128,512]{1,0:T(8,128)(2,1)S(1)}, bf16[128,512]{1,0:T(8,128)(2,1)S(1)}, u32[]{:S(2)}, u32[]{:S(2)}) collective-permute-start(bf16[128,512]{1,0:T(8,128)(2,1)S(1)} %get-tuple-element.45.gm_ref), channel_id=1, source_target_pairs={{8,16},{24,32},{40,48},{56,64},{72,80},{88,96},{104,112},{16,8},{3... | collective-permute-start | bytes 393224 | tf_op jit(solution)/shard_map/ppermute | solution.py:261
  60.4 38.2 %collective-permute-start.12 = (bf16[2,64,1024]{2,1,0:T(8,128)(2,1)}, bf16[2,64,1024]{2,1,0:T(8,128)(2,1)S(1)}, u32[]{:S(2)}, u32[]{:S(2)}) collective-permute-start(bf16[2,64,1024]{2,1,0:T(8,128)(2,1)} %get-tuple-element.30), channel_id=1, source_target_pairs={{0,16},{8,24},{16,0},{24,8},{32,48},{40,56},{48,32},{56,40},{64,80... | collective-permute-start | bytes 786440 | tf_op jit(solution)/shard_map/ppermute | solution.py:214
  63.7 34.9 %collective-permute-start.13 = (bf16[2,64,1024]{2,1,0:T(8,128)(2,1)}, bf16[2,64,1024]{2,1,0:T(8,128)(2,1)S(1)}, u32[]{:S(2)}, u32[]{:S(2)}) collective-permute-start(bf16[2,64,1024]{2,1,0:T(8,128)(2,1)} %get-tuple-element.31), channel_id=1, source_target_pairs={{0,48},{8,56},{16,32},{24,40},{32,16},{40,24},{48,0},{56,8},{64,11... | collective-permute-start | bytes 786440 | tf_op jit(solution)/shard_map/ppermute | solution.py:214
  65.9 32.7 %collective-permute-start.14 = (bf16[2,64,1024]{2,1,0:T(8,128)(2,1)}, bf16[2,64,1024]{2,1,0:T(8,128)(2,1)S(1)}, u32[]{:S(2)}, u32[]{:S(2)}) collective-permute-start(bf16[2,64,1024]{2,1,0:T(8,128)(2,1)} %get-tuple-element.32), channel_id=1, source_target_pairs={{0,32},{8,40},{16,48},{24,56},{32,0},{40,8},{48,16},{56,24},{64,96... | collective-permute-start | bytes 786440 | tf_op jit(solution)/shard_map/ppermute | solution.py:214
  84.0 2.5 %collective-permute-start.15 = (bf16[8,32,256]{2,1,0:T(8,128)(2,1)S(1)}, bf16[8,32,256]{2,1,0:T(8,128)(2,1)S(1)}, u32[]{:S(2)}, u32[]{:S(2)}) collective-permute-start(bf16[8,32,256]{2,1,0:T(8,128)(2,1)S(1)} %slice.69), channel_id=1, source_target_pairs={{0,8},{8,0},{16,24},{24,16},{32,40},{40,32},{48,56},{56,48},{64,72... | collective-permute-start | bytes 393224 | tf_op jit(solution)/shard_map/ppermute | solution.py:214
  88.8 4.1 %collective-permute-start.16 = (bf16[2,32,256]{2,1,0:T(8,128)(2,1)}, bf16[2,32,256]{2,1,0:T(8,128)(2,1)S(1)}, u32[]{:S(2)}, u32[]{:S(2)}) collective-permute-start(bf16[2,32,256]{2,1,0:T(8,128)(2,1)} %get-tuple-element.35), channel_id=1, source_target_pairs={{0,16},{8,24},{16,0},{24,8},{32,48},{40,56},{48,32},{56,40},{64,80... | collective-permute-start | bytes 98312 | tf_op jit(solution)/shard_map/ppermute | solution.py:214
  88.8 6.2 %collective-permute-start.17 = (bf16[2,32,256]{2,1,0:T(8,128)(2,1)}, bf16[2,32,256]{2,1,0:T(8,128)(2,1)S(1)}, u32[]{:S(2)}, u32[]{:S(2)}) collective-permute-start(bf16[2,32,256]{2,1,0:T(8,128)(2,1)} %get-tuple-element.36), channel_id=1, source_target_pairs={{0,48},{8,56},{16,32},{24,40},{32,16},{40,24},{48,0},{56,8},{64,11... | collective-permute-start | bytes 98312 | tf_op jit(solution)/shard_map/ppermute | solution.py:214
  92.9 5.6 %collective-permute-start.18 = (bf16[2,32,256]{2,1,0:T(8,128)(2,1)}, bf16[2,32,256]{2,1,0:T(8,128)(2,1)S(1)}, u32[]{:S(2)}, u32[]{:S(2)}) collective-permute-start(bf16[2,32,256]{2,1,0:T(8,128)(2,1)} %get-tuple-element.37), channel_id=1, source_target_pairs={{0,32},{8,40},{16,48},{24,56},{32,0},{40,8},{48,16},{56,24},{64,96... | collective-permute-start | bytes 98312 | tf_op jit(solution)/shard_map/ppermute | solution.py:214
  101.4 7.3 %collective-permute-start.19 = (bf16[80,1024]{1,0:T(8,128)(2,1)}, bf16[80,1024]{1,0:T(8,128)(2,1)S(1)}, u32[]{:S(2)}, u32[]{:S(2)}) collective-permute-start(bf16[80,1024]{1,0:T(8,128)(2,1)} %shard_map.107), channel_id=1, source_target_pairs={{0,64},{8,72},{16,80},{24,88},{32,96},{40,104},{48,112},{56,120},{... | collective-permute-start | bytes 491528 | tf_op jit(solution)/shard_map/ppermute | solution.py:214
  (15 other events, 80.1 us)
where the time goes:
time: 115 us; the launch traced here: 113 us
  waiting for transfers between devices  37.1 us (32%)
  Pallas kernels  33.7 us (29%)
  starting transfers between devices  29.9 us (26%)
  local copies, waits for them, and re-layouts  9.19 us (8%)
  other arithmetic  2.77 us (2%)
    ppermute x19, waiting for transfers between devices, swap(): lax.ppermute(v, axis, [(i, i ^ mask) for i in range(lax.axis_size(axis))])  37.1 us
    pallas_call x7, Pallas kernels, call(): pl.pallas_call(body, out_shape=out_shape, in_specs=[smem()] * scalars + [...  33.7 us
    ppermute x19, starting transfers between devices, swap(): lax.ppermute(v, axis, [(i, i ^ mask) for i in range(lax.axis_size(axis))])  29.2 us
    unnamed x40, local copies, waits for them, and re-layouts  7.65 us
  transfers between devices with their start and end apart: 20, of which 7 were waited for; matrix products, arithmetic and copies ran while one was open for 4% of the time, Pallas kernels for 24%

commit v1 on v0

v1 whole, which is shorter than its diff:
```python
import functools

import jax
import jax.numpy as jnp
from jax import lax
from jax.experimental import pallas as pl
from jax.experimental.pallas import tpu as pltpu
from jax.sharding import PartitionSpec as P


GROUP = 64
VN = 32
F32 = jnp.float32
BF16 = jnp.bfloat16


def iota(shape, dim):
    return lax.broadcasted_iota(jnp.int32, shape, dim)


def dot(a, b, dims=(((1,), (0,)), ((), ()))):
    return lax.dot_general(a, b, dims, preferred_element_type=F32)


NT = (((1,), (1,)), ((), ()))


RELS = (0, 1, 3, 2)


def gate_rows(pos_ref, v_ref, g_ref, mine, other):
    half = mine.shape[0]
    core = pos_ref[4] % 2
    for ref, part in ((mine, core), (other, 1 - core)):
        band = pl.ds(pl.multiple_of(part * half, half), half)
        ref[...] = (v_ref[band, :].astype(F32) * g_ref[band, :].astype(F32)).astype(BF16)


def first_product(pos_ref, w_ref, og_ref, keep, send):
    z = pos_ref[0]
    x = pos_ref[1]
    og = og_ref[...]
    for i, rel in enumerate(RELS):
        w = [w_ref[pl.ds(((z ^ rel) * 2 + (x ^ a)) * 128, 128), :] for a in range(2)]
        p = dot(jnp.concatenate(w, axis=0), og, NT).astype(BF16)
        keep[128 * i : 128 * (i + 1), :] = p[:128]
        send[128 * i : 128 * (i + 1), :] = p[128:]


def middle_sums(k_ref, r_ref, *outs):
    n = k_ref.shape[0] // 4
    for i, ref in enumerate(outs):
        band = slice(n * i, n * i + n)
        ref[...] = (k_ref[band, :].astype(F32) + r_ref[band, :].astype(F32)).astype(ref.dtype)


def gate_grads(k_ref, r1, r3, r2, v_ref, g_ref, gate_ref, conv_ref):
    total = k_ref[...] + r1[...].astype(F32) + r3[...].astype(F32) + r2[...].astype(F32)
    gate_ref[...] = total * v_ref[...].astype(F32)
    conv_ref[...] = (total * g_ref[...].astype(F32)).astype(BF16)


def second_product(pos_ref, b0, b1, b3, b2, og_ref, ogs_ref, *refs):
    outs, g_ref = refs[:4], refs[4]
    for i, ref in enumerate((b0, b1, b2, b3)):
        g_ref[i] = ref[0]
        g_ref[4 + i] = ref[1]
    z = pos_ref[0]
    x = pos_ref[1]
    xh = pos_ref[2]
    y = pos_ref[3]
    tok = og_ref.shape[0]
    for ref, rel in zip(outs, RELS):
        for a in range(2):
            j = (xh ^ a) * 4 + (y ^ rel)
            g = g_ref[((j % 2) ^ x) * 4 + ((j // 2) ^ z)]
            ref[a] = (dot(g[:, :tok], og_ref[...]) + dot(g[:, tok:], ogs_ref[...])).astype(BF16)


def lagged(x, first, width):
    pair = [pltpu.roll(x, s % width, 1) if s % width else x for s in first]
    return jnp.concatenate(pair, axis=0).astype(BF16)


def conv_grads(pos_ref, reach_ref, gm_ref, gs_ref, gp_ref, f_ref, x_ref,
               o_ref, keep_ref, send_ref, h_ref, u_ref, t_ref):
    rows, n = gm_ref.shape
    width = 3 * n
    lanes = n // 128
    chan = pos_ref[0] * 2 + pos_ref[1]
    place = pos_ref[4]
    core0 = (place & 1) == 0
    own_rows = (iota((128, 256), 0) & 7) == (iota((128, 256), 1) & 7)
    ef = (iota((128, 256), 0) == (iota((128, 256), 1) >> 3)).astype(BF16)
    eb = (iota((128, 256), 0) == (VN - 1) - (iota((128, 256), 1) >> 3)).astype(BF16)
    own_cols = iota((16, 8, 256), 1) == (iota((16, 8, 256), 2) & 7)
    taps = f_ref.shape[2]
    lag = iota((8, taps), 1)

    def step(i, carry):
        base = pl.multiple_of(i * 16, 16)
        band = pl.ds(base, 16)
        gm = gm_ref[band, :].astype(F32)
        gs = gs_ref[band, :].astype(F32)
        gp = gp_ref[band, :].astype(F32)
        ext16 = jnp.concatenate([jnp.where(core0, gp, gs), gm, jnp.where(core0, gs, gp)], axis=1)
        own16 = x_ref[band, :].astype(F32)
        filt16 = [f_ref[d, band, :].astype(F32) for d in range(2)]
        inside = lag < reach_ref[(chan * rows + base) // GROUP]
        zero = jnp.zeros((8, n), F32)
        outs = []
        for h in range(2):
            ext = ext16[8 * h : 8 * h + 8]
            two = jnp.concatenate([ext, pltpu.roll(ext, width - 1, 1)], axis=0).astype(BF16)
            for k in range(VN // 2):
                moved = two if k == 0 else pltpu.roll(two, width - 2 * k, 1)
                h_ref[h, 16 * k : 16 * k + 16, :] = moved
            lhs = []
            for d, e in ((0, ef), (1, eb)):
                f8 = jnp.where(inside, filt16[d][8 * h : 8 * h + 8], 0.0)
                rolled = [f8 if b == 0 else pltpu.roll(f8, taps - 32 * b, 1) for b in range(4)]
                cut = [rolled[u % 4][:, 128 * (u // 4) : 128 * (u // 4) + 128] for u in range(16)]
                spread = dot(jnp.concatenate(cut, axis=0).astype(BF16), e)
                lhs.append(jnp.where(own_rows, spread, 0.0).astype(BF16))
            total = None
            for d in range(2):
                acc = [[None] * (lanes + (b > 0)) for b in range(4)]
                for j in range(lanes):
                    if d == 0:
                        lo, hi = (0, 64) if j == 0 else (64, 128) if j == lanes - 1 else (0, 128)
                    else:
                        lo, hi = (48, 128) if j == 0 else (0, 64) if j == lanes - 1 else (0, 128)
                    at = n * (1 - d) + 256 * j
                    p = dot(lhs[d][lo:hi], h_ref[h, :, at : at + 256])
                    for u in range(lo // 8, hi // 8):
                        a, b = divmod(u + d, 4)
                        for c in range(2):
                            q = 2 * j + c
                            slot = q - a if d == 0 else q - (lanes - (b > 0)) + a
                            if 0 <= slot < len(acc[b]):
                                part = p[8 * u - lo : 8 * u - lo + 8, 128 * c : 128 * c + 128]
                                acc[b][slot] = part if acc[b][slot] is None else acc[b][slot] + part
                for b in range(4):
                    line = jnp.concatenate(acc[b], axis=1)
                    if b and d == 0:
                        line = pltpu.roll(line, n + 128 - 32 * b, 1)[:, :n]
                    elif b:
                        line = pltpu.roll(line, 32 * b, 1)[:, 128:]
                    total = line if total is None else total + line
            outs.append(total)
            own = jnp.concatenate([zero, own16[8 * h : 8 * h + 8], zero], axis=1)
            bases = (
                (lagged(own, (0, 32), width), lagged(own, (64, 96), width)),
                (lagged(own, (-32, -64), width), lagged(own, (-96, -128), width)),
            )
            for d in range(2):
                for k in range(8):
                    start = n - 128 * (k // 2) if d == 0 else 128 * (k // 2)
                    u_ref[h, d, 16 * k : 16 * k + 16, :] = bases[d][k % 2][:, start : start + 2 * n]
            for d in range(2):
                start = n * (1 - d)
                cross = dot(u_ref[h, d], h_ref[h, :, start : start + 2 * n], NT)
                sums = jnp.sum(jnp.where(own_cols, cross.reshape(16, 8, 256), 0.0), axis=1)
                row = d * (rows // 8) + 2 * i + h
                for u in range(16):
                    r = u ^ place
                    slot = (r & 1) * 8 + ((r >> 1) & 3) * 2 + (r >> 3)
                    t_ref[slot, pl.ds(row, 1), :] = sums[u : u + 1]
        o_ref[band, :] = jnp.concatenate(outs, axis=0)
        return carry

    lax.fori_loop(0, rows // 16, step, 0)
    keep_ref[...] = t_ref[0:8]
    send_ref[...] = t_ref[8:16].astype(BF16)


def split_taps(t_ref, got_ref, k, s1, s3, s2):
    for rel, ref in ((0, k), (1, s1), (3, s3), (2, s2)):
        both = t_ref[2 * rel : 2 * rel + 2] + got_ref[2 * rel : 2 * rel + 2].astype(F32)
        ref[...] = both.astype(ref.dtype)


def last_send(ek, e1, e3, e2, fk, f1, f3, f2, o_ref):
    e = ek[1].astype(F32)
    for ref in (e1, e3, e2):
        e = e + ref[1].astype(F32)
    f = fk[1]
    for ref in (f1, f3, f2):
        f = f + ref[1].astype(F32)
    n = f.shape[0] // 4
    o_ref[0 : e.shape[0], :] = e.astype(BF16)
    tail = jnp.concatenate([f[n * i : n * i + n] for i in range(4)], axis=1)
    o_ref[e.shape[0] :, :] = jnp.concatenate([tail, tail], axis=0).astype(BF16)


def finish(pos_ref, reach_ref, ek, e1, e3, e2, fk, f1, f3, f2, got, w_ref, t_ref, *, scale):
    e = ek[0].astype(F32)
    for ref in (e1, e3, e2):
        e = e + ref[0].astype(F32)
    m = e.shape[0]
    w_ref[...] = (e + got[0:m, :].astype(F32)) * scale
    f = fk[0]
    for ref in (f1, f3, f2):
        f = f + ref[0].astype(F32)
    n = f.shape[0] // 4
    tail = got[m:, :].astype(F32)[0:n]
    wide = f.shape[1]
    f = f + jnp.concatenate([tail[:, wide * i : wide * i + wide] for i in range(4)], axis=0)
    chan = pos_ref[0] * 2 + pos_ref[1]
    place = pos_ref[4]
    own_cols = iota((16, 8, 256), 1) == (iota((16, 8, 256), 2) & 7)
    first = chan * 128 // GROUP
    limit = jnp.where(iota((VN, 128), 1) < GROUP, reach_ref[first], reach_ref[first + 1])
    keep = place * VN + iota((VN, 128), 0) < limit
    for d in range(2):
        v = iota((VN, 256), 1) >> 3
        e = (iota((VN, 256), 0) == (v if d == 0 else (VN - 1) - v)).astype(BF16)
        part = f[16 * d : 16 * d + 16, :]
        spread = jnp.broadcast_to(part[:, None, :], (16, 8, 256))
        spread = jnp.where(own_cols, spread, 0.0).reshape(128, 256)
        high = spread.astype(BF16)
        low = (spread - high.astype(F32)).astype(BF16)
        t_ref[d] = jnp.where(keep, (dot(e, high, NT) + dot(e, low, NT)) * scale, 0.0)


def swap(v, axis, mask):
    return lax.ppermute(v, axis, [(i, i ^ mask) for i in range(lax.axis_size(axis))])


def smem():
    return pl.BlockSpec(memory_space=pltpu.SMEM)


def call(body, out_shape, args, scalars=1, scratch=(), limit=16):
    vmem = pl.BlockSpec(memory_space=pltpu.VMEM)
    held = [pltpu.with_memory_space_constraint(a, pltpu.VMEM) for a in args[scalars:]]
    return pl.pallas_call(
        body,
        out_shape=out_shape,
        in_specs=[smem()] * scalars + [vmem] * len(held),
        out_specs=jax.tree.map(lambda _: vmem, out_shape),
        scratch_shapes=list(scratch),
        compiler_params=pltpu.CompilerParams(vmem_limit_bytes=limit << 20),
    )(*args[:scalars], *held)


def on_device_0(out_grad, out_weight, conv_input, gate_values, conv_output, filters, filter_reach):
    shape = jax.ShapeDtypeStruct
    rows, tok = conv_input.shape
    feats = out_grad.shape[1]
    seq_count = lax.axis_size("seq")
    place = lax.axis_index("seq").astype(jnp.int32)
    chan = lax.axis_index("chan").astype(jnp.int32)
    pos = jnp.stack([chan >> 1, chan & 1, place >> 3, (place >> 1) & 3, place])
    half = rows // 2
    scale = 1.0 / float(tok * seq_count) ** 0.5

    mine, other = call(gate_rows, [shape((half, tok), BF16)] * 2, (pos, conv_output, gate_values))
    own = jnp.concatenate([mine, swap(other, "seq", 1)], axis=1)
    og_core = swap(out_grad, "seq", 1)
    pair = jnp.stack([own, swap(own, "chan", 1)])
    b1 = swap(pair, "chan", 2)
    b3 = swap(pair, "chan", 6)
    b2 = swap(pair, "chan", 4)

    keep, send = call(
        first_product, [shape((rows * 4, tok), BF16)] * 2, (pos, out_weight, out_grad)
    )
    keep, s1, s3, s2 = call(
        middle_sums,
        [shape((rows, tok), F32)] + [shape((rows, tok), BF16)] * 3,
        (keep, swap(send, "chan", 1)),
        scalars=0,
    )
    s1, s3, s2 = swap(s1, "chan", 2), swap(s3, "chan", 6), swap(s2, "chan", 4)
    grad_gate, grad_conv = call(
        gate_grads,
        [shape((rows, tok), F32), shape((rows, tok), BF16)],
        (keep, s1, s3, s2, conv_output, gate_values),
        scalars=0,
    )

    halo_core = swap(grad_conv, "seq", 1)
    pairs = [(i, i + 1) for i in range(1, seq_count - 1, 2)]
    halo_out = lax.ppermute(grad_conv, "seq", pairs + [(b, a) for a, b in pairs])

    e = call(
        second_product,
        [shape((2, half, feats), BF16)] * 4,
        (pos, pair, b1, b3, b2, out_grad, og_core),
        scratch=[pltpu.VMEM((8, half, 2 * tok), BF16)],
    )
    e = [e[0], swap(e[1], "seq", 2), swap(e[2], "seq", 6), swap(e[3], "seq", 4)]

    grad_input, tap_keep, tap_send = call(
        conv_grads,
        [
            shape((rows, tok), F32),
            shape((8, rows // 4, 256), F32),
            shape((8, rows // 4, 256), BF16),
        ],
        (pos, filter_reach, grad_conv, halo_core, halo_out, filters, conv_input),
        scalars=2,
        scratch=[
            pltpu.VMEM((2, 256, 3 * tok), BF16),
            pltpu.VMEM((2, 2, 128, 2 * tok), BF16),
            pltpu.VMEM((16, rows // 4, 256), F32),
        ],
    )
    f_got = swap(tap_send, "seq", 1)
    piece = (2, rows // 4, 256)
    f = call(
        split_taps, [shape(piece, F32)] + [shape(piece, BF16)] * 3,
        (tap_keep, f_got), scalars=0,
    )
    f = [f[0], swap(f[1], "seq", 2), swap(f[2], "seq", 6), swap(f[3], "seq", 4)]
    last = call(last_send, shape((half + 16, feats), BF16), (*e, *f), scalars=0)
    got = swap(last, "seq", 8)
    grad_weight, grad_filters = call(
        functools.partial(finish, scale=scale),
        [shape((half, feats), F32), shape((2, VN, rows), F32)],
        (pos, filter_reach, *e, *f, got),
        scalars=2,
    )
    return (grad_input, grad_gate, grad_weight, jnp.transpose(grad_filters, (0, 2, 1)))


def solution(mesh):
    return jax.shard_map(
        on_device_0,
        mesh=mesh,
        in_specs=(
            P("seq", "chan"),
            P(None, "chan"),
            P("chan", "seq"),
            P("chan", "seq"),
            P("chan", "seq"),
            P(None, "chan", None),
            P(),
        ),
        out_specs=(P("chan", "seq"), P("chan", "seq"), P("seq", "chan"), P(None, "chan", "seq")),
        check_vma=False,
    )
```

time: 115 us -> 90.1 us (0.78); the launches traced: 113 us -> 89.9 us
  Pallas kernels: 33.7 us -> 22.1 us
  local copies, waits for them, and re-layouts: 9.19 us -> 2.94 us
  waiting for transfers between devices: 37.1 us -> 32.2 us
  other arithmetic: 2.77 us -> 0.03 us
  starting transfers between devices: 29.9 us -> 31.8 us
    pallas_call x7 -> x9, Pallas kernels: 33.7 us -> 22.1 us  [call(): pl.pallas_call(body, out_shape=out_shape, in_specs=[smem()] * scalars + [...]
    ppermute x19, waiting for transfers between devices: 37.1 us -> 32.2 us  [swap(): lax.ppermute(v, axis, [(i, i ^ mask) for i in range(lax.axis_size(axis))])]
    unnamed x40 -> x17, local copies, waits for them, and re-layouts: 7.65 us -> 2.85 us
    ppermute x19, starting transfers between devices: 29.2 us -> 31.2 us  [swap(): lax.ppermute(v, axis, [(i, i ^ mask) for i in range(lax.axis_size(axis))])]
    mul x1 -> x0, other arithmetic: 1.73 us -> none  [on_device_0(): grad_gate = grad_gated * conv_output.astype(F32)]
  transfers between devices with their start and end apart: 20 -> 20, of which waited for: 7 -> 8; matrix products, arithmetic and copies ran while one was open for 4% -> 0% of each run, Pallas kernels for 24% -> 23%
where the time goes in v1:
time: 90.1 us; the launch traced here: 89.9 us
  waiting for transfers between devices  32.2 us (36%)
  starting transfers between devices  31.8 us (35%)
  Pallas kernels  22.1 us (25%)
  local copies, waits for them, and re-layouts  2.94 us (3%)
    ppermute x19, waiting for transfers between devices, swap(): lax.ppermute(v, axis, [(i, i ^ mask) for i in range(lax.axis_size(axis))])  32.2 us
    ppermute x19, starting transfers between devices, swap(): lax.ppermute(v, axis, [(i, i ^ mask) for i in range(lax.axis_size(axis))])  31.2 us
    pallas_call x9, Pallas kernels, call(): pl.pallas_call(body, out_shape=out_shape, in_specs=[smem()] * scalars + [...  22.1 us
    unnamed x17, local copies, waits for them, and re-layouts  2.85 us
  transfers between devices with their start and end apart: 20, of which 8 were waited for; matrix products, arithmetic and copies ran while one was open for 0% of the time, Pallas kernels for 23%

profile of v1, /device:TPU:0, one launch (start us, length us, event | category | flops | bytes accessed | tf_op | source)
XLA Modules:
  0.0 89.9 jit_solution(8979279802694281018)
XLA Ops:
  2.0 1.6 %copy-done.2 = bf16[1024,1024]{1,0:T(8,128)(2,1)S(1)} copy-done((bf16[1024,1024]{1,0:T(8,128)(2,1)S(1)}, bf16[1024,1024]{1,0:T(8,128)(2,1)}, u32[]{:S(2)}) %copy-start.2) | copy-done | bytes 2097176
  3.6 1.8 %shard_map.102 = (bf16[512,512]{1,0:T(8,128)(2,1)S(1)}, bf16[512,512]{1,0:T(8,128)(2,1)S(1)}) custom-call(s32[5]{0:T(128)S(1)} %stack.32.pos_ref, bf16[1024,1024]{1,0:T(8,128)(2,1)S(1)} %copy-done.2, bf16[512,1024]{1,0:T(8,128)(2,1)S(1)} %copy-done), custom_call_target="tpu_custom_call" | custom-call | tf_op jit(solution)/shard_map/pallas_call | solution.py:237
  5.5 1.7 %collective-permute-start = (bf16[512,512]{1,0:T(8,128)(2,1)S(1)}, bf16[512,512]{1,0:T(8,128)(2,1)S(1)}, u32[]{:S(2)}, u32[]{:S(2)}) collective-permute-start(bf16[512,512]{1,0:T(8,128)(2,1)S(1)} %get-tuple-element.28), channel_id=1, source_target_pairs={{0,1},{1,0},{2,3},{3,2},{4,5},{5,4},{6,7},{7,6},{8,9},{9,8},{10,11... | collective-permute-start | bytes 1572872 | tf_op jit(solution)/shard_map/ppermute | solution.py:227
  9.5 10.8 %collective-permute-done.r_ref = bf16[512,512]{1,0:T(8,128)(2,1)S(1)} collective-permute-done((bf16[512,512]{1,0:T(8,128)(2,1)S(1)}, bf16[512,512]{1,0:T(8,128)(2,1)S(1)}, u32[]{:S(2)}, u32[]{:S(2)}) %collective-permute-start) | collective-permute-done | bytes 524320 | tf_op jit(solution)/shard_map/ppermute | solution.py:227
  20.5 2.1 %collective-permute-start.1 = (bf16[128,512]{1,0:T(8,128)(2,1)S(1)}, bf16[128,512]{1,0:T(8,128)(2,1)S(1)}, u32[]{:S(2)}, u32[]{:S(2)}) collective-permute-start(bf16[128,512]{1,0:T(8,128)(2,1)S(1)} %get-tuple-element.30), channel_id=1, source_target_pairs={{0,2},{1,3},{2,0},{3,1},{4,6},{5,7},{6,4},{7,5},{8,10},{9,11},{10,... | collective-permute-start | bytes 393224 | tf_op jit(solution)/shard_map/ppermute | solution.py:227
  22.6 2.5 %collective-permute-start.2 = (bf16[128,512]{1,0:T(8,128)(2,1)S(1)}, bf16[128,512]{1,0:T(8,128)(2,1)S(1)}, u32[]{:S(2)}, u32[]{:S(2)}) collective-permute-start(bf16[128,512]{1,0:T(8,128)(2,1)S(1)} %get-tuple-element.31), channel_id=1, source_target_pairs={{0,6},{1,7},{2,4},{3,5},{4,2},{5,3},{6,0},{7,1},{8,14},{9,15},{10,... | collective-permute-start | bytes 393224 | tf_op jit(solution)/shard_map/ppermute | solution.py:227
  25.2 1.6 %collective-permute-start.10 = (bf16[2,64,1024]{2,1,0:T(8,128)(2,1)S(1)}, bf16[2,64,1024]{2,1,0:T(8,128)(2,1)S(1)}, u32[]{:S(2)}, u32[]{:S(2)}) collective-permute-start(bf16[2,64,1024]{2,1,0:T(8,128)(2,1)S(1)} %pad_maximum_fusion.b0), channel_id=1, source_target_pairs={{0,4},{1,5},{2,6},{3,7},{4,0},{5,1},{6,2},{7,3},{8,12},{9,13},{10,... | collective-permute-start | bytes 786440 | tf_op jit(solution)/shard_map/ppermute | solution.py:227
  26.8 2.1 %collective-permute-start.9 = (bf16[2,64,1024]{2,1,0:T(8,128)(2,1)S(1)}, bf16[2,64,1024]{2,1,0:T(8,128)(2,1)S(1)}, u32[]{:S(2)}, u32[]{:S(2)}) collective-permute-start(bf16[2,64,1024]{2,1,0:T(8,128)(2,1)S(1)} %pad_maximum_fusion.b0), channel_id=1, source_target_pairs={{0,6},{1,7},{2,4},{3,5},{4,2},{5,3},{6,0},{7,1},{8,14},{9,15},{10,... | collective-permute-start | bytes 786440 | tf_op jit(solution)/shard_map/ppermute | solution.py:227
  29.0 4.0 %collective-permute-done.2.r3 = bf16[128,512]{1,0:T(8,128)(2,1)S(1)} collective-permute-done((bf16[128,512]{1,0:T(8,128)(2,1)S(1)}, bf16[128,512]{1,0:T(8,128)(2,1)S(1)}, u32[]{:S(2)}, u32[]{:S(2)}) %collective-permute-start.2) | collective-permute-done | bytes 131104 | tf_op jit(solution)/shard_map/ppermute | solution.py:227
  32.9 4.8 %collective-permute-start.3 = (bf16[128,512]{1,0:T(8,128)(2,1)S(1)}, bf16[128,512]{1,0:T(8,128)(2,1)S(1)}, u32[]{:S(2)}, u32[]{:S(2)}) collective-permute-start(bf16[128,512]{1,0:T(8,128)(2,1)S(1)} %get-tuple-element.32), channel_id=1, source_target_pairs={{0,4},{1,5},{2,6},{3,7},{4,0},{5,1},{6,2},{7,3},{8,12},{9,13},{10,... | collective-permute-start | bytes 393224 | tf_op jit(solution)/shard_map/ppermute | solution.py:227
  37.8 5.4 %collective-permute-done.3.r2 = bf16[128,512]{1,0:T(8,128)(2,1)S(1)} collective-permute-done((bf16[128,512]{1,0:T(8,128)(2,1)S(1)}, bf16[128,512]{1,0:T(8,128)(2,1)S(1)}, u32[]{:S(2)}, u32[]{:S(2)}) %collective-permute-start.3) | collective-permute-done | bytes 131104 | tf_op jit(solution)/shard_map/ppermute | solution.py:227
  44.7 3.0 %collective-permute-start.4 = (bf16[128,512]{1,0:T(8,128)(2,1)S(1)}, bf16[128,512]{1,0:T(8,128)(2,1)S(1)}, u32[]{:S(2)}, u32[]{:S(2)}) collective-permute-start(bf16[128,512]{1,0:T(8,128)(2,1)S(1)} %get-tuple-element.33.gm_ref), channel_id=1, source_target_pairs={{0,8},{8,0},{16,24},{24,16},{32,40},{40,32},{48,56},{56,48},{64,72... | collective-permute-start | bytes 393224 | tf_op jit(solution)/shard_map/ppermute | solution.py:227
  47.7 3.6 %shard_map.107 = (bf16[2,64,1024]{2,1,0:T(8,128)(2,1)S(1)}, bf16[2,64,1024]{2,1,0:T(8,128)(2,1)S(1)}, bf16[2,64,1024]{2,1,0:T(8,128)(2,1)S(1)}, bf16[2,64,1024]{2,1,0:T(8,128)(2,1)S(1)}) custom-call(s32[5]{0:T(128)S(1)} %stack.32.pos_ref, bf16[2,64,1024]{2,1,0:T(8,128)(2,1)S(1)} %pad_maximum_fusion.b0, bf16[2,64,1024]{2,1,0:T(8,128)(2,1)S(1)} %collective-permute-done.8.b1, ...), custom_call_target="tpu_custom_call" | custom-call | tf_op jit(solution)/shard_map/pallas_call | solution.py:237
  51.3 1.7 %collective-permute-start.12 = (bf16[2,64,1024]{2,1,0:T(8,128)(2,1)S(1)}, bf16[2,64,1024]{2,1,0:T(8,128)(2,1)S(1)}, u32[]{:S(2)}, u32[]{:S(2)}) collective-permute-start(bf16[2,64,1024]{2,1,0:T(8,128)(2,1)S(1)} %get-tuple-element.39), channel_id=1, source_target_pairs={{0,16},{8,24},{16,0},{24,8},{32,48},{40,56},{48,32},{56,40},{64,80... | collective-permute-start | bytes 786440 | tf_op jit(solution)/shard_map/ppermute | solution.py:227
  53.0 2.6 %collective-permute-start.13 = (bf16[2,64,1024]{2,1,0:T(8,128)(2,1)S(1)}, bf16[2,64,1024]{2,1,0:T(8,128)(2,1)S(1)}, u32[]{:S(2)}, u32[]{:S(2)}) collective-permute-start(bf16[2,64,1024]{2,1,0:T(8,128)(2,1)S(1)} %get-tuple-element.40), channel_id=1, source_target_pairs={{0,48},{8,56},{16,32},{24,40},{32,16},{40,24},{48,0},{56,8},{64,11... | collective-permute-start | bytes 786440 | tf_op jit(solution)/shard_map/ppermute | solution.py:227
  55.6 1.4 %collective-permute-start.14 = (bf16[2,64,1024]{2,1,0:T(8,128)(2,1)S(1)}, bf16[2,64,1024]{2,1,0:T(8,128)(2,1)S(1)}, u32[]{:S(2)}, u32[]{:S(2)}) collective-permute-start(bf16[2,64,1024]{2,1,0:T(8,128)(2,1)S(1)} %get-tuple-element.41), channel_id=1, source_target_pairs={{0,32},{8,40},{16,48},{24,56},{32,0},{40,8},{48,16},{56,24},{64,96... | collective-permute-start | bytes 786440 | tf_op jit(solution)/shard_map/ppermute | solution.py:227
  57.0 13.6 %shard_map.105 = (f32[128,512]{1,0:T(8,128)}, f32[8,32,256]{2,1,0:T(8,128)S(1)}, bf16[8,32,256]{2,1,0:T(8,128)(2,1)S(1)}) custom-call(s32[5]{0:T(128)S(1)} %stack.32.pos_ref, s32[16]{0:T(128)S(1)} %copy-done.7, bf16[128,512]{1,0:T(8,128)(2,1)S(1)} %get-tuple-element.33.gm_ref, bf16[128,512]{1,0:T(8,128)(2,1)S(1)} %collective-permute-done.4.gs_ref, ...), custom_call_target="tpu_custom_call" | custom-call | tf_op jit(solution)/shard_map/pallas_call | solution.py:237
  70.6 1.3 %collective-permute-done.15.got_ref = bf16[8,32,256]{2,1,0:T(8,128)(2,1)S(1)} collective-permute-done((bf16[8,32,256]{2,1,0:T(8,128)(2,1)S(1)}, bf16[8,32,256]{2,1,0:T(8,128)(2,1)S(1)}, u32[]{:S(2)}, u32[]{:S(2)}) %collective-permute-start.15) | collective-permute-done | bytes 131104 | tf_op jit(solution)/shard_map/ppermute | solution.py:227
  72.1 2.7 %collective-permute-start.17 = (bf16[2,32,256]{2,1,0:T(8,128)(2,1)S(1)}, bf16[2,32,256]{2,1,0:T(8,128)(2,1)S(1)}, u32[]{:S(2)}, u32[]{:S(2)}) collective-permute-start(bf16[2,32,256]{2,1,0:T(8,128)(2,1)S(1)} %get-tuple-element.46), channel_id=1, source_target_pairs={{0,48},{8,56},{16,32},{24,40},{32,16},{40,24},{48,0},{56,8},{64,11... | collective-permute-start | bytes 98312 | tf_op jit(solution)/shard_map/ppermute | solution.py:227
  76.0 2.2 %collective-permute-start.18 = (bf16[2,32,256]{2,1,0:T(8,128)(2,1)S(1)}, bf16[2,32,256]{2,1,0:T(8,128)(2,1)S(1)}, u32[]{:S(2)}, u32[]{:S(2)}) collective-permute-start(bf16[2,32,256]{2,1,0:T(8,128)(2,1)S(1)} %get-tuple-element.47), channel_id=1, source_target_pairs={{0,32},{8,40},{16,48},{24,56},{32,0},{40,8},{48,16},{56,24},{64,96... | collective-permute-start | bytes 98312 | tf_op jit(solution)/shard_map/ppermute | solution.py:227
  78.2 3.2 %collective-permute-done.18.f2 = bf16[2,32,256]{2,1,0:T(8,128)(2,1)S(1)} collective-permute-done((bf16[2,32,256]{2,1,0:T(8,128)(2,1)S(1)}, bf16[2,32,256]{2,1,0:T(8,128)(2,1)S(1)}, u32[]{:S(2)}, u32[]{:S(2)}) %collective-permute-start.18) | collective-permute-done | bytes 32800 | tf_op jit(solution)/shard_map/ppermute | solution.py:227
  81.5 1.7 %collective-permute-start.19 = (bf16[80,1024]{1,0:T(8,128)(2,1)S(1)}, bf16[80,1024]{1,0:T(8,128)(2,1)S(1)}, u32[]{:S(2)}, u32[]{:S(2)}) collective-permute-start(bf16[80,1024]{1,0:T(8,128)(2,1)S(1)} %shard_map.109), channel_id=1, source_target_pairs={{0,64},{8,72},{16,80},{24,88},{32,96},{40,104},{48,112},{56,120},{... | collective-permute-start | bytes 491528 | tf_op jit(solution)/shard_map/ppermute | solution.py:227
  83.2 5.2 %collective-permute-done.19.got = bf16[80,1024]{1,0:T(8,128)(2,1)S(1)} collective-permute-done((bf16[80,1024]{1,0:T(8,128)(2,1)S(1)}, bf16[80,1024]{1,0:T(8,128)(2,1)S(1)}, u32[]{:S(2)}, u32[]{:S(2)}) %collective-permute-start.19) | collective-permute-done | bytes 163872 | tf_op jit(solution)/shard_map/ppermute | solution.py:227
  88.4 1.5 %shard_map.110 = (f32[64,1024]{1,0:T(8,128)}, f32[2,32,128]{2,1,0:T(8,128)}) custom-call(s32[5]{0:T(128)S(1)} %stack.32.pos_ref, s32[16]{0:T(128)S(1)} %copy-done.7, bf16[2,64,1024]{2,1,0:T(8,128)(2,1)S(1)} %get-tuple-element.38.ek, bf16[2,64,1024]{2,1,0:T(8,128)(2,1)S(1)} %collective-permute-done.12.e1, ...), custom_call_target="tpu_custom_call" | custom-call | tf_op jit(solution)/shard_map/pallas_call | solution.py:237
  (45 shorter events, 6.8 us)
Async XLA Ops:
  0.6 47.1 %collective-permute-start.11 = (bf16[512,1024]{1,0:T(8,128)(2,1)}, bf16[512,1024]{1,0:T(8,128)(2,1)S(1)}, u32[]{:S(2)}, u32[]{:S(2)}) collective-permute-start(bf16[512,1024]{1,0:T(8,128)(2,1)} %og_ref.3), channel_id=1, source_target_pairs={{0,8},{8,0},{16,24},{24,16},{32,40},{40,32},{48,56},{56,48},{64,72... | collective-permute-start | bytes 3145736 | tf_op jit(solution)/shard_map/ppermute | solution.py:227
  5.5 42.2 %copy-start.1 = (bf16[512,1024]{1,0:T(8,128)(2,1)S(1)}, bf16[512,1024]{1,0:T(8,128)(2,1)}, u32[]{:S(2)}) copy-start(bf16[512,1024]{1,0:T(8,128)(2,1)} %og_ref.3) | copy-start | bytes 3145732
  5.5 14.9 %collective-permute-start = (bf16[512,512]{1,0:T(8,128)(2,1)S(1)}, bf16[512,512]{1,0:T(8,128)(2,1)S(1)}, u32[]{:S(2)}, u32[]{:S(2)}) collective-permute-start(bf16[512,512]{1,0:T(8,128)(2,1)S(1)} %get-tuple-element.28), channel_id=1, source_target_pairs={{0,1},{1,0},{2,3},{3,2},{4,5},{5,4},{6,7},{7,6},{8,9},{9,8},{10,11... | collective-permute-start | bytes 1572872 | tf_op jit(solution)/shard_map/ppermute | solution.py:227
  7.8 1.3 %collective-permute-start.6 = (bf16[64,512]{1,0:T(8,128)(2,1)S(1)}, bf16[64,512]{1,0:T(8,128)(2,1)S(1)}, u32[]{:S(2)}, u32[]{:S(2)}) collective-permute-start(bf16[64,512]{1,0:T(8,128)(2,1)S(1)} %get-tuple-element.37), channel_id=1, source_target_pairs={{0,8},{8,0},{16,24},{24,16},{32,40},{40,32},{48,56},{56,48},{64,72... | collective-permute-start | bytes 196616 | tf_op jit(solution)/shard_map/ppermute | solution.py:227
  9.1 16.0 %collective-permute-start.7 = (bf16[64,1024]{1,0:T(8,128)(2,1)S(1)}, bf16[64,1024]{1,0:T(8,128)(2,1)S(1)}, u32[]{:S(2)}, u32[]{:S(2)}) collective-permute-start(bf16[64,1024]{1,0:T(8,128)(2,1)S(1)} %constant_dynamic-update-slice_fusion), channel_id=1, source_target_pairs={{0,1},{1,0},{2,3},{3,2},{4,5},{5,4},{6,7},{7,6},{8,9},{9,8},{10,11... | collective-permute-start | bytes 393224 | tf_op jit(solution)/shard_map/ppermute | solution.py:227
  20.5 8.5 %collective-permute-start.1 = (bf16[128,512]{1,0:T(8,128)(2,1)S(1)}, bf16[128,512]{1,0:T(8,128)(2,1)S(1)}, u32[]{:S(2)}, u32[]{:S(2)}) collective-permute-start(bf16[128,512]{1,0:T(8,128)(2,1)S(1)} %get-tuple-element.30), channel_id=1, source_target_pairs={{0,2},{1,3},{2,0},{3,1},{4,6},{5,7},{6,4},{7,5},{8,10},{9,11},{10,... | collective-permute-start | bytes 393224 | tf_op jit(solution)/shard_map/ppermute | solution.py:227
  22.6 10.4 %collective-permute-start.2 = (bf16[128,512]{1,0:T(8,128)(2,1)S(1)}, bf16[128,512]{1,0:T(8,128)(2,1)S(1)}, u32[]{:S(2)}, u32[]{:S(2)}) collective-permute-start(bf16[128,512]{1,0:T(8,128)(2,1)S(1)} %get-tuple-element.31), channel_id=1, source_target_pairs={{0,6},{1,7},{2,4},{3,5},{4,2},{5,3},{6,0},{7,1},{8,14},{9,15},{10,... | collective-permute-start | bytes 393224 | tf_op jit(solution)/shard_map/ppermute | solution.py:227
  25.2 31.9 %copy-start.5 = (bf16[2,128,512]{2,1,0:T(8,128)(2,1)S(1)}, bf16[2,128,512]{2,1,0:T(8,128)(2,1)}, u32[]{:S(2)}) copy-start(bf16[2,128,512]{2,1,0:T(8,128)(2,1)} %f_ref.1) | copy-start | bytes 786436
  25.2 31.9 %copy-start.6 = (bf16[128,512]{1,0:T(8,128)(2,1)S(1)}, bf16[128,512]{1,0:T(8,128)(2,1)}, u32[]{:S(2)}) copy-start(bf16[128,512]{1,0:T(8,128)(2,1)} %x_ref.1) | copy-start | bytes 393220
  25.2 31.9 %copy-start.7 = (s32[16]{0:T(128)S(1)}, s32[16]{0:T(128)}, u32[]{:S(2)}) copy-start(s32[16]{0:T(128)} %reach_ref.3) | copy-start | bytes 196
  25.2 19.5 %collective-permute-start.10 = (bf16[2,64,1024]{2,1,0:T(8,128)(2,1)S(1)}, bf16[2,64,1024]{2,1,0:T(8,128)(2,1)S(1)}, u32[]{:S(2)}, u32[]{:S(2)}) collective-permute-start(bf16[2,64,1024]{2,1,0:T(8,128)(2,1)S(1)} %pad_maximum_fusion.b0), channel_id=1, source_target_pairs={{0,4},{1,5},{2,6},{3,7},{4,0},{5,1},{6,2},{7,3},{8,12},{9,13},{10,... | collective-permute-start | bytes 786440 | tf_op jit(solution)/shard_map/ppermute | solution.py:227
  26.8 20.8 %collective-permute-start.9 = (bf16[2,64,1024]{2,1,0:T(8,128)(2,1)S(1)}, bf16[2,64,1024]{2,1,0:T(8,128)(2,1)S(1)}, u32[]{:S(2)}, u32[]{:S(2)}) collective-permute-start(bf16[2,64,1024]{2,1,0:T(8,128)(2,1)S(1)} %pad_maximum_fusion.b0), channel_id=1, source_target_pairs={{0,6},{1,7},{2,4},{3,5},{4,2},{5,3},{6,0},{7,1},{8,14},{9,15},{10,... | collective-permute-start | bytes 786440 | tf_op jit(solution)/shard_map/ppermute | solution.py:227
  29.0 18.7 %collective-permute-start.8 = (bf16[2,64,1024]{2,1,0:T(8,128)(2,1)S(1)}, bf16[2,64,1024]{2,1,0:T(8,128)(2,1)S(1)}, u32[]{:S(2)}, u32[]{:S(2)}) collective-permute-start(bf16[2,64,1024]{2,1,0:T(8,128)(2,1)S(1)} %pad_maximum_fusion.b0), channel_id=1, source_target_pairs={{0,2},{1,3},{2,0},{3,1},{4,6},{5,7},{6,4},{7,5},{8,10},{9,11},{10,... | collective-permute-start | bytes 786440 | tf_op jit(solution)/shard_map/ppermute | solution.py:227
  32.9 10.3 %collective-permute-start.3 = (bf16[128,512]{1,0:T(8,128)(2,1)S(1)}, bf16[128,512]{1,0:T(8,128)(2,1)S(1)}, u32[]{:S(2)}, u32[]{:S(2)}) collective-permute-start(bf16[128,512]{1,0:T(8,128)(2,1)S(1)} %get-tuple-element.32), channel_id=1, source_target_pairs={{0,4},{1,5},{2,6},{3,7},{4,0},{5,1},{6,2},{7,3},{8,12},{9,13},{10,... | collective-permute-start | bytes 393224 | tf_op jit(solution)/shard_map/ppermute | solution.py:227
  44.0 13.0 %collective-permute-start.5 = (bf16[128,512]{1,0:T(8,128)(2,1)S(1)}, bf16[128,512]{1,0:T(8,128)(2,1)S(1)}, u32[]{:S(2)}, u32[]{:S(2)}) collective-permute-start(bf16[128,512]{1,0:T(8,128)(2,1)S(1)} %get-tuple-element.33.gm_ref), channel_id=1, source_target_pairs={{8,16},{24,32},{40,48},{56,64},{72,80},{88,96},{104,112},{16,8},{3... | collective-permute-start | bytes 393224 | tf_op jit(solution)/shard_map/ppermute | solution.py:285
  44.7 12.4 %collective-permute-start.4 = (bf16[128,512]{1,0:T(8,128)(2,1)S(1)}, bf16[128,512]{1,0:T(8,128)(2,1)S(1)}, u32[]{:S(2)}, u32[]{:S(2)}) collective-permute-start(bf16[128,512]{1,0:T(8,128)(2,1)S(1)} %get-tuple-element.33.gm_ref), channel_id=1, source_target_pairs={{0,8},{8,0},{16,24},{24,16},{32,40},{40,32},{48,56},{56,48},{64,72... | collective-permute-start | bytes 393224 | tf_op jit(solution)/shard_map/ppermute | solution.py:227
  51.3 30.0 %collective-permute-start.12 = (bf16[2,64,1024]{2,1,0:T(8,128)(2,1)S(1)}, bf16[2,64,1024]{2,1,0:T(8,128)(2,1)S(1)}, u32[]{:S(2)}, u32[]{:S(2)}) collective-permute-start(bf16[2,64,1024]{2,1,0:T(8,128)(2,1)S(1)} %get-tuple-element.39), channel_id=1, source_target_pairs={{0,16},{8,24},{16,0},{24,8},{32,48},{40,56},{48,32},{56,40},{64,80... | collective-permute-start | bytes 786440 | tf_op jit(solution)/shard_map/ppermute | solution.py:227
  53.0 28.4 %collective-permute-start.13 = (bf16[2,64,1024]{2,1,0:T(8,128)(2,1)S(1)}, bf16[2,64,1024]{2,1,0:T(8,128)(2,1)S(1)}, u32[]{:S(2)}, u32[]{:S(2)}) collective-permute-start(bf16[2,64,1024]{2,1,0:T(8,128)(2,1)S(1)} %get-tuple-element.40), channel_id=1, source_target_pairs={{0,48},{8,56},{16,32},{24,40},{32,16},{40,24},{48,0},{56,8},{64,11... | collective-permute-start | bytes 786440 | tf_op jit(solution)/shard_map/ppermute | solution.py:227
  55.6 25.8 %collective-permute-start.14 = (bf16[2,64,1024]{2,1,0:T(8,128)(2,1)S(1)}, bf16[2,64,1024]{2,1,0:T(8,128)(2,1)S(1)}, u32[]{:S(2)}, u32[]{:S(2)}) collective-permute-start(bf16[2,64,1024]{2,1,0:T(8,128)(2,1)S(1)} %get-tuple-element.41), channel_id=1, source_target_pairs={{0,32},{8,40},{16,48},{24,56},{32,0},{40,8},{48,16},{56,24},{64,96... | collective-permute-start | bytes 786440 | tf_op jit(solution)/shard_map/ppermute | solution.py:227
  70.6 1.3 %collective-permute-start.15 = (bf16[8,32,256]{2,1,0:T(8,128)(2,1)S(1)}, bf16[8,32,256]{2,1,0:T(8,128)(2,1)S(1)}, u32[]{:S(2)}, u32[]{:S(2)}) collective-permute-start(bf16[8,32,256]{2,1,0:T(8,128)(2,1)S(1)} %get-tuple-element.43), channel_id=1, source_target_pairs={{0,8},{8,0},{16,24},{24,16},{32,40},{40,32},{48,56},{56,48},{64,72... | collective-permute-start | bytes 393224 | tf_op jit(solution)/shard_map/ppermute | solution.py:227
  72.0 4.0 %collective-permute-start.16 = (bf16[2,32,256]{2,1,0:T(8,128)(2,1)S(1)}, bf16[2,32,256]{2,1,0:T(8,128)(2,1)S(1)}, u32[]{:S(2)}, u32[]{:S(2)}) collective-permute-start(bf16[2,32,256]{2,1,0:T(8,128)(2,1)S(1)} %get-tuple-element.45), channel_id=1, source_target_pairs={{0,16},{8,24},{16,0},{24,8},{32,48},{40,56},{48,32},{56,40},{64,80... | collective-permute-start | bytes 98312 | tf_op jit(solution)/shard_map/ppermute | solution.py:227
  72.1 6.1 %collective-permute-start.17 = (bf16[2,32,256]{2,1,0:T(8,128)(2,1)S(1)}, bf16[2,32,256]{2,1,0:T(8,128)(2,1)S(1)}, u32[]{:S(2)}, u32[]{:S(2)}) collective-permute-start(bf16[2,32,256]{2,1,0:T(8,128)(2,1)S(1)} %get-tuple-element.46), channel_id=1, source_target_pairs={{0,48},{8,56},{16,32},{24,40},{32,16},{40,24},{48,0},{56,8},{64,11... | collective-permute-start | bytes 98312 | tf_op jit(solution)/shard_map/ppermute | solution.py:227
  76.0 5.4 %collective-permute-start.18 = (bf16[2,32,256]{2,1,0:T(8,128)(2,1)S(1)}, bf16[2,32,256]{2,1,0:T(8,128)(2,1)S(1)}, u32[]{:S(2)}, u32[]{:S(2)}) collective-permute-start(bf16[2,32,256]{2,1,0:T(8,128)(2,1)S(1)} %get-tuple-element.47), channel_id=1, source_target_pairs={{0,32},{8,40},{16,48},{24,56},{32,0},{40,8},{48,16},{56,24},{64,96... | collective-permute-start | bytes 98312 | tf_op jit(solution)/shard_map/ppermute | solution.py:227
  81.5 6.9 %collective-permute-start.19 = (bf16[80,1024]{1,0:T(8,128)(2,1)S(1)}, bf16[80,1024]{1,0:T(8,128)(2,1)S(1)}, u32[]{:S(2)}, u32[]{:S(2)}) collective-permute-start(bf16[80,1024]{1,0:T(8,128)(2,1)S(1)} %shard_map.109), channel_id=1, source_target_pairs={{0,64},{8,72},{16,80},{24,88},{32,96},{40,104},{48,112},{56,120},{... | collective-permute-start | bytes 491528 | tf_op jit(solution)/shard_map/ppermute | solution.py:227
  (4 other events, 9.9 us)

commit v2 on v1

v2 whole, which is shorter than its diff:
```python
import functools

import jax
import jax.numpy as jnp
from jax import lax
from jax.experimental import pallas as pl
from jax.experimental.pallas import tpu as pltpu
from jax.sharding import PartitionSpec as P


GROUP = 64
VN = 32
F32 = jnp.float32
BF16 = jnp.bfloat16


def iota(shape, dim):
    return lax.broadcasted_iota(jnp.int32, shape, dim)


def dot(a, b, dims=(((1,), (0,)), ((), ()))):
    return lax.dot_general(a, b, dims, preferred_element_type=F32)


NT = (((1,), (1,)), ((), ()))


RELS = (0, 1, 3, 2)


def gate_rows(pos_ref, v_hbm, g_hbm, mine, other, v_ref, g_ref, sems):
    loads = [
        pltpu.make_async_copy(v_hbm, v_ref, sems.at[0]),
        pltpu.make_async_copy(g_hbm, g_ref, sems.at[1]),
    ]
    for load in loads:
        load.start()
    for load in loads:
        load.wait()
    half = mine.shape[0]
    core = pos_ref[4] & 1
    for ref, part in ((mine, core), (other, 1 - core)):
        band = pl.ds(pl.multiple_of(part * half, half), half)
        ref[...] = (v_ref[band, :].astype(F32) * g_ref[band, :].astype(F32)).astype(BF16)


def first_product(pos_ref, w_hbm, og_hbm, keep, send, w_ref, og_ref, sems):
    z = pos_ref[0]
    x = pos_ref[1]
    og_load = pltpu.make_async_copy(og_hbm, og_ref, sems.at[8])
    og_load.start()
    loads = []
    for i, rel in enumerate(RELS):
        for a in range(2):
            rows = pl.ds(pl.multiple_of(((z ^ rel) * 2 + (x ^ a)) * 128, 128), 128)
            part = w_ref.at[i, 128 * a : 128 * (a + 1)]
            loads.append(pltpu.make_async_copy(w_hbm.at[rows], part, sems.at[2 * i + a]))
            loads[-1].start()
    og_load.wait()
    og = og_ref[...]
    for i in range(4):
        loads[2 * i].wait()
        loads[2 * i + 1].wait()
        p = dot(w_ref[i], og, NT).astype(BF16)
        keep[128 * i : 128 * (i + 1), :] = p[:128]
        send[128 * i : 128 * (i + 1), :] = p[128:]


def middle_sums(k_ref, r_ref, *outs):
    n = k_ref.shape[0] // 4
    for i, ref in enumerate(outs):
        band = slice(n * i, n * i + n)
        ref[...] = (k_ref[band, :].astype(F32) + r_ref[band, :].astype(F32)).astype(ref.dtype)


def gate_grads(k_ref, r1, r3, r2, v_ref, g_ref, gate_ref, conv_ref):
    total = k_ref[...] + r1[...].astype(F32) + r3[...].astype(F32) + r2[...].astype(F32)
    gate_ref[...] = total * v_ref[...].astype(F32)
    conv_ref[...] = (total * g_ref[...].astype(F32)).astype(BF16)


def second_product(pos_ref, b0, b1, b3, b2, og_ref, ogs_ref, *refs):
    outs, g_ref = refs[:4], refs[4]
    for i, ref in enumerate((b0, b1, b2, b3)):
        g_ref[i] = ref[0]
        g_ref[4 + i] = ref[1]
    z = pos_ref[0]
    x = pos_ref[1]
    xh = pos_ref[2]
    y = pos_ref[3]
    tok = og_ref.shape[0]
    for ref, rel in zip(outs, RELS):
        for a in range(2):
            j = (xh ^ a) * 4 + (y ^ rel)
            g = g_ref[((j % 2) ^ x) * 4 + ((j // 2) ^ z)]
            ref[a] = (dot(g[:, :tok], og_ref[...]) + dot(g[:, tok:], ogs_ref[...])).astype(BF16)


def lagged(x, shifts, width):
    pair = [pltpu.roll(x, s % width, 1) if s % width else x for s in shifts]
    return jnp.concatenate(pair, axis=0).astype(BF16)


def prepare(pos_ref, reach_ref, f_ref, x_ref, l_ref, ui_ref, uo_ref):
    rows, n = x_ref.shape
    width = 3 * n
    chan = pos_ref[0] * 2 + pos_ref[1]
    own_rows = (iota((128, 256), 0) & 7) == (iota((128, 256), 1) & 7)
    ef = (iota((128, 256), 0) == (iota((128, 256), 1) >> 3)).astype(BF16)
    eb = (iota((128, 256), 0) == (VN - 1) - (iota((128, 256), 1) >> 3)).astype(BF16)
    taps = f_ref.shape[2]
    lag = iota((8, taps), 1)

    def step(i, carry):
        base = pl.multiple_of(i * 16, 16)
        band = pl.ds(base, 16)
        own16 = x_ref[band, :].astype(F32)
        filt16 = [f_ref[d, band, :].astype(F32) for d in range(2)]
        inside = lag < reach_ref[(chan * rows + base) // GROUP]
        zero = jnp.zeros((8, n), F32)
        for h in range(2):
            group = 2 * i + h
            for d, e in ((0, ef), (1, eb)):
                f8 = jnp.where(inside, filt16[d][8 * h : 8 * h + 8], 0.0)
                rolled = [f8 if b == 0 else pltpu.roll(f8, taps - 32 * b, 1) for b in range(4)]
                cut = [rolled[u % 4][:, 128 * (u // 4) : 128 * (u // 4) + 128] for u in range(16)]
                spread = dot(jnp.concatenate(cut, axis=0).astype(BF16), e)
                l_ref[group, d] = jnp.where(own_rows, spread, 0.0).astype(BF16)
            own = jnp.concatenate([zero, own16[8 * h : 8 * h + 8], zero], axis=1)
            bases = (
                (lagged(own, (0, 32), width), lagged(own, (64, 96), width)),
                (lagged(own, (-32, -64), width), lagged(own, (-96, -128), width)),
            )
            for d in range(2):
                for k in range(8):
                    start = n - 128 * (k // 2) if d == 0 else 128 * (k // 2)
                    part = bases[d][k % 2][:, start : start + 2 * n]
                    inner, outer = (part[:, :n], part[:, n:]) if d == 0 else (part[:, n:], part[:, :n])
                    at = 128 * d + 16 * k
                    ui_ref[group, at : at + 16, :] = inner
                    uo_ref[group, at : at + 16, :] = outer
        return carry

    lax.fori_loop(0, rows // 16, step, 0)


def conv_grads(pos_ref, gm_ref, gs_ref, gp_ref, l_ref, ui_ref, uo_ref,
               o_ref, keep_ref, send_ref, h_ref, t_ref):
    rows, n = gm_ref.shape
    width = 3 * n
    lanes = n // 128
    place = pos_ref[4]
    core0 = (place & 1) == 0
    own_cols = iota((16, 8, 256), 1) == (iota((16, 8, 256), 2) & 7)

    def step(i, carry):
        band = pl.ds(pl.multiple_of(i * 16, 16), 16)
        gm = gm_ref[band, :].astype(F32)
        gs = gs_ref[band, :].astype(F32)
        gp = gp_ref[band, :].astype(F32)
        ext16 = jnp.concatenate([jnp.where(core0, gp, gs), gm, jnp.where(core0, gs, gp)], axis=1)
        outs = []
        for h in range(2):
            group = 2 * i + h
            ext = ext16[8 * h : 8 * h + 8]
            two = jnp.concatenate([ext, pltpu.roll(ext, width - 1, 1)], axis=0).astype(BF16)
            for k in range(VN // 2):
                moved = two if k == 0 else pltpu.roll(two, width - 2 * k, 1)
                h_ref[h, 16 * k : 16 * k + 16, :] = moved
            total = None
            for d in range(2):
                acc = [[None] * (lanes + (b > 0)) for b in range(4)]
                for j in range(lanes):
                    if d == 0:
                        lo, hi = (0, 64) if j == 0 else (64, 128) if j == lanes - 1 else (0, 128)
                    else:
                        lo, hi = (48, 128) if j == 0 else (0, 64) if j == lanes - 1 else (0, 128)
                    at = n * (1 - d) + 256 * j
                    p = dot(l_ref[group, d, lo:hi, :], h_ref[h, :, at : at + 256])
                    for u in range(lo // 8, hi // 8):
                        a, b = divmod(u + d, 4)
                        for c in range(2):
                            q = 2 * j + c
                            slot = q - a if d == 0 else q - (lanes - (b > 0)) + a
                            if 0 <= slot < len(acc[b]):
                                part = p[8 * u - lo : 8 * u - lo + 8, 128 * c : 128 * c + 128]
                                acc[b][slot] = part if acc[b][slot] is None else acc[b][slot] + part
                for b in range(4):
                    line = jnp.concatenate(acc[b], axis=1)
                    if b and d == 0:
                        line = pltpu.roll(line, n + 128 - 32 * b, 1)[:, :n]
                    elif b:
                        line = pltpu.roll(line, 32 * b, 1)[:, 128:]
                    total = line if total is None else total + line
            outs.append(total)
            inner = dot(ui_ref[group], h_ref[h, :, n : 2 * n], NT)
            for d in range(2):
                start = 2 * n * (1 - d)
                cross = inner[128 * d : 128 * d + 128] + dot(
                    uo_ref[group, 128 * d : 128 * d + 128, :], h_ref[h, :, start : start + n], NT
                )
                sums = jnp.sum(jnp.where(own_cols, cross.reshape(16, 8, 256), 0.0), axis=1)
                row = d * (rows // 8) + group
                for u in range(16):
                    r = u ^ place
                    slot = (r & 1) * 8 + ((r >> 1) & 3) * 2 + (r >> 3)
                    t_ref[slot, pl.ds(row, 1), :] = sums[u : u + 1]
        o_ref[band, :] = jnp.concatenate(outs, axis=0)
        return carry

    lax.fori_loop(0, rows // 16, step, 0)
    keep_ref[...] = t_ref[0:8]
    send_ref[...] = t_ref[8:16].astype(BF16)


def split_taps(t_ref, got_ref, k, s1, s3, s2):
    for rel, ref in ((0, k), (1, s1), (3, s3), (2, s2)):
        both = t_ref[2 * rel : 2 * rel + 2] + got_ref[2 * rel : 2 * rel + 2].astype(F32)
        ref[...] = both.astype(ref.dtype)


def sum_pieces(k, r1, r3, r2, keep, send):
    for ref, i in ((keep, 0), (send, 1)):
        total = k[i].astype(F32)
        for r in (r1, r3, r2):
            total = total + r[i].astype(F32)
        ref[...] = total.astype(ref.dtype)


def finish_rows(keep, got, o_ref, *, scale):
    o_ref[...] = (keep[...] + got[...].astype(F32)) * scale


def finish_taps(pos_ref, reach_ref, part_ref, got, t_ref, *, scale):
    f = part_ref[...] + got[...].astype(F32)
    chan = pos_ref[0] * 2 + pos_ref[1]
    place = pos_ref[4]
    own_cols = iota((16, 8, 256), 1) == (iota((16, 8, 256), 2) & 7)
    first = chan * 128 // GROUP
    limit = jnp.where(iota((VN, 128), 1) < GROUP, reach_ref[first], reach_ref[first + 1])
    inside = place * VN + iota((VN, 128), 0) < limit
    for d in range(2):
        v = iota((VN, 256), 1) >> 3
        e = (iota((VN, 256), 0) == (v if d == 0 else (VN - 1) - v)).astype(BF16)
        part = f[16 * d : 16 * d + 16, :]
        spread = jnp.broadcast_to(part[:, None, :], (16, 8, 256))
        spread = jnp.where(own_cols, spread, 0.0).reshape(128, 256)
        high = spread.astype(BF16)
        low = (spread - high.astype(F32)).astype(BF16)
        t_ref[d] = jnp.where(inside, (dot(e, high, NT) + dot(e, low, NT)) * scale, 0.0)


def swap(v, axis, mask):
    return lax.ppermute(v, axis, [(i, i ^ mask) for i in range(lax.axis_size(axis))])


def smem():
    return pl.BlockSpec(memory_space=pltpu.SMEM)


def call(body, out_shape, args, scalars=1, scratch=(), limit=16, held_in=pltpu.VMEM):
    vmem = pl.BlockSpec(memory_space=pltpu.VMEM)
    where = pl.BlockSpec(memory_space=held_in)
    held = [pltpu.with_memory_space_constraint(a, held_in) for a in args[scalars:]]
    return pl.pallas_call(
        body,
        out_shape=out_shape,
        in_specs=[smem()] * scalars + [where] * len(held),
        out_specs=jax.tree.map(lambda _: vmem, out_shape),
        scratch_shapes=list(scratch),
        compiler_params=pltpu.CompilerParams(vmem_limit_bytes=limit << 20),
    )(*args[:scalars], *held)


def on_device_0(out_grad, out_weight, conv_input, gate_values, conv_output, filters, filter_reach):
    shape = jax.ShapeDtypeStruct
    rows, tok = conv_input.shape
    feats = out_grad.shape[1]
    seq_count = lax.axis_size("seq")
    place = lax.axis_index("seq").astype(jnp.int32)
    chan = lax.axis_index("chan").astype(jnp.int32)
    pos = jnp.stack([chan >> 1, chan & 1, place >> 3, (place >> 1) & 3, place])
    half = rows // 2
    scale = 1.0 / float(tok * seq_count) ** 0.5

    mine, other = call(
        gate_rows,
        [shape((half, tok), BF16)] * 2,
        (pos, conv_output, gate_values),
        scratch=[pltpu.VMEM((rows, tok), BF16)] * 2 + [pltpu.SemaphoreType.DMA((2,))],
        held_in=pltpu.HBM,
    )
    own = jnp.concatenate([mine, swap(other, "seq", 1)], axis=1)
    og_core = swap(out_grad, "seq", 1)
    pair = jnp.stack([own, swap(own, "chan", 1)])
    b1 = swap(pair, "chan", 2)
    b3 = swap(pair, "chan", 6)
    b2 = swap(pair, "chan", 4)

    keep, send = call(
        first_product,
        [shape((rows * 4, tok), BF16)] * 2,
        (pos, out_weight, out_grad),
        scratch=[
            pltpu.VMEM((4, 2 * rows, feats), BF16),
            pltpu.VMEM((tok, feats), BF16),
            pltpu.SemaphoreType.DMA((9,)),
        ],
        held_in=pltpu.HBM,
    )
    keep, s1, s3, s2 = call(
        middle_sums,
        [shape((rows, tok), F32)] + [shape((rows, tok), BF16)] * 3,
        (keep, swap(send, "chan", 1)),
        scalars=0,
    )
    s1, s3, s2 = swap(s1, "chan", 2), swap(s3, "chan", 6), swap(s2, "chan", 4)
    grad_gate, grad_conv = call(
        gate_grads,
        [shape((rows, tok), F32), shape((rows, tok), BF16)],
        (keep, s1, s3, s2, conv_output, gate_values),
        scalars=0,
    )

    halo_core = swap(grad_conv, "seq", 1)
    pairs = [(i, i + 1) for i in range(1, seq_count - 1, 2)]
    halo_out = lax.ppermute(grad_conv, "seq", pairs + [(b, a) for a, b in pairs])

    e = call(
        second_product,
        [shape((2, half, feats), BF16)] * 4,
        (pos, pair, b1, b3, b2, out_grad, og_core),
        scratch=[pltpu.VMEM((8, half, 2 * tok), BF16)],
    )
    e = [e[0], swap(e[1], "seq", 2), swap(e[2], "seq", 6), swap(e[3], "seq", 4)]

    groups = rows // 8
    prepared = call(
        prepare,
        [
            shape((groups, 2, 128, 256), BF16),
            shape((groups, 256, tok), BF16),
            shape((groups, 256, tok), BF16),
        ],
        (pos, filter_reach, filters, conv_input),
        scalars=2,
    )
    grad_input, tap_keep, tap_send = call(
        conv_grads,
        [
            shape((rows, tok), F32),
            shape((8, rows // 4, 256), F32),
            shape((8, rows // 4, 256), BF16),
        ],
        (pos, grad_conv, halo_core, halo_out, *prepared),
        scratch=[
            pltpu.VMEM((2, 256, 3 * tok), BF16),
            pltpu.VMEM((16, rows // 4, 256), F32),
        ],
    )
    f_got = swap(tap_send, "seq", 1)
    piece = (2, rows // 4, 256)
    f = call(
        split_taps, [shape(piece, F32)] + [shape(piece, BF16)] * 3,
        (tap_keep, f_got), scalars=0,
    )
    f = [f[0], swap(f[1], "seq", 2), swap(f[2], "seq", 6), swap(f[3], "seq", 4)]
    e_keep, e_send = call(
        sum_pieces, [shape((half, feats), F32), shape((half, feats), BF16)], e, scalars=0
    )
    e_got = swap(e_send, "seq", 8)
    f_keep, f_send = call(sum_pieces, [shape(piece[1:], F32), shape(piece[1:], BF16)], f, scalars=0)
    f_got = swap(f_send, "seq", 8)
    grad_weight = call(
        functools.partial(finish_rows, scale=scale),
        shape((half, feats), F32),
        (e_keep, e_got),
        scalars=0,
    )
    grad_filters = call(
        functools.partial(finish_taps, scale=scale),
        shape((2, VN, rows), F32),
        (pos, filter_reach, f_keep, f_got),
        scalars=2,
    )
    return (grad_input, grad_gate, grad_weight, jnp.transpose(grad_filters, (0, 2, 1)))


def solution(mesh):
    return jax.shard_map(
        on_device_0,
        mesh=mesh,
        in_specs=(
            P("seq", "chan"),
            P(None, "chan"),
            P("chan", "seq"),
            P("chan", "seq"),
            P("chan", "seq"),
            P(None, "chan", None),
            P(),
        ),
        out_specs=(P("chan", "seq"), P("chan", "seq"), P("seq", "chan"), P(None, "chan", "seq")),
        check_vma=False,
    )
```

time: 90.1 us -> 89.8 us (level)
  waiting for transfers between devices: 32.2 us -> 27.3 us
  Pallas kernels: 22.1 us -> 26.8 us
  local copies, waits for them, and re-layouts: 2.94 us -> 0.12 us
  starting transfers between devices: 31.8 us -> 34.6 us
    ppermute x19 -> x20, waiting for transfers between devices: 32.2 us -> 27.3 us  [swap(): lax.ppermute(v, axis, [(i, i ^ mask) for i in range(lax.axis_size(axis))])]
    pallas_call x9 -> x12, Pallas kernels: 22.1 us -> 26.8 us  [call(): pl.pallas_call(body, out_shape=out_shape, in_specs=[smem()] * scalars + [...]
    unnamed x17 -> x13, local copies, waits for them, and re-layouts: 2.85 us -> 0.03 us
    ppermute x19 -> x20, starting transfers between devices: 31.2 us -> 33.9 us  [swap(): lax.ppermute(v, axis, [(i, i ^ mask) for i in range(lax.axis_size(axis))])]
  transfers between devices with their start and end apart: 20 -> 21, of which waited for: 8 -> 7; matrix products, arithmetic and copies ran while one was open for 0% -> 0% of each run, Pallas kernels for 23% -> 29%
where the time goes in v2:
time: 89.8 us; the launch traced here: 89.7 us
  starting transfers between devices  34.6 us (39%)
  waiting for transfers between devices  27.3 us (30%)
  Pallas kernels  26.8 us (30%)
    ppermute x20, starting transfers between devices, swap(): lax.ppermute(v, axis, [(i, i ^ mask) for i in range(lax.axis_size(axis))])  33.9 us
    ppermute x20, waiting for transfers between devices, swap(): lax.ppermute(v, axis, [(i, i ^ mask) for i in range(lax.axis_size(axis))])  27.3 us
    pallas_call x12, Pallas kernels, call(): pl.pallas_call(body, out_shape=out_shape, in_specs=[smem()] * scalars + [...  26.8 us
  transfers between devices with their start and end apart: 21, of which 7 were waited for; matrix products, arithmetic and copies ran while one was open for 0% of the time, Pallas kernels for 29%

profile of v2, /device:TPU:0, one launch (start us, length us, event | category | flops | bytes accessed | tf_op | source)
XLA Modules:
  0.0 89.7 jit_solution(11257522329344686667)
XLA Ops:
  0.9 3.9 %shard_map.102 = (bf16[512,512]{1,0:T(8,128)(2,1)S(1)}, bf16[512,512]{1,0:T(8,128)(2,1)S(1)}) custom-call(s32[5]{0:T(128)S(1)} %stack.32.pos_ref, bf16[1024,1024]{1,0:T(8,128)(2,1)} %w_hbm.1, bf16[512,1024]{1,0:T(8,128)(2,1)} %og_ref.1), custom_call_target="tpu_custom_call" | custom-call | tf_op jit(solution)/shard_map/pallas_call | solution.py:265
  4.7 1.7 %collective-permute-start = (bf16[512,512]{1,0:T(8,128)(2,1)S(1)}, bf16[512,512]{1,0:T(8,128)(2,1)S(1)}, u32[]{:S(2)}, u32[]{:S(2)}) collective-permute-start(bf16[512,512]{1,0:T(8,128)(2,1)S(1)} %get-tuple-element.33), channel_id=1, source_target_pairs={{0,1},{1,0},{2,3},{3,2},{4,5},{5,4},{6,7},{7,6},{8,9},{9,8},{10,11... | collective-permute-start | bytes 1572872 | tf_op jit(solution)/shard_map/ppermute | solution.py:254
  6.4 1.6 %shard_map.107 = (bf16[64,512]{1,0:T(8,128)(2,1)S(1)}, bf16[64,512]{1,0:T(8,128)(2,1)S(1)}) custom-call(s32[5]{0:T(128)S(1)} %stack.32.pos_ref, bf16[128,512]{1,0:T(8,128)(2,1)} %v_hbm.1, bf16[128,512]{1,0:T(8,128)(2,1)} %g_hbm.1), custom_call_target="tpu_custom_call" | custom-call | tf_op jit(solution)/shard_map/pallas_call | solution.py:265
  9.8 12.2 %collective-permute-done.7 = bf16[64,1024]{1,0:T(8,128)(2,1)S(1)} collective-permute-done((bf16[64,1024]{1,0:T(8,128)(2,1)S(1)}, bf16[64,1024]{1,0:T(8,128)(2,1)S(1)}, u32[]{:S(2)}, u32[]{:S(2)}) %collective-permute-start.7) | collective-permute-done | bytes 131104 | tf_op jit(solution)/shard_map/ppermute | solution.py:254
  22.0 4.1 %collective-permute-start.10 = (bf16[2,64,1024]{2,1,0:T(8,128)(2,1)S(1)}, bf16[2,64,1024]{2,1,0:T(8,128)(2,1)S(1)}, u32[]{:S(2)}, u32[]{:S(2)}) collective-permute-start(bf16[2,64,1024]{2,1,0:T(8,128)(2,1)S(1)} %pad_maximum_fusion.b0), channel_id=1, source_target_pairs={{0,4},{1,5},{2,6},{3,7},{4,0},{5,1},{6,2},{7,3},{8,12},{9,13},{10,... | collective-permute-start | bytes 786440 | tf_op jit(solution)/shard_map/ppermute | solution.py:254
  27.2 1.2 %collective-permute-start.1 = (bf16[128,512]{1,0:T(8,128)(2,1)S(1)}, bf16[128,512]{1,0:T(8,128)(2,1)S(1)}, u32[]{:S(2)}, u32[]{:S(2)}) collective-permute-start(bf16[128,512]{1,0:T(8,128)(2,1)S(1)} %get-tuple-element.35), channel_id=1, source_target_pairs={{0,2},{1,3},{2,0},{3,1},{4,6},{5,7},{6,4},{7,5},{8,10},{9,11},{10,... | collective-permute-start | bytes 393224 | tf_op jit(solution)/shard_map/ppermute | solution.py:254
  28.4 4.8 %collective-permute-done.10.b2 = bf16[2,64,1024]{2,1,0:T(8,128)(2,1)S(1)} collective-permute-done((bf16[2,64,1024]{2,1,0:T(8,128)(2,1)S(1)}, bf16[2,64,1024]{2,1,0:T(8,128)(2,1)S(1)}, u32[]{:S(2)}, u32[]{:S(2)}) %collective-permute-start.10) | collective-permute-done | bytes 262176 | tf_op jit(solution)/shard_map/ppermute | solution.py:254
  33.2 3.7 %collective-permute-start.2 = (bf16[128,512]{1,0:T(8,128)(2,1)S(1)}, bf16[128,512]{1,0:T(8,128)(2,1)S(1)}, u32[]{:S(2)}, u32[]{:S(2)}) collective-permute-start(bf16[128,512]{1,0:T(8,128)(2,1)S(1)} %get-tuple-element.36), channel_id=1, source_target_pairs={{0,6},{1,7},{2,4},{3,5},{4,2},{5,3},{6,0},{7,1},{8,14},{9,15},{10,... | collective-permute-start | bytes 393224 | tf_op jit(solution)/shard_map/ppermute | solution.py:254
  36.9 2.9 %collective-permute-done.8.b1 = bf16[2,64,1024]{2,1,0:T(8,128)(2,1)S(1)} collective-permute-done((bf16[2,64,1024]{2,1,0:T(8,128)(2,1)S(1)}, bf16[2,64,1024]{2,1,0:T(8,128)(2,1)S(1)}, u32[]{:S(2)}, u32[]{:S(2)}) %collective-permute-start.8) | collective-permute-done | bytes 262176 | tf_op jit(solution)/shard_map/ppermute | solution.py:254
  39.9 1.2 %collective-permute-start.3 = (bf16[128,512]{1,0:T(8,128)(2,1)S(1)}, bf16[128,512]{1,0:T(8,128)(2,1)S(1)}, u32[]{:S(2)}, u32[]{:S(2)}) collective-permute-start(bf16[128,512]{1,0:T(8,128)(2,1)S(1)} %get-tuple-element.37), channel_id=1, source_target_pairs={{0,4},{1,5},{2,6},{3,7},{4,0},{5,1},{6,2},{7,3},{8,12},{9,13},{10,... | collective-permute-start | bytes 393224 | tf_op jit(solution)/shard_map/ppermute | solution.py:254
  41.0 3.6 %shard_map.108 = (bf16[2,64,1024]{2,1,0:T(8,128)(2,1)S(1)}, bf16[2,64,1024]{2,1,0:T(8,128)(2,1)S(1)}, bf16[2,64,1024]{2,1,0:T(8,128)(2,1)S(1)}, bf16[2,64,1024]{2,1,0:T(8,128)(2,1)S(1)}) custom-call(s32[5]{0:T(128)S(1)} %stack.32.pos_ref, bf16[2,64,1024]{2,1,0:T(8,128)(2,1)S(1)} %pad_maximum_fusion.b0, bf16[2,64,1024]{2,1,0:T(8,128)(2,1)S(1)} %collective-permute-done.8.b1, ...), custom_call_target="tpu_custom_call" | custom-call | tf_op jit(solution)/shard_map/pallas_call | solution.py:265
  44.7 1.7 %collective-permute-start.12 = (bf16[2,64,1024]{2,1,0:T(8,128)(2,1)S(1)}, bf16[2,64,1024]{2,1,0:T(8,128)(2,1)S(1)}, u32[]{:S(2)}, u32[]{:S(2)}) collective-permute-start(bf16[2,64,1024]{2,1,0:T(8,128)(2,1)S(1)} %get-tuple-element.47), channel_id=1, source_target_pairs={{0,16},{8,24},{16,0},{24,8},{32,48},{40,56},{48,32},{56,40},{64,80... | collective-permute-start | bytes 786440 | tf_op jit(solution)/shard_map/ppermute | solution.py:254
  46.3 2.2 %collective-permute-start.13 = (bf16[2,64,1024]{2,1,0:T(8,128)(2,1)S(1)}, bf16[2,64,1024]{2,1,0:T(8,128)(2,1)S(1)}, u32[]{:S(2)}, u32[]{:S(2)}) collective-permute-start(bf16[2,64,1024]{2,1,0:T(8,128)(2,1)S(1)} %get-tuple-element.48), channel_id=1, source_target_pairs={{0,48},{8,56},{16,32},{24,40},{32,16},{40,24},{48,0},{56,8},{64,11... | collective-permute-start | bytes 786440 | tf_op jit(solution)/shard_map/ppermute | solution.py:254
  50.7 3.0 %shard_map.105 = (bf16[16,2,128,256]{3,2,1,0:T(8,128)(2,1)S(1)}, bf16[16,256,512]{2,1,0:T(8,128)(2,1)S(1)}, bf16[16,256,512]{2,1,0:T(8,128)(2,1)S(1)}) custom-call(s32[5]{0:T(128)S(1)} %stack.32.pos_ref, s32[16]{0:T(128)S(1)} %copy-done.5, bf16[2,128,512]{2,1,0:T(8,128)(2,1)S(1)} %copy-done.3, bf16[128,512]{1,0:T(8,128)(2,1)S(1)} %copy-done.4), custom_call_target="tpu_custom_call" | custom-call | tf_op jit(solution)/shard_map/pallas_call | solution.py:265
  53.7 11.6 %shard_map.106 = (f32[128,512]{1,0:T(8,128)}, f32[8,32,256]{2,1,0:T(8,128)S(1)}, bf16[8,32,256]{2,1,0:T(8,128)(2,1)S(1)}) custom-call(s32[5]{0:T(128)S(1)} %stack.32.pos_ref, bf16[128,512]{1,0:T(8,128)(2,1)S(1)} %get-tuple-element.38.gm_ref, bf16[128,512]{1,0:T(8,128)(2,1)S(1)} %collective-permute-done.4.gs_ref, ...), custom_call_target="tpu_custom_call" | custom-call | tf_op jit(solution)/shard_map/pallas_call | solution.py:265
  65.3 3.8 %collective-permute-start.16 = (bf16[8,32,256]{2,1,0:T(8,128)(2,1)S(1)}, bf16[8,32,256]{2,1,0:T(8,128)(2,1)S(1)}, u32[]{:S(2)}, u32[]{:S(2)}) collective-permute-start(bf16[8,32,256]{2,1,0:T(8,128)(2,1)S(1)} %get-tuple-element.53), channel_id=1, source_target_pairs={{0,8},{8,0},{16,24},{24,16},{32,40},{40,32},{48,56},{56,48},{64,72... | collective-permute-start | bytes 393224 | tf_op jit(solution)/shard_map/ppermute | solution.py:254
  69.2 6.0 %collective-permute-start.15 = (bf16[64,1024]{1,0:T(8,128)(2,1)S(1)}, bf16[64,1024]{1,0:T(8,128)(2,1)S(1)}, u32[]{:S(2)}, u32[]{:S(2)}) collective-permute-start(bf16[64,1024]{1,0:T(8,128)(2,1)S(1)} %get-tuple-element.51), channel_id=1, source_target_pairs={{0,64},{8,72},{16,80},{24,88},{32,96},{40,104},{48,112},{56,120},{... | collective-permute-start | bytes 393224 | tf_op jit(solution)/shard_map/ppermute | solution.py:254
  75.3 1.5 %collective-permute-start.18 = (bf16[2,32,256]{2,1,0:T(8,128)(2,1)S(1)}, bf16[2,32,256]{2,1,0:T(8,128)(2,1)S(1)}, u32[]{:S(2)}, u32[]{:S(2)}) collective-permute-start(bf16[2,32,256]{2,1,0:T(8,128)(2,1)S(1)} %get-tuple-element.56), channel_id=1, source_target_pairs={{0,48},{8,56},{16,32},{24,40},{32,16},{40,24},{48,0},{56,8},{64,11... | collective-permute-start | bytes 98312 | tf_op jit(solution)/shard_map/ppermute | solution.py:254
  76.8 2.6 %collective-permute-start.19 = (bf16[2,32,256]{2,1,0:T(8,128)(2,1)S(1)}, bf16[2,32,256]{2,1,0:T(8,128)(2,1)S(1)}, u32[]{:S(2)}, u32[]{:S(2)}) collective-permute-start(bf16[2,32,256]{2,1,0:T(8,128)(2,1)S(1)} %get-tuple-element.57), channel_id=1, source_target_pairs={{0,32},{8,40},{16,48},{24,56},{32,0},{40,8},{48,16},{56,24},{64,96... | collective-permute-start | bytes 98312 | tf_op jit(solution)/shard_map/ppermute | solution.py:254
  79.4 1.1 %collective-permute-done.18.r3 = bf16[2,32,256]{2,1,0:T(8,128)(2,1)S(1)} collective-permute-done((bf16[2,32,256]{2,1,0:T(8,128)(2,1)S(1)}, bf16[2,32,256]{2,1,0:T(8,128)(2,1)S(1)}, u32[]{:S(2)}, u32[]{:S(2)}) %collective-permute-start.18) | collective-permute-done | bytes 32800 | tf_op jit(solution)/shard_map/ppermute | solution.py:254
  80.5 1.7 %collective-permute-done.19.r2 = bf16[2,32,256]{2,1,0:T(8,128)(2,1)S(1)} collective-permute-done((bf16[2,32,256]{2,1,0:T(8,128)(2,1)S(1)}, bf16[2,32,256]{2,1,0:T(8,128)(2,1)S(1)}, u32[]{:S(2)}, u32[]{:S(2)}) %collective-permute-start.19) | collective-permute-done | bytes 32800 | tf_op jit(solution)/shard_map/ppermute | solution.py:254
  82.3 1.8 %collective-permute-start.20 = (bf16[32,256]{1,0:T(8,128)(2,1)S(1)}, bf16[32,256]{1,0:T(8,128)(2,1)S(1)}, u32[]{:S(2)}, u32[]{:S(2)}) collective-permute-start(bf16[32,256]{1,0:T(8,128)(2,1)S(1)} %get-tuple-element.59), channel_id=1, source_target_pairs={{0,64},{8,72},{16,80},{24,88},{32,96},{40,104},{48,112},{56,120},{... | collective-permute-start | bytes 49160 | tf_op jit(solution)/shard_map/ppermute | solution.py:254
  84.1 3.5 %collective-permute-done.20.got = bf16[32,256]{1,0:T(8,128)(2,1)S(1)} collective-permute-done((bf16[32,256]{1,0:T(8,128)(2,1)S(1)}, bf16[32,256]{1,0:T(8,128)(2,1)S(1)}, u32[]{:S(2)}, u32[]{:S(2)}) %collective-permute-start.20) | collective-permute-done | bytes 16416 | tf_op jit(solution)/shard_map/ppermute | solution.py:254
  87.6 1.4 %shard_map.113 = f32[2,32,128]{2,1,0:T(8,128)} custom-call(s32[5]{0:T(128)S(1)} %stack.32.pos_ref, s32[16]{0:T(128)S(1)} %copy-done.5, f32[32,256]{1,0:T(8,128)S(1)} %get-tuple-element.58.part_ref, bf16[32,256]{1,0:T(8,128)(2,1)S(1)} %collective-permute-done.20.got), custom_call_target="tpu_custom_call" | custom-call | tf_op jit(solution)/shard_map/pallas_call | solution.py:265
  (46 shorter events, 6.4 us)
Async XLA Ops:
  0.6 40.4 %collective-permute-start.11 = (bf16[512,1024]{1,0:T(8,128)(2,1)}, bf16[512,1024]{1,0:T(8,128)(2,1)S(1)}, u32[]{:S(2)}, u32[]{:S(2)}) collective-permute-start(bf16[512,1024]{1,0:T(8,128)(2,1)} %og_ref.1), channel_id=1, source_target_pairs={{0,8},{8,0},{16,24},{24,16},{32,40},{40,32},{48,56},{56,48},{64,72... | collective-permute-start | bytes 3145736 | tf_op jit(solution)/shard_map/ppermute | solution.py:254
  0.8 49.9 %copy-start.3 = (bf16[2,128,512]{2,1,0:T(8,128)(2,1)S(1)}, bf16[2,128,512]{2,1,0:T(8,128)(2,1)}, u32[]{:S(2)}) copy-start(bf16[2,128,512]{2,1,0:T(8,128)(2,1)} %f_ref.1) | copy-start | bytes 786436
  0.8 49.9 %copy-start.4 = (bf16[128,512]{1,0:T(8,128)(2,1)S(1)}, bf16[128,512]{1,0:T(8,128)(2,1)}, u32[]{:S(2)}) copy-start(bf16[128,512]{1,0:T(8,128)(2,1)} %x_ref.1) | copy-start | bytes 393220
  0.8 49.9 %copy-start.5 = (s32[16]{0:T(128)S(1)}, s32[16]{0:T(128)}, u32[]{:S(2)}) copy-start(s32[16]{0:T(128)} %reach_ref.3) | copy-start | bytes 196
  4.7 22.3 %collective-permute-start = (bf16[512,512]{1,0:T(8,128)(2,1)S(1)}, bf16[512,512]{1,0:T(8,128)(2,1)S(1)}, u32[]{:S(2)}, u32[]{:S(2)}) collective-permute-start(bf16[512,512]{1,0:T(8,128)(2,1)S(1)} %get-tuple-element.33), channel_id=1, source_target_pairs={{0,1},{1,0},{2,3},{3,2},{4,5},{5,4},{6,7},{7,6},{8,9},{9,8},{10,11... | collective-permute-start | bytes 1572872 | tf_op jit(solution)/shard_map/ppermute | solution.py:254
  8.0 1.3 %collective-permute-start.6 = (bf16[64,512]{1,0:T(8,128)(2,1)S(1)}, bf16[64,512]{1,0:T(8,128)(2,1)S(1)}, u32[]{:S(2)}, u32[]{:S(2)}) collective-permute-start(bf16[64,512]{1,0:T(8,128)(2,1)S(1)} %get-tuple-element.45), channel_id=1, source_target_pairs={{0,8},{8,0},{16,24},{24,16},{32,40},{40,32},{48,56},{56,48},{64,72... | collective-permute-start | bytes 196616 | tf_op jit(solution)/shard_map/ppermute | solution.py:254
  9.3 12.6 %collective-permute-start.7 = (bf16[64,1024]{1,0:T(8,128)(2,1)S(1)}, bf16[64,1024]{1,0:T(8,128)(2,1)S(1)}, u32[]{:S(2)}, u32[]{:S(2)}) collective-permute-start(bf16[64,1024]{1,0:T(8,128)(2,1)S(1)} %constant_dynamic-update-slice_fusion), channel_id=1, source_target_pairs={{0,1},{1,0},{2,3},{3,2},{4,5},{5,4},{6,7},{7,6},{8,9},{9,8},{10,11... | collective-permute-start | bytes 393224 | tf_op jit(solution)/shard_map/ppermute | solution.py:254
  22.0 11.2 %collective-permute-start.10 = (bf16[2,64,1024]{2,1,0:T(8,128)(2,1)S(1)}, bf16[2,64,1024]{2,1,0:T(8,128)(2,1)S(1)}, u32[]{:S(2)}, u32[]{:S(2)}) collective-permute-start(bf16[2,64,1024]{2,1,0:T(8,128)(2,1)S(1)} %pad_maximum_fusion.b0), channel_id=1, source_target_pairs={{0,4},{1,5},{2,6},{3,7},{4,0},{5,1},{6,2},{7,3},{8,12},{9,13},{10,... | collective-permute-start | bytes 786440 | tf_op jit(solution)/shard_map/ppermute | solution.py:254
  26.0 13.8 %collective-permute-start.8 = (bf16[2,64,1024]{2,1,0:T(8,128)(2,1)S(1)}, bf16[2,64,1024]{2,1,0:T(8,128)(2,1)S(1)}, u32[]{:S(2)}, u32[]{:S(2)}) collective-permute-start(bf16[2,64,1024]{2,1,0:T(8,128)(2,1)S(1)} %pad_maximum_fusion.b0), channel_id=1, source_target_pairs={{0,2},{1,3},{2,0},{3,1},{4,6},{5,7},{6,4},{7,5},{8,10},{9,11},{10,... | collective-permute-start | bytes 786440 | tf_op jit(solution)/shard_map/ppermute | solution.py:254
  27.0 14.0 %collective-permute-start.9 = (bf16[2,64,1024]{2,1,0:T(8,128)(2,1)S(1)}, bf16[2,64,1024]{2,1,0:T(8,128)(2,1)S(1)}, u32[]{:S(2)}, u32[]{:S(2)}) collective-permute-start(bf16[2,64,1024]{2,1,0:T(8,128)(2,1)S(1)} %pad_maximum_fusion.b0), channel_id=1, source_target_pairs={{0,6},{1,7},{2,4},{3,5},{4,2},{5,3},{6,0},{7,1},{8,14},{9,15},{10,... | collective-permute-start | bytes 786440 | tf_op jit(solution)/shard_map/ppermute | solution.py:254
  27.2 21.3 %collective-permute-start.1 = (bf16[128,512]{1,0:T(8,128)(2,1)S(1)}, bf16[128,512]{1,0:T(8,128)(2,1)S(1)}, u32[]{:S(2)}, u32[]{:S(2)}) collective-permute-start(bf16[128,512]{1,0:T(8,128)(2,1)S(1)} %get-tuple-element.35), channel_id=1, source_target_pairs={{0,2},{1,3},{2,0},{3,1},{4,6},{5,7},{6,4},{7,5},{8,10},{9,11},{10,... | collective-permute-start | bytes 393224 | tf_op jit(solution)/shard_map/ppermute | solution.py:254
  33.2 16.0 %collective-permute-start.2 = (bf16[128,512]{1,0:T(8,128)(2,1)S(1)}, bf16[128,512]{1,0:T(8,128)(2,1)S(1)}, u32[]{:S(2)}, u32[]{:S(2)}) collective-permute-start(bf16[128,512]{1,0:T(8,128)(2,1)S(1)} %get-tuple-element.36), channel_id=1, source_target_pairs={{0,6},{1,7},{2,4},{3,5},{4,2},{5,3},{6,0},{7,1},{8,14},{9,15},{10,... | collective-permute-start | bytes 393224 | tf_op jit(solution)/shard_map/ppermute | solution.py:254
  39.9 9.4 %collective-permute-start.3 = (bf16[128,512]{1,0:T(8,128)(2,1)S(1)}, bf16[128,512]{1,0:T(8,128)(2,1)S(1)}, u32[]{:S(2)}, u32[]{:S(2)}) collective-permute-start(bf16[128,512]{1,0:T(8,128)(2,1)S(1)} %get-tuple-element.37), channel_id=1, source_target_pairs={{0,4},{1,5},{2,6},{3,7},{4,0},{5,1},{6,2},{7,3},{8,12},{9,13},{10,... | collective-permute-start | bytes 393224 | tf_op jit(solution)/shard_map/ppermute | solution.py:254
  44.7 24.4 %collective-permute-start.12 = (bf16[2,64,1024]{2,1,0:T(8,128)(2,1)S(1)}, bf16[2,64,1024]{2,1,0:T(8,128)(2,1)S(1)}, u32[]{:S(2)}, u32[]{:S(2)}) collective-permute-start(bf16[2,64,1024]{2,1,0:T(8,128)(2,1)S(1)} %get-tuple-element.47), channel_id=1, source_target_pairs={{0,16},{8,24},{16,0},{24,8},{32,48},{40,56},{48,32},{56,40},{64,80... | collective-permute-start | bytes 786440 | tf_op jit(solution)/shard_map/ppermute | solution.py:254
  46.3 22.8 %collective-permute-start.13 = (bf16[2,64,1024]{2,1,0:T(8,128)(2,1)S(1)}, bf16[2,64,1024]{2,1,0:T(8,128)(2,1)S(1)}, u32[]{:S(2)}, u32[]{:S(2)}) collective-permute-start(bf16[2,64,1024]{2,1,0:T(8,128)(2,1)S(1)} %get-tuple-element.48), channel_id=1, source_target_pairs={{0,48},{8,56},{16,32},{24,40},{32,16},{40,24},{48,0},{56,8},{64,11... | collective-permute-start | bytes 786440 | tf_op jit(solution)/shard_map/ppermute | solution.py:254
  48.5 20.6 %collective-permute-start.14 = (bf16[2,64,1024]{2,1,0:T(8,128)(2,1)S(1)}, bf16[2,64,1024]{2,1,0:T(8,128)(2,1)S(1)}, u32[]{:S(2)}, u32[]{:S(2)}) collective-permute-start(bf16[2,64,1024]{2,1,0:T(8,128)(2,1)S(1)} %get-tuple-element.49), channel_id=1, source_target_pairs={{0,32},{8,40},{16,48},{24,56},{32,0},{40,8},{48,16},{56,24},{64,96... | collective-permute-start | bytes 786440 | tf_op jit(solution)/shard_map/ppermute | solution.py:254
  50.0 3.7 %collective-permute-start.4 = (bf16[128,512]{1,0:T(8,128)(2,1)S(1)}, bf16[128,512]{1,0:T(8,128)(2,1)S(1)}, u32[]{:S(2)}, u32[]{:S(2)}) collective-permute-start(bf16[128,512]{1,0:T(8,128)(2,1)S(1)} %get-tuple-element.38.gm_ref), channel_id=1, source_target_pairs={{0,8},{8,0},{16,24},{24,16},{32,40},{40,32},{48,56},{56,48},{64,72... | collective-permute-start | bytes 393224 | tf_op jit(solution)/shard_map/ppermute | solution.py:254
  50.0 3.7 %collective-permute-start.5 = (bf16[128,512]{1,0:T(8,128)(2,1)S(1)}, bf16[128,512]{1,0:T(8,128)(2,1)S(1)}, u32[]{:S(2)}, u32[]{:S(2)}) collective-permute-start(bf16[128,512]{1,0:T(8,128)(2,1)S(1)} %get-tuple-element.38.gm_ref), channel_id=1, source_target_pairs={{8,16},{24,32},{40,48},{56,64},{72,80},{88,96},{104,112},{16,8},{3... | collective-permute-start | bytes 393224 | tf_op jit(solution)/shard_map/ppermute | solution.py:327
  65.3 9.9 %collective-permute-start.16 = (bf16[8,32,256]{2,1,0:T(8,128)(2,1)S(1)}, bf16[8,32,256]{2,1,0:T(8,128)(2,1)S(1)}, u32[]{:S(2)}, u32[]{:S(2)}) collective-permute-start(bf16[8,32,256]{2,1,0:T(8,128)(2,1)S(1)} %get-tuple-element.53), channel_id=1, source_target_pairs={{0,8},{8,0},{16,24},{24,16},{32,40},{40,32},{48,56},{56,48},{64,72... | collective-permute-start | bytes 393224 | tf_op jit(solution)/shard_map/ppermute | solution.py:254
  69.2 19.8 %collective-permute-start.15 = (bf16[64,1024]{1,0:T(8,128)(2,1)S(1)}, bf16[64,1024]{1,0:T(8,128)(2,1)S(1)}, u32[]{:S(2)}, u32[]{:S(2)}) collective-permute-start(bf16[64,1024]{1,0:T(8,128)(2,1)S(1)} %get-tuple-element.51), channel_id=1, source_target_pairs={{0,64},{8,72},{16,80},{24,88},{32,96},{40,104},{48,112},{56,120},{... | collective-permute-start | bytes 393224 | tf_op jit(solution)/shard_map/ppermute | solution.py:254
  75.2 4.2 %collective-permute-start.17 = (bf16[2,32,256]{2,1,0:T(8,128)(2,1)S(1)}, bf16[2,32,256]{2,1,0:T(8,128)(2,1)S(1)}, u32[]{:S(2)}, u32[]{:S(2)}) collective-permute-start(bf16[2,32,256]{2,1,0:T(8,128)(2,1)S(1)} %get-tuple-element.55), channel_id=1, source_target_pairs={{0,16},{8,24},{16,0},{24,8},{32,48},{40,56},{48,32},{56,40},{64,80... | collective-permute-start | bytes 98312 | tf_op jit(solution)/shard_map/ppermute | solution.py:254
  75.3 5.2 %collective-permute-start.18 = (bf16[2,32,256]{2,1,0:T(8,128)(2,1)S(1)}, bf16[2,32,256]{2,1,0:T(8,128)(2,1)S(1)}, u32[]{:S(2)}, u32[]{:S(2)}) collective-permute-start(bf16[2,32,256]{2,1,0:T(8,128)(2,1)S(1)} %get-tuple-element.56), channel_id=1, source_target_pairs={{0,48},{8,56},{16,32},{24,40},{32,16},{40,24},{48,0},{56,8},{64,11... | collective-permute-start | bytes 98312 | tf_op jit(solution)/shard_map/ppermute | solution.py:254
  76.8 5.4 %collective-permute-start.19 = (bf16[2,32,256]{2,1,0:T(8,128)(2,1)S(1)}, bf16[2,32,256]{2,1,0:T(8,128)(2,1)S(1)}, u32[]{:S(2)}, u32[]{:S(2)}) collective-permute-start(bf16[2,32,256]{2,1,0:T(8,128)(2,1)S(1)} %get-tuple-element.57), channel_id=1, source_target_pairs={{0,32},{8,40},{16,48},{24,56},{32,0},{40,8},{48,16},{56,24},{64,96... | collective-permute-start | bytes 98312 | tf_op jit(solution)/shard_map/ppermute | solution.py:254
  82.3 5.3 %collective-permute-start.20 = (bf16[32,256]{1,0:T(8,128)(2,1)S(1)}, bf16[32,256]{1,0:T(8,128)(2,1)S(1)}, u32[]{:S(2)}, u32[]{:S(2)}) collective-permute-start(bf16[32,256]{1,0:T(8,128)(2,1)S(1)} %get-tuple-element.59), channel_id=1, source_target_pairs={{0,64},{8,72},{16,80},{24,88},{32,96},{40,104},{48,112},{56,120},{... | collective-permute-start | bytes 49160 | tf_op jit(solution)/shard_map/ppermute | solution.py:254
  (3 other events, 137.2 us)

commit v3 on v2

--- a/solution.py
+++ b/solution.py
@@ -79,11 +79,11 @@
     conv_ref[...] = (total * g_ref[...].astype(F32)).astype(BF16)
 
 
-def second_product(pos_ref, b0, b1, b3, b2, og_ref, ogs_ref, *refs):
+def second_product(pos_ref, own, rx, own1, rx3, owns, rxs, og_ref, ogs_ref, *refs):
     outs, g_ref = refs[:4], refs[4]
-    for i, ref in enumerate((b0, b1, b2, b3)):
-        g_ref[i] = ref[0]
-        g_ref[4 + i] = ref[1]
+    pieces = (own, own1, owns.at[1], owns.at[0], rx, rxs.at[0], rxs.at[1], rx3)
+    for i, ref in enumerate(pieces):
+        g_ref[i] = ref[...]
     z = pos_ref[0]
     x = pos_ref[1]
     xh = pos_ref[2]
@@ -213,16 +213,24 @@
     send_ref[...] = t_ref[8:16].astype(BF16)
 
 
-def split_taps(t_ref, got_ref, k, s1, s3, s2):
-    for rel, ref in ((0, k), (1, s1), (3, s3), (2, s2)):
-        both = t_ref[2 * rel : 2 * rel + 2] + got_ref[2 * rel : 2 * rel + 2].astype(F32)
-        ref[...] = both.astype(ref.dtype)
-
-
-def sum_pieces(k, r1, r3, r2, keep, send):
+def split_taps(t_ref, got_ref, k0, k3, send):
+    n = k0.shape[0]
+    for ref, at in ((k0, 0), (send, n), (k3, 3 * n)):
+        m = ref.shape[0]
+        ref[...] = (t_ref[at : at + m] + got_ref[at : at + m].astype(F32)).astype(ref.dtype)
+
+
+def middle_taps(k0, k3, got, keep, send):
+    n = k0.shape[0]
+    keep[...] = k0[...] + got[0:n].astype(F32)
+    send[...] = (k3[...] + got[n:].astype(F32)).astype(BF16)
+
+
+def sum_pieces(k, *refs):
+    parts, keep, send = refs[:-2], refs[-2], refs[-1]
     for ref, i in ((keep, 0), (send, 1)):
         total = k[i].astype(F32)
-        for r in (r1, r3, r2):
+        for r in parts:
             total = total + r[i].astype(F32)
         ref[...] = total.astype(ref.dtype)
 
@@ -292,10 +300,11 @@
     )
     own = jnp.concatenate([mine, swap(other, "seq", 1)], axis=1)
     og_core = swap(out_grad, "seq", 1)
-    pair = jnp.stack([own, swap(own, "chan", 1)])
-    b1 = swap(pair, "chan", 2)
-    b3 = swap(pair, "chan", 6)
-    b2 = swap(pair, "chan", 4)
+    rx = swap(own, "chan", 1)
+    own1 = swap(own, "chan", 2)
+    rx3 = swap(rx, "chan", 6)
+    owns = swap(jnp.stack([own, own1]), "chan", 6)
+    rxs = swap(jnp.stack([rx, rx3]), "chan", 2)
 
     keep, send = call(
         first_product,
@@ -329,7 +338,7 @@
     e = call(
         second_product,
         [shape((2, half, feats), BF16)] * 4,
-        (pos, pair, b1, b3, b2, out_grad, og_core),
+        (pos, own, rx, own1, rx3, owns, rxs, out_grad, og_core),
         scratch=[pltpu.VMEM((8, half, 2 * tok), BF16)],
     )
     e = [e[0], swap(e[1], "seq", 2), swap(e[2], "seq", 6), swap(e[3], "seq", 4)]
@@ -360,11 +369,19 @@
     )
     f_got = swap(tap_send, "seq", 1)
     piece = (2, rows // 4, 256)
-    f = call(
-        split_taps, [shape(piece, F32)] + [shape(piece, BF16)] * 3,
-        (tap_keep, f_got), scalars=0,
-    )
-    f = [f[0], swap(f[1], "seq", 2), swap(f[2], "seq", 6), swap(f[3], "seq", 4)]
+    f0, f3, f_send = call(
+        split_taps,
+        [shape(piece, F32)] * 2 + [shape((4,) + piece[1:], BF16)],
+        (tap_keep, f_got),
+        scalars=0,
+    )
+    f0, f_send = call(
+        middle_taps,
+        [shape(piece, F32), shape(piece, BF16)],
+        (f0, f3, swap(f_send, "seq", 2)),
+        scalars=0,
+    )
+    f = [f0, swap(f_send, "seq", 6)]
     e_keep, e_send = call(
         sum_pieces, [shape((half, feats), F32), shape((half, feats), BF16)], e, scalars=0
     )

time: 89.8 us -> 89.4 us (level)
  starting transfers between devices: 34.6 us -> 33.2 us
    ppermute x20, starting transfers between devices: 33.9 us -> 32.6 us  [swap(): lax.ppermute(v, axis, [(i, i ^ mask) for i in range(lax.axis_size(axis))])]
    pallas_call x12 -> x13, Pallas kernels: 26.8 us -> 26.8 us  [call(): pl.pallas_call(body, out_shape=out_shape, in_specs=[smem()] * scalars + [...]
where the time goes in v3:
time: 89.4 us; the launch traced here: 89.2 us
  starting transfers between devices  33.2 us (37%)
  waiting for transfers between devices  28.1 us (31%)
  Pallas kernels  26.8 us (30%)
    ppermute x20, starting transfers between devices, swap(): lax.ppermute(v, axis, [(i, i ^ mask) for i in range(lax.axis_size(axis))])  32.6 us
    ppermute x20, waiting for transfers between devices, swap(): lax.ppermute(v, axis, [(i, i ^ mask) for i in range(lax.axis_size(axis))])  28.1 us
    pallas_call x13, Pallas kernels, call(): pl.pallas_call(body, out_shape=out_shape, in_specs=[smem()] * scalars + [...  26.8 us
  transfers between devices with their start and end apart: 21, of which 7 were waited for; matrix products, arithmetic and copies ran while one was open for 0% of the time, Pallas kernels for 29%

profile of v3, /device:TPU:0, one launch (start us, length us, event | category | flops | bytes accessed | tf_op | source)
XLA Modules:
  0.0 89.2 jit_solution(9306953422739313837)
XLA Ops:
  0.9 3.9 %shard_map.102 = (bf16[512,512]{1,0:T(8,128)(2,1)S(1)}, bf16[512,512]{1,0:T(8,128)(2,1)S(1)}) custom-call(s32[5]{0:T(128)S(1)} %stack.41.pos_ref, bf16[1024,1024]{1,0:T(8,128)(2,1)} %w_hbm.1, bf16[512,1024]{1,0:T(8,128)(2,1)} %og_ref.1), custom_call_target="tpu_custom_call" | custom-call | tf_op jit(solution)/shard_map/pallas_call | solution.py:273
  4.7 1.7 %collective-permute-start = (bf16[512,512]{1,0:T(8,128)(2,1)S(1)}, bf16[512,512]{1,0:T(8,128)(2,1)S(1)}, u32[]{:S(2)}, u32[]{:S(2)}) collective-permute-start(bf16[512,512]{1,0:T(8,128)(2,1)S(1)} %get-tuple-element.34), channel_id=1, source_target_pairs={{0,1},{1,0},{2,3},{3,2},{4,5},{5,4},{6,7},{7,6},{8,9},{9,8},{10,11... | collective-permute-start | bytes 1572872 | tf_op jit(solution)/shard_map/ppermute | solution.py:262
  6.4 1.6 %shard_map.107 = (bf16[64,512]{1,0:T(8,128)(2,1)S(1)}, bf16[64,512]{1,0:T(8,128)(2,1)S(1)}) custom-call(s32[5]{0:T(128)S(1)} %stack.41.pos_ref, bf16[128,512]{1,0:T(8,128)(2,1)} %v_hbm.1, bf16[128,512]{1,0:T(8,128)(2,1)} %g_hbm.1), custom_call_target="tpu_custom_call" | custom-call | tf_op jit(solution)/shard_map/pallas_call | solution.py:273
  8.3 1.0 %collective-permute-done.6 = bf16[64,512]{1,0:T(8,128)(2,1)S(1)} collective-permute-done((bf16[64,512]{1,0:T(8,128)(2,1)S(1)}, bf16[64,512]{1,0:T(8,128)(2,1)S(1)}, u32[]{:S(2)}, u32[]{:S(2)}) %collective-permute-start.6) | collective-permute-done | bytes 65568 | tf_op jit(solution)/shard_map/ppermute | solution.py:262
  9.8 2.0 %collective-permute-start.8 = (bf16[64,1024]{1,0:T(8,128)(2,1)S(1)}, bf16[64,1024]{1,0:T(8,128)(2,1)S(1)}, u32[]{:S(2)}, u32[]{:S(2)}) collective-permute-start(bf16[64,1024]{1,0:T(8,128)(2,1)S(1)} %constant_dynamic-update-slice_fusion.own), channel_id=1, source_target_pairs={{0,2},{1,3},{2,0},{3,1},{4,6},{5,7},{6,4},{7,5},{8,10},{9,11},{10,... | collective-permute-start | bytes 393224 | tf_op jit(solution)/shard_map/ppermute | solution.py:262
  11.8 10.2 %collective-permute-done.7.rx = bf16[64,1024]{1,0:T(8,128)(2,1)S(1)} collective-permute-done((bf16[64,1024]{1,0:T(8,128)(2,1)S(1)}, bf16[64,1024]{1,0:T(8,128)(2,1)S(1)}, u32[]{:S(2)}, u32[]{:S(2)}) %collective-permute-start.7) | collective-permute-done | bytes 131104 | tf_op jit(solution)/shard_map/ppermute | solution.py:262
  21.9 4.2 %collective-permute-start.9 = (bf16[64,1024]{1,0:T(8,128)(2,1)S(1)}, bf16[64,1024]{1,0:T(8,128)(2,1)S(1)}, u32[]{:S(2)}, u32[]{:S(2)}) collective-permute-start(bf16[64,1024]{1,0:T(8,128)(2,1)S(1)} %collective-permute-done.7.rx), channel_id=1, source_target_pairs={{0,6},{1,7},{2,4},{3,5},{4,2},{5,3},{6,0},{7,1},{8,14},{9,15},{10,... | collective-permute-start | bytes 393224 | tf_op jit(solution)/shard_map/ppermute | solution.py:262
  26.2 3.8 %collective-permute-done.9.rx3 = bf16[64,1024]{1,0:T(8,128)(2,1)S(1)} collective-permute-done((bf16[64,1024]{1,0:T(8,128)(2,1)S(1)}, bf16[64,1024]{1,0:T(8,128)(2,1)S(1)}, u32[]{:S(2)}, u32[]{:S(2)}) %collective-permute-start.9) | collective-permute-done | bytes 131104 | tf_op jit(solution)/shard_map/ppermute | solution.py:262
  30.6 1.7 %collective-permute-start.1 = (bf16[128,512]{1,0:T(8,128)(2,1)S(1)}, bf16[128,512]{1,0:T(8,128)(2,1)S(1)}, u32[]{:S(2)}, u32[]{:S(2)}) collective-permute-start(bf16[128,512]{1,0:T(8,128)(2,1)S(1)} %get-tuple-element.36), channel_id=1, source_target_pairs={{0,2},{1,3},{2,0},{3,1},{4,6},{5,7},{6,4},{7,5},{8,10},{9,11},{10,... | collective-permute-start | bytes 393224 | tf_op jit(solution)/shard_map/ppermute | solution.py:262
  32.3 3.7 %collective-permute-start.2 = (bf16[128,512]{1,0:T(8,128)(2,1)S(1)}, bf16[128,512]{1,0:T(8,128)(2,1)S(1)}, u32[]{:S(2)}, u32[]{:S(2)}) collective-permute-start(bf16[128,512]{1,0:T(8,128)(2,1)S(1)} %get-tuple-element.37), channel_id=1, source_target_pairs={{0,6},{1,7},{2,4},{3,5},{4,2},{5,3},{6,0},{7,1},{8,14},{9,15},{10,... | collective-permute-start | bytes 393224 | tf_op jit(solution)/shard_map/ppermute | solution.py:262
  36.0 1.8 %collective-permute-start.3 = (bf16[128,512]{1,0:T(8,128)(2,1)S(1)}, bf16[128,512]{1,0:T(8,128)(2,1)S(1)}, u32[]{:S(2)}, u32[]{:S(2)}) collective-permute-start(bf16[128,512]{1,0:T(8,128)(2,1)S(1)} %get-tuple-element.38), channel_id=1, source_target_pairs={{0,4},{1,5},{2,6},{3,7},{4,0},{5,1},{6,2},{7,3},{8,12},{9,13},{10,... | collective-permute-start | bytes 393224 | tf_op jit(solution)/shard_map/ppermute | solution.py:262
  38.2 3.6 %shard_map.108 = (bf16[2,64,1024]{2,1,0:T(8,128)(2,1)S(1)}, bf16[2,64,1024]{2,1,0:T(8,128)(2,1)S(1)}, bf16[2,64,1024]{2,1,0:T(8,128)(2,1)S(1)}, bf16[2,64,1024]{2,1,0:T(8,128)(2,1)S(1)}) custom-call(s32[5]{0:T(128)S(1)} %stack.41.pos_ref, bf16[64,1024]{1,0:T(8,128)(2,1)S(1)} %constant_dynamic-update-slice_fusion.own, ...), custom_call_target="tpu_custom_call" | custom-call | tf_op jit(solution)/shard_map/pallas_call | solution.py:273
  41.8 1.6 %collective-permute-start.13 = (bf16[2,64,1024]{2,1,0:T(8,128)(2,1)S(1)}, bf16[2,64,1024]{2,1,0:T(8,128)(2,1)S(1)}, u32[]{:S(2)}, u32[]{:S(2)}) collective-permute-start(bf16[2,64,1024]{2,1,0:T(8,128)(2,1)S(1)} %get-tuple-element.48), channel_id=1, source_target_pairs={{0,16},{8,24},{16,0},{24,8},{32,48},{40,56},{48,32},{56,40},{64,80... | collective-permute-start | bytes 786440 | tf_op jit(solution)/shard_map/ppermute | solution.py:262
  43.4 2.2 %collective-permute-start.14 = (bf16[2,64,1024]{2,1,0:T(8,128)(2,1)S(1)}, bf16[2,64,1024]{2,1,0:T(8,128)(2,1)S(1)}, u32[]{:S(2)}, u32[]{:S(2)}) collective-permute-start(bf16[2,64,1024]{2,1,0:T(8,128)(2,1)S(1)} %get-tuple-element.49), channel_id=1, source_target_pairs={{0,48},{8,56},{16,32},{24,40},{32,16},{40,24},{48,0},{56,8},{64,11... | collective-permute-start | bytes 786440 | tf_op jit(solution)/shard_map/ppermute | solution.py:262
  46.4 0.8 shard_map.104
  47.8 3.0 %shard_map.105 = (bf16[16,2,128,256]{3,2,1,0:T(8,128)(2,1)S(1)}, bf16[16,256,512]{2,1,0:T(8,128)(2,1)S(1)}, bf16[16,256,512]{2,1,0:T(8,128)(2,1)S(1)}) custom-call(s32[5]{0:T(128)S(1)} %stack.41.pos_ref, s32[16]{0:T(128)S(1)} %copy-done.5, bf16[2,128,512]{2,1,0:T(8,128)(2,1)S(1)} %copy-done.3, bf16[128,512]{1,0:T(8,128)(2,1)S(1)} %copy-done.4), custom_call_target="tpu_custom_call" | custom-call | tf_op jit(solution)/shard_map/pallas_call | solution.py:273
  50.9 11.6 %shard_map.106 = (f32[128,512]{1,0:T(8,128)}, f32[8,32,256]{2,1,0:T(8,128)S(1)}, bf16[8,32,256]{2,1,0:T(8,128)(2,1)S(1)}) custom-call(s32[5]{0:T(128)S(1)} %stack.41.pos_ref, bf16[128,512]{1,0:T(8,128)(2,1)S(1)} %get-tuple-element.39.gm_ref, bf16[128,512]{1,0:T(8,128)(2,1)S(1)} %collective-permute-done.4.gs_ref, ...), custom_call_target="tpu_custom_call" | custom-call | tf_op jit(solution)/shard_map/pallas_call | solution.py:273
  62.4 3.6 %collective-permute-start.17 = (bf16[8,32,256]{2,1,0:T(8,128)(2,1)S(1)}, bf16[8,32,256]{2,1,0:T(8,128)(2,1)S(1)}, u32[]{:S(2)}, u32[]{:S(2)}) collective-permute-start(bf16[8,32,256]{2,1,0:T(8,128)(2,1)S(1)} %get-tuple-element.54), channel_id=1, source_target_pairs={{0,8},{8,0},{16,24},{24,16},{32,40},{40,32},{48,56},{56,48},{64,72... | collective-permute-start | bytes 393224 | tf_op jit(solution)/shard_map/ppermute | solution.py:262
  66.2 5.9 %collective-permute-start.16 = (bf16[64,1024]{1,0:T(8,128)(2,1)S(1)}, bf16[64,1024]{1,0:T(8,128)(2,1)S(1)}, u32[]{:S(2)}, u32[]{:S(2)}) collective-permute-start(bf16[64,1024]{1,0:T(8,128)(2,1)S(1)} %get-tuple-element.52), channel_id=1, source_target_pairs={{0,64},{8,72},{16,80},{24,88},{32,96},{40,104},{48,112},{56,120},{... | collective-permute-start | bytes 393224 | tf_op jit(solution)/shard_map/ppermute | solution.py:262
  72.3 4.3 %collective-permute-done.18.got = bf16[4,32,256]{2,1,0:T(8,128)(2,1)S(1)} collective-permute-done((bf16[4,32,256]{2,1,0:T(8,128)(2,1)S(1)}, bf16[4,32,256]{2,1,0:T(8,128)(2,1)S(1)}, u32[]{:S(2)}, u32[]{:S(2)}) %collective-permute-start.18) | collective-permute-done | bytes 65568 | tf_op jit(solution)/shard_map/ppermute | solution.py:262
  77.3 4.4 %collective-permute-done.19.refs_0_ = bf16[2,32,256]{2,1,0:T(8,128)(2,1)S(1)} collective-permute-done((bf16[2,32,256]{2,1,0:T(8,128)(2,1)S(1)}, bf16[2,32,256]{2,1,0:T(8,128)(2,1)S(1)}, u32[]{:S(2)}, u32[]{:S(2)}) %collective-permute-start.19) | collective-permute-done | bytes 32800 | tf_op jit(solution)/shard_map/ppermute | solution.py:262
  81.7 1.2 %collective-permute-start.20 = (bf16[32,256]{1,0:T(8,128)(2,1)S(1)}, bf16[32,256]{1,0:T(8,128)(2,1)S(1)}, u32[]{:S(2)}, u32[]{:S(2)}) collective-permute-start(bf16[32,256]{1,0:T(8,128)(2,1)S(1)} %get-tuple-element.61), channel_id=1, source_target_pairs={{0,64},{8,72},{16,80},{24,88},{32,96},{40,104},{48,112},{56,120},{... | collective-permute-start | bytes 49160 | tf_op jit(solution)/shard_map/ppermute | solution.py:262
  82.9 4.1 %collective-permute-done.20.got = bf16[32,256]{1,0:T(8,128)(2,1)S(1)} collective-permute-done((bf16[32,256]{1,0:T(8,128)(2,1)S(1)}, bf16[32,256]{1,0:T(8,128)(2,1)S(1)}, u32[]{:S(2)}, u32[]{:S(2)}) %collective-permute-start.20) | collective-permute-done | bytes 16416 | tf_op jit(solution)/shard_map/ppermute | solution.py:262
  87.1 1.4 %shard_map.114 = f32[2,32,128]{2,1,0:T(8,128)} custom-call(s32[5]{0:T(128)S(1)} %stack.41.pos_ref, s32[16]{0:T(128)S(1)} %copy-done.5, f32[32,256]{1,0:T(8,128)S(1)} %get-tuple-element.60.part_ref, bf16[32,256]{1,0:T(8,128)(2,1)S(1)} %collective-permute-done.20.got), custom_call_target="tpu_custom_call" | custom-call | tf_op jit(solution)/shard_map/pallas_call | solution.py:273
  (48 shorter events, 5.1 us)
Async XLA Ops:
  0.6 37.5 %collective-permute-start.12 = (bf16[512,1024]{1,0:T(8,128)(2,1)}, bf16[512,1024]{1,0:T(8,128)(2,1)S(1)}, u32[]{:S(2)}, u32[]{:S(2)}) collective-permute-start(bf16[512,1024]{1,0:T(8,128)(2,1)} %og_ref.1), channel_id=1, source_target_pairs={{0,8},{8,0},{16,24},{24,16},{32,40},{40,32},{48,56},{56,48},{64,72... | collective-permute-start | bytes 3145736 | tf_op jit(solution)/shard_map/ppermute | solution.py:262
  0.8 47.0 %copy-start.3 = (bf16[2,128,512]{2,1,0:T(8,128)(2,1)S(1)}, bf16[2,128,512]{2,1,0:T(8,128)(2,1)}, u32[]{:S(2)}) copy-start(bf16[2,128,512]{2,1,0:T(8,128)(2,1)} %f_ref.1) | copy-start | bytes 786436
  0.8 47.0 %copy-start.4 = (bf16[128,512]{1,0:T(8,128)(2,1)S(1)}, bf16[128,512]{1,0:T(8,128)(2,1)}, u32[]{:S(2)}) copy-start(bf16[128,512]{1,0:T(8,128)(2,1)} %x_ref.1) | copy-start | bytes 393220
  0.8 47.0 %copy-start.5 = (s32[16]{0:T(128)S(1)}, s32[16]{0:T(128)}, u32[]{:S(2)}) copy-start(s32[16]{0:T(128)} %reach_ref.3) | copy-start | bytes 196
  4.7 25.7 %collective-permute-start = (bf16[512,512]{1,0:T(8,128)(2,1)S(1)}, bf16[512,512]{1,0:T(8,128)(2,1)S(1)}, u32[]{:S(2)}, u32[]{:S(2)}) collective-permute-start(bf16[512,512]{1,0:T(8,128)(2,1)S(1)} %get-tuple-element.34), channel_id=1, source_target_pairs={{0,1},{1,0},{2,3},{3,2},{4,5},{5,4},{6,7},{7,6},{8,9},{9,8},{10,11... | collective-permute-start | bytes 1572872 | tf_op jit(solution)/shard_map/ppermute | solution.py:262
  8.0 1.3 %collective-permute-start.6 = (bf16[64,512]{1,0:T(8,128)(2,1)S(1)}, bf16[64,512]{1,0:T(8,128)(2,1)S(1)}, u32[]{:S(2)}, u32[]{:S(2)}) collective-permute-start(bf16[64,512]{1,0:T(8,128)(2,1)S(1)} %get-tuple-element.46), channel_id=1, source_target_pairs={{0,8},{8,0},{16,24},{24,16},{32,40},{40,32},{48,56},{56,48},{64,72... | collective-permute-start | bytes 196616 | tf_op jit(solution)/shard_map/ppermute | solution.py:262
  9.3 12.6 %collective-permute-start.7 = (bf16[64,1024]{1,0:T(8,128)(2,1)S(1)}, bf16[64,1024]{1,0:T(8,128)(2,1)S(1)}, u32[]{:S(2)}, u32[]{:S(2)}) collective-permute-start(bf16[64,1024]{1,0:T(8,128)(2,1)S(1)} %constant_dynamic-update-slice_fusion.own), channel_id=1, source_target_pairs={{0,1},{1,0},{2,3},{3,2},{4,5},{5,4},{6,7},{7,6},{8,9},{9,8},{10,11... | collective-permute-start | bytes 393224 | tf_op jit(solution)/shard_map/ppermute | solution.py:262
  9.8 16.3 %collective-permute-start.8 = (bf16[64,1024]{1,0:T(8,128)(2,1)S(1)}, bf16[64,1024]{1,0:T(8,128)(2,1)S(1)}, u32[]{:S(2)}, u32[]{:S(2)}) collective-permute-start(bf16[64,1024]{1,0:T(8,128)(2,1)S(1)} %constant_dynamic-update-slice_fusion.own), channel_id=1, source_target_pairs={{0,2},{1,3},{2,0},{3,1},{4,6},{5,7},{6,4},{7,5},{8,10},{9,11},{10,... | collective-permute-start | bytes 393224 | tf_op jit(solution)/shard_map/ppermute | solution.py:262
  21.9 8.0 %collective-permute-start.9 = (bf16[64,1024]{1,0:T(8,128)(2,1)S(1)}, bf16[64,1024]{1,0:T(8,128)(2,1)S(1)}, u32[]{:S(2)}, u32[]{:S(2)}) collective-permute-start(bf16[64,1024]{1,0:T(8,128)(2,1)S(1)} %collective-permute-done.7.rx), channel_id=1, source_target_pairs={{0,6},{1,7},{2,4},{3,5},{4,2},{5,3},{6,0},{7,1},{8,14},{9,15},{10,... | collective-permute-start | bytes 393224 | tf_op jit(solution)/shard_map/ppermute | solution.py:262
  26.1 9.9 %collective-permute-start.10 = (bf16[2,64,1024]{2,1,0:T(8,128)(2,1)S(1)}, bf16[2,64,1024]{2,1,0:T(8,128)(2,1)S(1)}, u32[]{:S(2)}, u32[]{:S(2)}) collective-permute-start(bf16[2,64,1024]{2,1,0:T(8,128)(2,1)S(1)} %pad_maximum_fusion), channel_id=1, source_target_pairs={{0,6},{1,7},{2,4},{3,5},{4,2},{5,3},{6,0},{7,1},{8,14},{9,15},{10,... | collective-permute-start | bytes 786440 | tf_op jit(solution)/shard_map/ppermute | solution.py:262
  30.0 8.2 %collective-permute-start.11 = (bf16[2,64,1024]{2,1,0:T(8,128)(2,1)S(1)}, bf16[2,64,1024]{2,1,0:T(8,128)(2,1)S(1)}, u32[]{:S(2)}, u32[]{:S(2)}) collective-permute-start(bf16[2,64,1024]{2,1,0:T(8,128)(2,1)S(1)} %pad_maximum_fusion.1), channel_id=1, source_target_pairs={{0,2},{1,3},{2,0},{3,1},{4,6},{5,7},{6,4},{7,5},{8,10},{9,11},{10,... | collective-permute-start | bytes 786440 | tf_op jit(solution)/shard_map/ppermute | solution.py:262
  30.6 15.1 %collective-permute-start.1 = (bf16[128,512]{1,0:T(8,128)(2,1)S(1)}, bf16[128,512]{1,0:T(8,128)(2,1)S(1)}, u32[]{:S(2)}, u32[]{:S(2)}) collective-permute-start(bf16[128,512]{1,0:T(8,128)(2,1)S(1)} %get-tuple-element.36), channel_id=1, source_target_pairs={{0,2},{1,3},{2,0},{3,1},{4,6},{5,7},{6,4},{7,5},{8,10},{9,11},{10,... | collective-permute-start | bytes 393224 | tf_op jit(solution)/shard_map/ppermute | solution.py:262
  32.3 14.0 %collective-permute-start.2 = (bf16[128,512]{1,0:T(8,128)(2,1)S(1)}, bf16[128,512]{1,0:T(8,128)(2,1)S(1)}, u32[]{:S(2)}, u32[]{:S(2)}) collective-permute-start(bf16[128,512]{1,0:T(8,128)(2,1)S(1)} %get-tuple-element.37), channel_id=1, source_target_pairs={{0,6},{1,7},{2,4},{3,5},{4,2},{5,3},{6,0},{7,1},{8,14},{9,15},{10,... | collective-permute-start | bytes 393224 | tf_op jit(solution)/shard_map/ppermute | solution.py:262
  36.0 10.3 %collective-permute-start.3 = (bf16[128,512]{1,0:T(8,128)(2,1)S(1)}, bf16[128,512]{1,0:T(8,128)(2,1)S(1)}, u32[]{:S(2)}, u32[]{:S(2)}) collective-permute-start(bf16[128,512]{1,0:T(8,128)(2,1)S(1)} %get-tuple-element.38), channel_id=1, source_target_pairs={{0,4},{1,5},{2,6},{3,7},{4,0},{5,1},{6,2},{7,3},{8,12},{9,13},{10,... | collective-permute-start | bytes 393224 | tf_op jit(solution)/shard_map/ppermute | solution.py:262
  41.8 24.3 %collective-permute-start.13 = (bf16[2,64,1024]{2,1,0:T(8,128)(2,1)S(1)}, bf16[2,64,1024]{2,1,0:T(8,128)(2,1)S(1)}, u32[]{:S(2)}, u32[]{:S(2)}) collective-permute-start(bf16[2,64,1024]{2,1,0:T(8,128)(2,1)S(1)} %get-tuple-element.48), channel_id=1, source_target_pairs={{0,16},{8,24},{16,0},{24,8},{32,48},{40,56},{48,32},{56,40},{64,80... | collective-permute-start | bytes 786440 | tf_op jit(solution)/shard_map/ppermute | solution.py:262
  43.4 22.6 %collective-permute-start.14 = (bf16[2,64,1024]{2,1,0:T(8,128)(2,1)S(1)}, bf16[2,64,1024]{2,1,0:T(8,128)(2,1)S(1)}, u32[]{:S(2)}, u32[]{:S(2)}) collective-permute-start(bf16[2,64,1024]{2,1,0:T(8,128)(2,1)S(1)} %get-tuple-element.49), channel_id=1, source_target_pairs={{0,48},{8,56},{16,32},{24,40},{32,16},{40,24},{48,0},{56,8},{64,11... | collective-permute-start | bytes 786440 | tf_op jit(solution)/shard_map/ppermute | solution.py:262
  45.6 20.4 %collective-permute-start.15 = (bf16[2,64,1024]{2,1,0:T(8,128)(2,1)S(1)}, bf16[2,64,1024]{2,1,0:T(8,128)(2,1)S(1)}, u32[]{:S(2)}, u32[]{:S(2)}) collective-permute-start(bf16[2,64,1024]{2,1,0:T(8,128)(2,1)S(1)} %get-tuple-element.50), channel_id=1, source_target_pairs={{0,32},{8,40},{16,48},{24,56},{32,0},{40,8},{48,16},{56,24},{64,96... | collective-permute-start | bytes 786440 | tf_op jit(solution)/shard_map/ppermute | solution.py:262
  47.1 3.7 %collective-permute-start.4 = (bf16[128,512]{1,0:T(8,128)(2,1)S(1)}, bf16[128,512]{1,0:T(8,128)(2,1)S(1)}, u32[]{:S(2)}, u32[]{:S(2)}) collective-permute-start(bf16[128,512]{1,0:T(8,128)(2,1)S(1)} %get-tuple-element.39.gm_ref), channel_id=1, source_target_pairs={{0,8},{8,0},{16,24},{24,16},{32,40},{40,32},{48,56},{56,48},{64,72... | collective-permute-start | bytes 393224 | tf_op jit(solution)/shard_map/ppermute | solution.py:262
  47.1 3.7 %collective-permute-start.5 = (bf16[128,512]{1,0:T(8,128)(2,1)S(1)}, bf16[128,512]{1,0:T(8,128)(2,1)S(1)}, u32[]{:S(2)}, u32[]{:S(2)}) collective-permute-start(bf16[128,512]{1,0:T(8,128)(2,1)S(1)} %get-tuple-element.39.gm_ref), channel_id=1, source_target_pairs={{8,16},{24,32},{40,48},{56,64},{72,80},{88,96},{104,112},{16,8},{3... | collective-permute-start | bytes 393224 | tf_op jit(solution)/shard_map/ppermute | solution.py:336
  62.4 9.7 %collective-permute-start.17 = (bf16[8,32,256]{2,1,0:T(8,128)(2,1)S(1)}, bf16[8,32,256]{2,1,0:T(8,128)(2,1)S(1)}, u32[]{:S(2)}, u32[]{:S(2)}) collective-permute-start(bf16[8,32,256]{2,1,0:T(8,128)(2,1)S(1)} %get-tuple-element.54), channel_id=1, source_target_pairs={{0,8},{8,0},{16,24},{24,16},{32,40},{40,32},{48,56},{56,48},{64,72... | collective-permute-start | bytes 393224 | tf_op jit(solution)/shard_map/ppermute | solution.py:262
  66.2 22.3 %collective-permute-start.16 = (bf16[64,1024]{1,0:T(8,128)(2,1)S(1)}, bf16[64,1024]{1,0:T(8,128)(2,1)S(1)}, u32[]{:S(2)}, u32[]{:S(2)}) collective-permute-start(bf16[64,1024]{1,0:T(8,128)(2,1)S(1)} %get-tuple-element.52), channel_id=1, source_target_pairs={{0,64},{8,72},{16,80},{24,88},{32,96},{40,104},{48,112},{56,120},{... | collective-permute-start | bytes 393224 | tf_op jit(solution)/shard_map/ppermute | solution.py:262
  72.2 4.3 %collective-permute-start.18 = (bf16[4,32,256]{2,1,0:T(8,128)(2,1)S(1)}, bf16[4,32,256]{2,1,0:T(8,128)(2,1)S(1)}, u32[]{:S(2)}, u32[]{:S(2)}) collective-permute-start(bf16[4,32,256]{2,1,0:T(8,128)(2,1)S(1)} %get-tuple-element.57), channel_id=1, source_target_pairs={{0,16},{8,24},{16,0},{24,8},{32,48},{40,56},{48,32},{56,40},{64,80... | collective-permute-start | bytes 196616 | tf_op jit(solution)/shard_map/ppermute | solution.py:262
  76.5 5.2 %collective-permute-start.19 = (bf16[2,32,256]{2,1,0:T(8,128)(2,1)S(1)}, bf16[2,32,256]{2,1,0:T(8,128)(2,1)S(1)}, u32[]{:S(2)}, u32[]{:S(2)}) collective-permute-start(bf16[2,32,256]{2,1,0:T(8,128)(2,1)S(1)} %get-tuple-element.59), channel_id=1, source_target_pairs={{0,48},{8,56},{16,32},{24,40},{32,16},{40,24},{48,0},{56,8},{64,11... | collective-permute-start | bytes 98312 | tf_op jit(solution)/shard_map/ppermute | solution.py:262
  81.7 5.3 %collective-permute-start.20 = (bf16[32,256]{1,0:T(8,128)(2,1)S(1)}, bf16[32,256]{1,0:T(8,128)(2,1)S(1)}, u32[]{:S(2)}, u32[]{:S(2)}) collective-permute-start(bf16[32,256]{1,0:T(8,128)(2,1)S(1)} %get-tuple-element.61), channel_id=1, source_target_pairs={{0,64},{8,72},{16,80},{24,88},{32,96},{40,104},{48,112},{56,120},{... | collective-permute-start | bytes 49160 | tf_op jit(solution)/shard_map/ppermute | solution.py:262
  (3 other events, 128.6 us)

commit v4 on v2

--- a/solution.py
+++ b/solution.py
@@ -144,29 +144,59 @@
     lax.fori_loop(0, rows // 16, step, 0)
 
 
-def conv_grads(pos_ref, gm_ref, gs_ref, gp_ref, l_ref, ui_ref, uo_ref,
-               o_ref, keep_ref, send_ref, h_ref, t_ref):
+def with_halos(pos_ref, gm_ref, gs_ref, gp_ref, band):
+    core0 = (pos_ref[4] & 1) == 0
+    gm = gm_ref[band, :].astype(F32)
+    gs = gs_ref[band, :].astype(F32)
+    gp = gp_ref[band, :].astype(F32)
+    return jnp.concatenate([jnp.where(core0, gp, gs), gm, jnp.where(core0, gs, gp)], axis=1)
+
+
+def fill_shifted(h_ref, h, ext):
+    width = ext.shape[1]
+    two = jnp.concatenate([ext, pltpu.roll(ext, width - 1, 1)], axis=0).astype(BF16)
+    for k in range(VN // 2):
+        moved = two if k == 0 else pltpu.roll(two, width - 2 * k, 1)
+        h_ref[h, 16 * k : 16 * k + 16, :] = moved
+
+
+def tap_grads(pos_ref, gm_ref, gs_ref, gp_ref, ui_ref, uo_ref, t_ref, h_ref, acc_ref):
     rows, n = gm_ref.shape
-    width = 3 * n
-    lanes = n // 128
-    place = pos_ref[4]
-    core0 = (place & 1) == 0
     own_cols = iota((16, 8, 256), 1) == (iota((16, 8, 256), 2) & 7)
 
     def step(i, carry):
         band = pl.ds(pl.multiple_of(i * 16, 16), 16)
-        gm = gm_ref[band, :].astype(F32)
-        gs = gs_ref[band, :].astype(F32)
-        gp = gp_ref[band, :].astype(F32)
-        ext16 = jnp.concatenate([jnp.where(core0, gp, gs), gm, jnp.where(core0, gs, gp)], axis=1)
+        ext16 = with_halos(pos_ref, gm_ref, gs_ref, gp_ref, band)
+        for h in range(2):
+            group = 2 * i + h
+            fill_shifted(h_ref, h, ext16[8 * h : 8 * h + 8])
+            inner = dot(ui_ref[group], h_ref[h, :, n : 2 * n], NT)
+            for d in range(2):
+                start = 2 * n * (1 - d)
+                cross = inner[128 * d : 128 * d + 128] + dot(
+                    uo_ref[group, 128 * d : 128 * d + 128, :], h_ref[h, :, start : start + n], NT
+                )
+                sums = jnp.sum(jnp.where(own_cols, cross.reshape(16, 8, 256), 0.0), axis=1)
+                row = d * (rows // 8) + group
+                for u in range(16):
+                    acc_ref[u, pl.ds(row, 1), :] = sums[u : u + 1]
+        return carry
+
+    lax.fori_loop(0, rows // 16, step, 0)
+    t_ref[...] = acc_ref[...].astype(BF16)
+
+
+def input_grad(pos_ref, gm_ref, gs_ref, gp_ref, l_ref, o_ref, h_ref):
+    rows, n = gm_ref.shape
+    lanes = n // 128
+
+    def step(i, carry):
+        band = pl.ds(pl.multiple_of(i * 16, 16), 16)
+        ext16 = with_halos(pos_ref, gm_ref, gs_ref, gp_ref, band)
         outs = []
         for h in range(2):
             group = 2 * i + h
-            ext = ext16[8 * h : 8 * h + 8]
-            two = jnp.concatenate([ext, pltpu.roll(ext, width - 1, 1)], axis=0).astype(BF16)
-            for k in range(VN // 2):
-                moved = two if k == 0 else pltpu.roll(two, width - 2 * k, 1)
-                h_ref[h, 16 * k : 16 * k + 16, :] = moved
+            fill_shifted(h_ref, h, ext16[8 * h : 8 * h + 8])
             total = None
             for d in range(2):
                 acc = [[None] * (lanes + (b > 0)) for b in range(4)]
@@ -193,30 +223,10 @@
                         line = pltpu.roll(line, 32 * b, 1)[:, 128:]
                     total = line if total is None else total + line
             outs.append(total)
-            inner = dot(ui_ref[group], h_ref[h, :, n : 2 * n], NT)
-            for d in range(2):
-                start = 2 * n * (1 - d)
-                cross = inner[128 * d : 128 * d + 128] + dot(
-                    uo_ref[group, 128 * d : 128 * d + 128, :], h_ref[h, :, start : start + n], NT
-                )
-                sums = jnp.sum(jnp.where(own_cols, cross.reshape(16, 8, 256), 0.0), axis=1)
-                row = d * (rows // 8) + group
-                for u in range(16):
-                    r = u ^ place
-                    slot = (r & 1) * 8 + ((r >> 1) & 3) * 2 + (r >> 3)
-                    t_ref[slot, pl.ds(row, 1), :] = sums[u : u + 1]
         o_ref[band, :] = jnp.concatenate(outs, axis=0)
         return carry
 
     lax.fori_loop(0, rows // 16, step, 0)
-    keep_ref[...] = t_ref[0:8]
-    send_ref[...] = t_ref[8:16].astype(BF16)
-
-
-def split_taps(t_ref, got_ref, k, s1, s3, s2):
-    for rel, ref in ((0, k), (1, s1), (3, s3), (2, s2)):
-        both = t_ref[2 * rel : 2 * rel + 2] + got_ref[2 * rel : 2 * rel + 2].astype(F32)
-        ref[...] = both.astype(ref.dtype)
 
 
 def sum_pieces(k, r1, r3, r2, keep, send):
@@ -231,8 +241,10 @@
     o_ref[...] = (keep[...] + got[...].astype(F32)) * scale
 
 
-def finish_taps(pos_ref, reach_ref, part_ref, got, t_ref, *, scale):
-    f = part_ref[...] + got[...].astype(F32)
+def finish_taps(pos_ref, reach_ref, got, t_ref, *, scale):
+    f = got[0].astype(F32)
+    for i in range(1, got.shape[0]):
+        f = f + got[i].astype(F32)
     chan = pos_ref[0] * 2 + pos_ref[1]
     place = pos_ref[4]
     own_cols = iota((16, 8, 256), 1) == (iota((16, 8, 256), 2) & 7)
@@ -345,32 +357,20 @@
         (pos, filter_reach, filters, conv_input),
         scalars=2,
     )
-    grad_input, tap_keep, tap_send = call(
-        conv_grads,
-        [
-            shape((rows, tok), F32),
-            shape((8, rows // 4, 256), F32),
-            shape((8, rows // 4, 256), BF16),
-        ],
-        (pos, grad_conv, halo_core, halo_out, *prepared),
-        scratch=[
-            pltpu.VMEM((2, 256, 3 * tok), BF16),
-            pltpu.VMEM((16, rows // 4, 256), F32),
-        ],
-    )
-    f_got = swap(tap_send, "seq", 1)
-    piece = (2, rows // 4, 256)
-    f = call(
-        split_taps, [shape(piece, F32)] + [shape(piece, BF16)] * 3,
-        (tap_keep, f_got), scalars=0,
-    )
-    f = [f[0], swap(f[1], "seq", 2), swap(f[2], "seq", 6), swap(f[3], "seq", 4)]
+    halos = (pos, grad_conv, halo_core, halo_out)
+    shifted = pltpu.VMEM((2, 256, 3 * tok), BF16)
+    tap_sums = call(
+        tap_grads,
+        shape((seq_count, rows // 4, 256), BF16),
+        (*halos, *prepared[1:]),
+        scratch=[shifted, pltpu.VMEM((seq_count, rows // 4, 256), F32)],
+    )
+    tap_sums = lax.all_to_all(tap_sums, "seq", 0, 0)
+    grad_input = call(input_grad, shape((rows, tok), F32), (*halos, prepared[0]), scratch=[shifted])
     e_keep, e_send = call(
         sum_pieces, [shape((half, feats), F32), shape((half, feats), BF16)], e, scalars=0
     )
     e_got = swap(e_send, "seq", 8)
-    f_keep, f_send = call(sum_pieces, [shape(piece[1:], F32), shape(piece[1:], BF16)], f, scalars=0)
-    f_got = swap(f_send, "seq", 8)
     grad_weight = call(
         functools.partial(finish_rows, scale=scale),
         shape((half, feats), F32),
@@ -380,7 +380,7 @@
     grad_filters = call(
         functools.partial(finish_taps, scale=scale),
         shape((2, VN, rows), F32),
-        (pos, filter_reach, f_keep, f_got),
+        (pos, filter_reach, tap_sums),
         scalars=2,
     )
     return (grad_input, grad_gate, grad_weight, jnp.transpose(grad_filters, (0, 2, 1)))

time: 89.8 us -> 93.2 us (1.038)
  Pallas kernels: 26.8 us -> 34.8 us
  waiting for transfers between devices: 27.3 us -> 21 us
  local copies, waits for them, and re-layouts: 0.12 us -> 1.77 us
    ppermute x20 -> x15, starting transfers between devices: 33.9 us -> 21.6 us  [swap(): lax.ppermute(v, axis, [(i, i ^ mask) for i in range(lax.axis_size(axis))])]
    all_to_all x0 -> x1, starting transfers between devices: none -> 11.6 us  [on_device_0(): tap_sums = lax.all_to_all(tap_sums, 'seq', 0, 0)]
    pallas_call x12 -> x11, Pallas kernels: 26.8 us -> 34.8 us  [call(): pl.pallas_call(body, out_shape=out_shape, in_specs=[smem()] * scalars + [...]
    ppermute x20 -> x15, waiting for transfers between devices: 27.3 us -> 21 us  [swap(): lax.ppermute(v, axis, [(i, i ^ mask) for i in range(lax.axis_size(axis))])]
    unnamed x13 -> x17, local copies, waits for them, and re-layouts: 0.03 us -> 1.68 us
  transfers between devices with their start and end apart: 21 -> 17, of which waited for: 7 -> 4; matrix products, arithmetic and copies ran while one was open for 0% -> 0% of each run, Pallas kernels for 29% -> 37%
where the time goes in v4:
time: 93.2 us; the launch traced here: 92.2 us
  Pallas kernels  34.8 us (37%)
  starting transfers between devices  33.8 us (36%)
  waiting for transfers between devices  21 us (23%)
  local copies, waits for them, and re-layouts  1.77 us (2%)
    pallas_call x11, Pallas kernels, call(): pl.pallas_call(body, out_shape=out_shape, in_specs=[smem()] * scalars + [...  34.8 us
    ppermute x15, starting transfers between devices, swap(): lax.ppermute(v, axis, [(i, i ^ mask) for i in range(lax.axis_size(axis))])  21.6 us
    ppermute x15, waiting for transfers between devices, swap(): lax.ppermute(v, axis, [(i, i ^ mask) for i in range(lax.axis_size(axis))])  21 us
    all_to_all x1, starting transfers between devices, on_device_0(): tap_sums = lax.all_to_all(tap_sums, 'seq', 0, 0)  11.6 us
  transfers between devices with their start and end apart: 17, of which 4 were waited for; matrix products, arithmetic and copies ran while one was open for 0% of the time, Pallas kernels for 37%

profile of v4, /device:TPU:0, one launch (start us, length us, event | category | flops | bytes accessed | tf_op | source)
XLA Modules:
  0.0 92.2 jit_solution(13076247101488900960)
XLA Ops:
  0.9 3.9 %shard_map.102 = (bf16[512,512]{1,0:T(8,128)(2,1)S(1)}, bf16[512,512]{1,0:T(8,128)(2,1)S(1)}) custom-call(s32[5]{0:T(128)S(1)} %stack.32.pos_ref, bf16[1024,1024]{1,0:T(8,128)(2,1)} %w_hbm.1, bf16[512,1024]{1,0:T(8,128)(2,1)} %og_ref.1), custom_call_target="tpu_custom_call" | custom-call | tf_op jit(solution)/shard_map/pallas_call | solution.py:277
  4.7 1.7 %collective-permute-start = (bf16[512,512]{1,0:T(8,128)(2,1)S(1)}, bf16[512,512]{1,0:T(8,128)(2,1)S(1)}, u32[]{:S(2)}, u32[]{:S(2)}) collective-permute-start(bf16[512,512]{1,0:T(8,128)(2,1)S(1)} %get-tuple-element.24), channel_id=1, source_target_pairs={{0,1},{1,0},{2,3},{3,2},{4,5},{5,4},{6,7},{7,6},{8,9},{9,8},{10,11... | collective-permute-start | bytes 1572872 | tf_op jit(solution)/shard_map/ppermute | solution.py:266
  6.4 1.6 %shard_map.107 = (bf16[64,512]{1,0:T(8,128)(2,1)S(1)}, bf16[64,512]{1,0:T(8,128)(2,1)S(1)}) custom-call(s32[5]{0:T(128)S(1)} %stack.32.pos_ref, bf16[128,512]{1,0:T(8,128)(2,1)} %v_hbm.1, bf16[128,512]{1,0:T(8,128)(2,1)} %g_hbm.1), custom_call_target="tpu_custom_call" | custom-call | tf_op jit(solution)/shard_map/pallas_call | solution.py:277
  8.3 1.0 %collective-permute-done.6 = bf16[64,512]{1,0:T(8,128)(2,1)S(1)} collective-permute-done((bf16[64,512]{1,0:T(8,128)(2,1)S(1)}, bf16[64,512]{1,0:T(8,128)(2,1)S(1)}, u32[]{:S(2)}, u32[]{:S(2)}) %collective-permute-start.6) | collective-permute-done | bytes 65568 | tf_op jit(solution)/shard_map/ppermute | solution.py:266
  9.8 12.2 %collective-permute-done.7 = bf16[64,1024]{1,0:T(8,128)(2,1)S(1)} collective-permute-done((bf16[64,1024]{1,0:T(8,128)(2,1)S(1)}, bf16[64,1024]{1,0:T(8,128)(2,1)S(1)}, u32[]{:S(2)}, u32[]{:S(2)}) %collective-permute-start.7) | collective-permute-done | bytes 131104 | tf_op jit(solution)/shard_map/ppermute | solution.py:266
  22.0 4.1 %collective-permute-start.10 = (bf16[2,64,1024]{2,1,0:T(8,128)(2,1)S(1)}, bf16[2,64,1024]{2,1,0:T(8,128)(2,1)S(1)}, u32[]{:S(2)}, u32[]{:S(2)}) collective-permute-start(bf16[2,64,1024]{2,1,0:T(8,128)(2,1)S(1)} %pad_maximum_fusion.b0), channel_id=1, source_target_pairs={{0,4},{1,5},{2,6},{3,7},{4,0},{5,1},{6,2},{7,3},{8,12},{9,13},{10,... | collective-permute-start | bytes 786440 | tf_op jit(solution)/shard_map/ppermute | solution.py:266
  26.0 1.0 %collective-permute-start.8 = (bf16[2,64,1024]{2,1,0:T(8,128)(2,1)S(1)}, bf16[2,64,1024]{2,1,0:T(8,128)(2,1)S(1)}, u32[]{:S(2)}, u32[]{:S(2)}) collective-permute-start(bf16[2,64,1024]{2,1,0:T(8,128)(2,1)S(1)} %pad_maximum_fusion.b0), channel_id=1, source_target_pairs={{0,2},{1,3},{2,0},{3,1},{4,6},{5,7},{6,4},{7,5},{8,10},{9,11},{10,... | collective-permute-start | bytes 786440 | tf_op jit(solution)/shard_map/ppermute | solution.py:266
  27.2 1.2 %collective-permute-start.1 = (bf16[128,512]{1,0:T(8,128)(2,1)S(1)}, bf16[128,512]{1,0:T(8,128)(2,1)S(1)}, u32[]{:S(2)}, u32[]{:S(2)}) collective-permute-start(bf16[128,512]{1,0:T(8,128)(2,1)S(1)} %get-tuple-element.26), channel_id=1, source_target_pairs={{0,2},{1,3},{2,0},{3,1},{4,6},{5,7},{6,4},{7,5},{8,10},{9,11},{10,... | collective-permute-start | bytes 393224 | tf_op jit(solution)/shard_map/ppermute | solution.py:266
  28.4 4.8 %collective-permute-done.10.b2 = bf16[2,64,1024]{2,1,0:T(8,128)(2,1)S(1)} collective-permute-done((bf16[2,64,1024]{2,1,0:T(8,128)(2,1)S(1)}, bf16[2,64,1024]{2,1,0:T(8,128)(2,1)S(1)}, u32[]{:S(2)}, u32[]{:S(2)}) %collective-permute-start.10) | collective-permute-done | bytes 262176 | tf_op jit(solution)/shard_map/ppermute | solution.py:266
  33.2 3.7 %collective-permute-start.2 = (bf16[128,512]{1,0:T(8,128)(2,1)S(1)}, bf16[128,512]{1,0:T(8,128)(2,1)S(1)}, u32[]{:S(2)}, u32[]{:S(2)}) collective-permute-start(bf16[128,512]{1,0:T(8,128)(2,1)S(1)} %get-tuple-element.27), channel_id=1, source_target_pairs={{0,6},{1,7},{2,4},{3,5},{4,2},{5,3},{6,0},{7,1},{8,14},{9,15},{10,... | collective-permute-start | bytes 393224 | tf_op jit(solution)/shard_map/ppermute | solution.py:266
  36.9 2.9 %collective-permute-done.8.b1 = bf16[2,64,1024]{2,1,0:T(8,128)(2,1)S(1)} collective-permute-done((bf16[2,64,1024]{2,1,0:T(8,128)(2,1)S(1)}, bf16[2,64,1024]{2,1,0:T(8,128)(2,1)S(1)}, u32[]{:S(2)}, u32[]{:S(2)}) %collective-permute-start.8) | collective-permute-done | bytes 262176 | tf_op jit(solution)/shard_map/ppermute | solution.py:266
  39.9 1.2 %collective-permute-start.3 = (bf16[128,512]{1,0:T(8,128)(2,1)S(1)}, bf16[128,512]{1,0:T(8,128)(2,1)S(1)}, u32[]{:S(2)}, u32[]{:S(2)}) collective-permute-start(bf16[128,512]{1,0:T(8,128)(2,1)S(1)} %get-tuple-element.28), channel_id=1, source_target_pairs={{0,4},{1,5},{2,6},{3,7},{4,0},{5,1},{6,2},{7,3},{8,12},{9,13},{10,... | collective-permute-start | bytes 393224 | tf_op jit(solution)/shard_map/ppermute | solution.py:266
  41.0 4.3 %shard_map.108 = (bf16[2,64,1024]{2,1,0:T(8,128)(2,1)S(1)}, bf16[2,64,1024]{2,1,0:T(8,128)(2,1)}, bf16[2,64,1024]{2,1,0:T(8,128)(2,1)}, bf16[2,64,1024]{2,1,0:T(8,128)(2,1)}) custom-call(s32[5]{0:T(128)S(1)} %stack.32.pos_ref, bf16[2,64,1024]{2,1,0:T(8,128)(2,1)S(1)} %pad_maximum_fusion.b0, bf16[2,64,1024]{2,1,0:T(8,128)(2,1)S(1)} %collective-permute-done.8.b1, ...), custom_call_target="tpu_custom_call" | custom-call | tf_op jit(solution)/shard_map/pallas_call | solution.py:277
  45.4 1.6 %collective-permute-start.12 = (bf16[2,64,1024]{2,1,0:T(8,128)(2,1)}, bf16[2,64,1024]{2,1,0:T(8,128)(2,1)S(1)}, u32[]{:S(2)}, u32[]{:S(2)}) collective-permute-start(bf16[2,64,1024]{2,1,0:T(8,128)(2,1)} %get-tuple-element.35), channel_id=1, source_target_pairs={{0,16},{8,24},{16,0},{24,8},{32,48},{40,56},{48,32},{56,40},{64,80... | collective-permute-start | bytes 786440 | tf_op jit(solution)/shard_map/ppermute | solution.py:266
  46.9 2.2 %collective-permute-start.13 = (bf16[2,64,1024]{2,1,0:T(8,128)(2,1)}, bf16[2,64,1024]{2,1,0:T(8,128)(2,1)S(1)}, u32[]{:S(2)}, u32[]{:S(2)}) collective-permute-start(bf16[2,64,1024]{2,1,0:T(8,128)(2,1)} %get-tuple-element.36), channel_id=1, source_target_pairs={{0,48},{8,56},{16,32},{24,40},{32,16},{40,24},{48,0},{56,8},{64,11... | collective-permute-start | bytes 786440 | tf_op jit(solution)/shard_map/ppermute | solution.py:266
  49.9 0.8 shard_map.104
  51.3 3.0 %shard_map.105 = (bf16[16,2,128,256]{3,2,1,0:T(8,128)(2,1)S(1)}, bf16[16,256,512]{2,1,0:T(8,128)(2,1)S(1)}, bf16[16,256,512]{2,1,0:T(8,128)(2,1)S(1)}) custom-call(s32[5]{0:T(128)S(1)} %stack.32.pos_ref, s32[16]{0:T(128)S(1)} %copy-done.7, bf16[2,128,512]{2,1,0:T(8,128)(2,1)S(1)} %copy-done.3, bf16[128,512]{1,0:T(8,128)(2,1)S(1)} %copy-done.6), custom_call_target="tpu_custom_call" | custom-call | tf_op jit(solution)/shard_map/pallas_call | solution.py:277
  54.4 9.2 %shard_map.111 = bf16[16,32,256]{2,1,0:T(8,128)(2,1)} custom-call(s32[5]{0:T(128)S(1)} %stack.32.pos_ref, bf16[128,512]{1,0:T(8,128)(2,1)S(1)} %get-tuple-element.29.gm_ref, bf16[128,512]{1,0:T(8,128)(2,1)S(1)} %collective-permute-done.4.gs_ref, bf16[128,512]{1,0:T(8,128)(2,1)S(1)} %collective-permute-done.5.gp_ref, ...), custom_call_target="tpu_custom_call" | custom-call | tf_op jit(solution)/shard_map/pallas_call | solution.py:277
  63.6 11.6 %all-to-all-start = ((bf16[16,32,256]{2,1,0:T(8,128)(2,1)}), bf16[16,32,256]{2,1,0:T(8,128)(2,1)S(1)}, u32[]{:S(2)}, u32[]{:S(2)}) async-start(bf16[16,32,256]{2,1,0:T(8,128)(2,1)} %shard_map.111), calls=%async_computation | async-start | bytes 524288 | tf_op jit(solution)/shard_map/all_to_all | solution.py:368
  75.9 0.9 %copy-done.5 = bf16[2,64,1024]{2,1,0:T(8,128)(2,1)S(1)} copy-done((bf16[2,64,1024]{2,1,0:T(8,128)(2,1)S(1)}, bf16[2,64,1024]{2,1,0:T(8,128)(2,1)}, u32[]{:S(2)}) %copy-start.5) | copy-done | bytes 262168
  76.9 1.7 %shard_map.109 = (f32[64,1024]{1,0:T(8,128)S(1)}, bf16[64,1024]{1,0:T(8,128)(2,1)}) custom-call(bf16[2,64,1024]{2,1,0:T(8,128)(2,1)S(1)} %get-tuple-element.34.k, bf16[2,64,1024]{2,1,0:T(8,128)(2,1)S(1)} %collective-permute-done.12.r1, bf16[2,64,1024]{2,1,0:T(8,128)(2,1)S(1)} %copy-done.5, bf16[2,64,1024]{2,1,0:T(8,128)(2,1)} %collective-permute-done.14.r2), custom_call_target="tpu_custom_call" | custom-call | tf_op jit(solution)/shard_map/pallas_call | solution.py:277
  78.6 3.4 %collective-permute-start.15 = (bf16[64,1024]{1,0:T(8,128)(2,1)}, bf16[64,1024]{1,0:T(8,128)(2,1)S(1)}, u32[]{:S(2)}, u32[]{:S(2)}) collective-permute-start(bf16[64,1024]{1,0:T(8,128)(2,1)} %get-tuple-element.39), channel_id=1, source_target_pairs={{0,64},{8,72},{16,80},{24,88},{32,96},{40,104},{48,112},{56,120},{... | collective-permute-start | bytes 393224 | tf_op jit(solution)/shard_map/ppermute | solution.py:266
  82.0 8.0 %shard_map.106 = f32[128,512]{1,0:T(8,128)} custom-call(s32[5]{0:T(128)S(1)} %stack.32.pos_ref, bf16[128,512]{1,0:T(8,128)(2,1)S(1)} %get-tuple-element.29.gm_ref, bf16[128,512]{1,0:T(8,128)(2,1)S(1)} %collective-permute-done.4.gs_ref, bf16[128,512]{1,0:T(8,128)(2,1)S(1)} %collective-permute-done.5.gp_ref, bf16[16,2,128,256]{3,2,1,0:T(8,128)(2,1)S(1)} %get-tuple-element.30.l_ref), custom_call_target="tpu_custom_call" | custom-call | tf_op jit(solution)/shard_map/pallas_call | solution.py:277
  90.0 1.4 %shard_map.112 = f32[2,32,128]{2,1,0:T(8,128)} custom-call(s32[5]{0:T(128)S(1)} %stack.32.pos_ref, s32[16]{0:T(128)S(1)} %copy-done.7, bf16[16,32,256]{2,1,0:T(8,128)(2,1)S(1)} %all-to-all-done.got), custom_call_target="tpu_custom_call" | custom-call | tf_op jit(solution)/shard_map/pallas_call | solution.py:277
  (41 shorter events, 3.9 us)
Async XLA Ops:
  0.6 40.4 %copy-start = (bf16[512,1024]{1,0:T(8,128)(2,1)S(1)}, bf16[512,1024]{1,0:T(8,128)(2,1)}, u32[]{:S(2)}) copy-start(bf16[512,1024]{1,0:T(8,128)(2,1)} %og_ref.1) | copy-start | bytes 3145732
  0.6 40.4 %collective-permute-start.11 = (bf16[512,1024]{1,0:T(8,128)(2,1)}, bf16[512,1024]{1,0:T(8,128)(2,1)S(1)}, u32[]{:S(2)}, u32[]{:S(2)}) collective-permute-start(bf16[512,1024]{1,0:T(8,128)(2,1)} %og_ref.1), channel_id=1, source_target_pairs={{0,8},{8,0},{16,24},{24,16},{32,40},{40,32},{48,56},{56,48},{64,72... | collective-permute-start | bytes 3145736 | tf_op jit(solution)/shard_map/ppermute | solution.py:266
  0.8 49.0 %copy-start.1 = (bf16[128,512]{1,0:T(8,128)(2,1)S(1)}, bf16[128,512]{1,0:T(8,128)(2,1)}, u32[]{:S(2)}) copy-start(bf16[128,512]{1,0:T(8,128)(2,1)} %v_hbm.1) | copy-start | bytes 393220
  0.8 49.0 %copy-start.2 = (bf16[128,512]{1,0:T(8,128)(2,1)S(1)}, bf16[128,512]{1,0:T(8,128)(2,1)}, u32[]{:S(2)}) copy-start(bf16[128,512]{1,0:T(8,128)(2,1)} %g_hbm.1) | copy-start | bytes 393220
  0.8 50.5 %copy-start.3 = (bf16[2,128,512]{2,1,0:T(8,128)(2,1)S(1)}, bf16[2,128,512]{2,1,0:T(8,128)(2,1)}, u32[]{:S(2)}) copy-start(bf16[2,128,512]{2,1,0:T(8,128)(2,1)} %f_ref.1) | copy-start | bytes 786436
  0.8 50.5 %copy-start.6 = (bf16[128,512]{1,0:T(8,128)(2,1)S(1)}, bf16[128,512]{1,0:T(8,128)(2,1)}, u32[]{:S(2)}) copy-start(bf16[128,512]{1,0:T(8,128)(2,1)} %x_ref.1) | copy-start | bytes 393220
  0.8 50.5 %copy-start.7 = (s32[16]{0:T(128)S(1)}, s32[16]{0:T(128)}, u32[]{:S(2)}) copy-start(s32[16]{0:T(128)} %reach_ref.3) | copy-start | bytes 196
  4.7 22.3 %collective-permute-start = (bf16[512,512]{1,0:T(8,128)(2,1)S(1)}, bf16[512,512]{1,0:T(8,128)(2,1)S(1)}, u32[]{:S(2)}, u32[]{:S(2)}) collective-permute-start(bf16[512,512]{1,0:T(8,128)(2,1)S(1)} %get-tuple-element.24), channel_id=1, source_target_pairs={{0,1},{1,0},{2,3},{3,2},{4,5},{5,4},{6,7},{7,6},{8,9},{9,8},{10,11... | collective-permute-start | bytes 1572872 | tf_op jit(solution)/shard_map/ppermute | solution.py:266
  8.0 1.3 %collective-permute-start.6 = (bf16[64,512]{1,0:T(8,128)(2,1)S(1)}, bf16[64,512]{1,0:T(8,128)(2,1)S(1)}, u32[]{:S(2)}, u32[]{:S(2)}) collective-permute-start(bf16[64,512]{1,0:T(8,128)(2,1)S(1)} %get-tuple-element.33), channel_id=1, source_target_pairs={{0,8},{8,0},{16,24},{24,16},{32,40},{40,32},{48,56},{56,48},{64,72... | collective-permute-start | bytes 196616 | tf_op jit(solution)/shard_map/ppermute | solution.py:266
  9.3 12.6 %collective-permute-start.7 = (bf16[64,1024]{1,0:T(8,128)(2,1)S(1)}, bf16[64,1024]{1,0:T(8,128)(2,1)S(1)}, u32[]{:S(2)}, u32[]{:S(2)}) collective-permute-start(bf16[64,1024]{1,0:T(8,128)(2,1)S(1)} %constant_dynamic-update-slice_fusion), channel_id=1, source_target_pairs={{0,1},{1,0},{2,3},{3,2},{4,5},{5,4},{6,7},{7,6},{8,9},{9,8},{10,11... | collective-permute-start | bytes 393224 | tf_op jit(solution)/shard_map/ppermute | solution.py:266
  22.0 11.2 %collective-permute-start.10 = (bf16[2,64,1024]{2,1,0:T(8,128)(2,1)S(1)}, bf16[2,64,1024]{2,1,0:T(8,128)(2,1)S(1)}, u32[]{:S(2)}, u32[]{:S(2)}) collective-permute-start(bf16[2,64,1024]{2,1,0:T(8,128)(2,1)S(1)} %pad_maximum_fusion.b0), channel_id=1, source_target_pairs={{0,4},{1,5},{2,6},{3,7},{4,0},{5,1},{6,2},{7,3},{8,12},{9,13},{10,... | collective-permute-start | bytes 786440 | tf_op jit(solution)/shard_map/ppermute | solution.py:266
  26.0 13.8 %collective-permute-start.8 = (bf16[2,64,1024]{2,1,0:T(8,128)(2,1)S(1)}, bf16[2,64,1024]{2,1,0:T(8,128)(2,1)S(1)}, u32[]{:S(2)}, u32[]{:S(2)}) collective-permute-start(bf16[2,64,1024]{2,1,0:T(8,128)(2,1)S(1)} %pad_maximum_fusion.b0), channel_id=1, source_target_pairs={{0,2},{1,3},{2,0},{3,1},{4,6},{5,7},{6,4},{7,5},{8,10},{9,11},{10,... | collective-permute-start | bytes 786440 | tf_op jit(solution)/shard_map/ppermute | solution.py:266
  27.0 14.0 %collective-permute-start.9 = (bf16[2,64,1024]{2,1,0:T(8,128)(2,1)S(1)}, bf16[2,64,1024]{2,1,0:T(8,128)(2,1)S(1)}, u32[]{:S(2)}, u32[]{:S(2)}) collective-permute-start(bf16[2,64,1024]{2,1,0:T(8,128)(2,1)S(1)} %pad_maximum_fusion.b0), channel_id=1, source_target_pairs={{0,6},{1,7},{2,4},{3,5},{4,2},{5,3},{6,0},{7,1},{8,14},{9,15},{10,... | collective-permute-start | bytes 786440 | tf_op jit(solution)/shard_map/ppermute | solution.py:266
  27.2 21.9 %collective-permute-start.1 = (bf16[128,512]{1,0:T(8,128)(2,1)S(1)}, bf16[128,512]{1,0:T(8,128)(2,1)S(1)}, u32[]{:S(2)}, u32[]{:S(2)}) collective-permute-start(bf16[128,512]{1,0:T(8,128)(2,1)S(1)} %get-tuple-element.26), channel_id=1, source_target_pairs={{0,2},{1,3},{2,0},{3,1},{4,6},{5,7},{6,4},{7,5},{8,10},{9,11},{10,... | collective-permute-start | bytes 393224 | tf_op jit(solution)/shard_map/ppermute | solution.py:266
  33.2 16.7 %collective-permute-start.2 = (bf16[128,512]{1,0:T(8,128)(2,1)S(1)}, bf16[128,512]{1,0:T(8,128)(2,1)S(1)}, u32[]{:S(2)}, u32[]{:S(2)}) collective-permute-start(bf16[128,512]{1,0:T(8,128)(2,1)S(1)} %get-tuple-element.27), channel_id=1, source_target_pairs={{0,6},{1,7},{2,4},{3,5},{4,2},{5,3},{6,0},{7,1},{8,14},{9,15},{10,... | collective-permute-start | bytes 393224 | tf_op jit(solution)/shard_map/ppermute | solution.py:266
  39.9 10.0 %collective-permute-start.3 = (bf16[128,512]{1,0:T(8,128)(2,1)S(1)}, bf16[128,512]{1,0:T(8,128)(2,1)S(1)}, u32[]{:S(2)}, u32[]{:S(2)}) collective-permute-start(bf16[128,512]{1,0:T(8,128)(2,1)S(1)} %get-tuple-element.28), channel_id=1, source_target_pairs={{0,4},{1,5},{2,6},{3,7},{4,0},{5,1},{6,2},{7,3},{8,12},{9,13},{10,... | collective-permute-start | bytes 393224 | tf_op jit(solution)/shard_map/ppermute | solution.py:266
  45.4 29.9 %collective-permute-start.12 = (bf16[2,64,1024]{2,1,0:T(8,128)(2,1)}, bf16[2,64,1024]{2,1,0:T(8,128)(2,1)S(1)}, u32[]{:S(2)}, u32[]{:S(2)}) collective-permute-start(bf16[2,64,1024]{2,1,0:T(8,128)(2,1)} %get-tuple-element.35), channel_id=1, source_target_pairs={{0,16},{8,24},{16,0},{24,8},{32,48},{40,56},{48,32},{56,40},{64,80... | collective-permute-start | bytes 786440 | tf_op jit(solution)/shard_map/ppermute | solution.py:266
  46.9 28.3 %collective-permute-start.13 = (bf16[2,64,1024]{2,1,0:T(8,128)(2,1)}, bf16[2,64,1024]{2,1,0:T(8,128)(2,1)S(1)}, u32[]{:S(2)}, u32[]{:S(2)}) collective-permute-start(bf16[2,64,1024]{2,1,0:T(8,128)(2,1)} %get-tuple-element.36), channel_id=1, source_target_pairs={{0,48},{8,56},{16,32},{24,40},{32,16},{40,24},{48,0},{56,8},{64,11... | collective-permute-start | bytes 786440 | tf_op jit(solution)/shard_map/ppermute | solution.py:266
  49.1 26.8 %collective-permute-start.14 = (bf16[2,64,1024]{2,1,0:T(8,128)(2,1)}, bf16[2,64,1024]{2,1,0:T(8,128)(2,1)}, u32[]{:S(2)}, u32[]{:S(2)}) collective-permute-start(bf16[2,64,1024]{2,1,0:T(8,128)(2,1)} %get-tuple-element.37), channel_id=1, source_target_pairs={{0,32},{8,40},{16,48},{24,56},{32,0},{40,8},{48,16},{56,24},{64,96... | collective-permute-start | bytes 786440 | tf_op jit(solution)/shard_map/ppermute | solution.py:266
  50.6 3.7 %collective-permute-start.4 = (bf16[128,512]{1,0:T(8,128)(2,1)S(1)}, bf16[128,512]{1,0:T(8,128)(2,1)S(1)}, u32[]{:S(2)}, u32[]{:S(2)}) collective-permute-start(bf16[128,512]{1,0:T(8,128)(2,1)S(1)} %get-tuple-element.29.gm_ref), channel_id=1, source_target_pairs={{0,8},{8,0},{16,24},{24,16},{32,40},{40,32},{48,56},{56,48},{64,72... | collective-permute-start | bytes 393224 | tf_op jit(solution)/shard_map/ppermute | solution.py:266
  50.6 3.7 %collective-permute-start.5 = (bf16[128,512]{1,0:T(8,128)(2,1)S(1)}, bf16[128,512]{1,0:T(8,128)(2,1)S(1)}, u32[]{:S(2)}, u32[]{:S(2)}) collective-permute-start(bf16[128,512]{1,0:T(8,128)(2,1)S(1)} %get-tuple-element.29.gm_ref), channel_id=1, source_target_pairs={{8,16},{24,32},{40,48},{56,64},{72,80},{88,96},{104,112},{16,8},{3... | collective-permute-start | bytes 393224 | tf_op jit(solution)/shard_map/ppermute | solution.py:339
  63.6 26.5 %all-to-all-start = ((bf16[16,32,256]{2,1,0:T(8,128)(2,1)}), bf16[16,32,256]{2,1,0:T(8,128)(2,1)S(1)}, u32[]{:S(2)}, u32[]{:S(2)}) async-start(bf16[16,32,256]{2,1,0:T(8,128)(2,1)} %shard_map.111), calls=%async_computation | async-start | bytes 524288 | tf_op jit(solution)/shard_map/all_to_all | solution.py:368
  75.9 1.0 %copy-start.5 = (bf16[2,64,1024]{2,1,0:T(8,128)(2,1)S(1)}, bf16[2,64,1024]{2,1,0:T(8,128)(2,1)}, u32[]{:S(2)}) copy-start(bf16[2,64,1024]{2,1,0:T(8,128)(2,1)} %copy-done.4) | copy-start | bytes 786436
  78.6 12.9 %collective-permute-start.15 = (bf16[64,1024]{1,0:T(8,128)(2,1)}, bf16[64,1024]{1,0:T(8,128)(2,1)S(1)}, u32[]{:S(2)}, u32[]{:S(2)}) collective-permute-start(bf16[64,1024]{1,0:T(8,128)(2,1)} %get-tuple-element.39), channel_id=1, source_target_pairs={{0,64},{8,72},{16,80},{24,88},{32,96},{40,104},{48,112},{56,120},{... | collective-permute-start | bytes 393224 | tf_op jit(solution)/shard_map/ppermute | solution.py:266
  (1 other events, 0.7 us)

commit v5 on v4

--- a/solution.py
+++ b/solution.py
@@ -101,7 +101,7 @@
     return jnp.concatenate(pair, axis=0).astype(BF16)
 
 
-def prepare(pos_ref, reach_ref, f_ref, x_ref, l_ref, ui_ref, uo_ref):
+def prepare(pos_ref, reach_ref, f_ref, x_ref, l_ref, u_ref):
     rows, n = x_ref.shape
     width = 3 * n
     chan = pos_ref[0] * 2 + pos_ref[1]
@@ -134,22 +134,10 @@
             for d in range(2):
                 for k in range(8):
                     start = n - 128 * (k // 2) if d == 0 else 128 * (k // 2)
-                    part = bases[d][k % 2][:, start : start + 2 * n]
-                    inner, outer = (part[:, :n], part[:, n:]) if d == 0 else (part[:, n:], part[:, :n])
-                    at = 128 * d + 16 * k
-                    ui_ref[group, at : at + 16, :] = inner
-                    uo_ref[group, at : at + 16, :] = outer
+                    u_ref[group, d, 16 * k : 16 * k + 16, :] = bases[d][k % 2][:, start : start + 2 * n]
         return carry
 
     lax.fori_loop(0, rows // 16, step, 0)
-
-
-def with_halos(pos_ref, gm_ref, gs_ref, gp_ref, band):
-    core0 = (pos_ref[4] & 1) == 0
-    gm = gm_ref[band, :].astype(F32)
-    gs = gs_ref[band, :].astype(F32)
-    gp = gp_ref[band, :].astype(F32)
-    return jnp.concatenate([jnp.where(core0, gp, gs), gm, jnp.where(core0, gs, gp)], axis=1)
 
 
 def fill_shifted(h_ref, h, ext):
@@ -160,73 +148,100 @@
         h_ref[h, 16 * k : 16 * k + 16, :] = moved
 
 
-def tap_grads(pos_ref, gm_ref, gs_ref, gp_ref, ui_ref, uo_ref, t_ref, h_ref, acc_ref):
-    rows, n = gm_ref.shape
+def input_part(d, l_ref, h_ref, group, h):
+    n = h_ref.shape[2] // 2
+    lanes = n // 128
+    total = None
+    acc = [[None] * (lanes + (b > 0)) for b in range(4)]
+    for j in range(lanes):
+        if d == 0:
+            lo, hi = (0, 64) if j == 0 else (64, 128) if j == lanes - 1 else (0, 128)
+        else:
+            lo, hi = (48, 128) if j == 0 else (0, 64) if j == lanes - 1 else (0, 128)
+        p = dot(l_ref[group, d, lo:hi, :], h_ref[h, :, 256 * j : 256 * j + 256])
+        for u in range(lo // 8, hi // 8):
+            a, b = divmod(u + d, 4)
+            for c in range(2):
+                q = 2 * j + c
+                slot = q - a if d == 0 else q - (lanes - (b > 0)) + a
+                if 0 <= slot < len(acc[b]):
+                    part = p[8 * u - lo : 8 * u - lo + 8, 128 * c : 128 * c + 128]
+                    acc[b][slot] = part if acc[b][slot] is None else acc[b][slot] + part
+    for b in range(4):
+        line = jnp.concatenate(acc[b], axis=1)
+        if b and d == 0:
+            line = pltpu.roll(line, n + 128 - 32 * b, 1)[:, :n]
+        elif b:
+            line = pltpu.roll(line, 32 * b, 1)[:, 128:]
+        total = line if total is None else total + line
+    return total
+
+
+def tap_part(d, u_ref, h_ref, group, h, own_cols, acc_ref):
+    cross = dot(u_ref[group, d], h_ref[h], NT)
+    sums = jnp.sum(jnp.where(own_cols, cross.reshape(16, 8, 256), 0.0), axis=1)
+    for u in range(16):
+        acc_ref[u, pl.ds(group, 1), :] = sums[u : u + 1]
+
+
+def one_side(pos_ref, gm_ref, halo_ref, h_ref, per_group, outer):
+    core = pos_ref[4] & 1
+    for c in range(2):
+        d = 1 - c if outer else c
+
+        @pl.when(core == c)
+        def _():
+            def step(i, carry):
+                band = pl.ds(pl.multiple_of(i * 16, 16), 16)
+                gm = gm_ref[band, :].astype(F32)
+                halo = halo_ref[band, :].astype(F32)
+                ext16 = jnp.concatenate([gm, halo] if d == 0 else [halo, gm], axis=1)
+                for h in range(2):
+                    fill_shifted(h_ref, h, ext16[8 * h : 8 * h + 8])
+                per_group(d, i, band)
+                return carry
+
+            lax.fori_loop(0, gm_ref.shape[0] // 16, step, 0)
+
+
+def inner_side(pos_ref, gm_ref, halo_ref, l_ref, u_ref, o_ref, t_ref, h_ref, acc_ref):
     own_cols = iota((16, 8, 256), 1) == (iota((16, 8, 256), 2) & 7)
 
-    def step(i, carry):
-        band = pl.ds(pl.multiple_of(i * 16, 16), 16)
-        ext16 = with_halos(pos_ref, gm_ref, gs_ref, gp_ref, band)
+    def per_group(d, i, band):
+        o_ref[band, :] = jnp.concatenate(
+            [input_part(d, l_ref, h_ref, 2 * i + h, h) for h in range(2)], axis=0
+        )
         for h in range(2):
-            group = 2 * i + h
-            fill_shifted(h_ref, h, ext16[8 * h : 8 * h + 8])
-            inner = dot(ui_ref[group], h_ref[h, :, n : 2 * n], NT)
-            for d in range(2):
-                start = 2 * n * (1 - d)
-                cross = inner[128 * d : 128 * d + 128] + dot(
-                    uo_ref[group, 128 * d : 128 * d + 128, :], h_ref[h, :, start : start + n], NT
-                )
-                sums = jnp.sum(jnp.where(own_cols, cross.reshape(16, 8, 256), 0.0), axis=1)
-                row = d * (rows // 8) + group
-                for u in range(16):
-                    acc_ref[u, pl.ds(row, 1), :] = sums[u : u + 1]
-        return carry
-
-    lax.fori_loop(0, rows // 16, step, 0)
+            tap_part(d, u_ref, h_ref, 2 * i + h, h, own_cols, acc_ref)
+
+    one_side(pos_ref, gm_ref, halo_ref, h_ref, per_group, False)
     t_ref[...] = acc_ref[...].astype(BF16)
 
 
-def input_grad(pos_ref, gm_ref, gs_ref, gp_ref, l_ref, o_ref, h_ref):
-    rows, n = gm_ref.shape
-    lanes = n // 128
-
-    def step(i, carry):
-        band = pl.ds(pl.multiple_of(i * 16, 16), 16)
-        ext16 = with_halos(pos_ref, gm_ref, gs_ref, gp_ref, band)
-        outs = []
+def outer_taps(pos_ref, gm_ref, halo_ref, u_ref, inner_ref, t_ref, h_ref, acc_ref):
+    own_cols = iota((16, 8, 256), 1) == (iota((16, 8, 256), 2) & 7)
+
+    def per_group(d, i, band):
         for h in range(2):
-            group = 2 * i + h
-            fill_shifted(h_ref, h, ext16[8 * h : 8 * h + 8])
-            total = None
-            for d in range(2):
-                acc = [[None] * (lanes + (b > 0)) for b in range(4)]
-                for j in range(lanes):
-                    if d == 0:
-                        lo, hi = (0, 64) if j == 0 else (64, 128) if j == lanes - 1 else (0, 128)
-                    else:
-                        lo, hi = (48, 128) if j == 0 else (0, 64) if j == lanes - 1 else (0, 128)
-                    at = n * (1 - d) + 256 * j
-                    p = dot(l_ref[group, d, lo:hi, :], h_ref[h, :, at : at + 256])
-                    for u in range(lo // 8, hi // 8):
-                        a, b = divmod(u + d, 4)
-                        for c in range(2):
-                            q = 2 * j + c
-                            slot = q - a if d == 0 else q - (lanes - (b > 0)) + a
-                            if 0 <= slot < len(acc[b]):
-                                part = p[8 * u - lo : 8 * u - lo + 8, 128 * c : 128 * c + 128]
-                                acc[b][slot] = part if acc[b][slot] is None else acc[b][slot] + part
-                for b in range(4):
-                    line = jnp.concatenate(acc[b], axis=1)
-                    if b and d == 0:
-                        line = pltpu.roll(line, n + 128 - 32 * b, 1)[:, :n]
-                    elif b:
-                        line = pltpu.roll(line, 32 * b, 1)[:, 128:]
-                    total = line if total is None else total + line
-            outs.append(total)
-        o_ref[band, :] = jnp.concatenate(outs, axis=0)
-        return carry
-
-    lax.fori_loop(0, rows // 16, step, 0)
+            tap_part(d, u_ref, h_ref, 2 * i + h, h, own_cols, acc_ref)
+
+    one_side(pos_ref, gm_ref, halo_ref, h_ref, per_group, True)
+    count = inner_ref.shape[1]
+    core = pos_ref[4] & 1
+    for c in range(2):
+
+        @pl.when(core == c)
+        def _():
+            t_ref[:, count * c : count * c + count, :] = inner_ref[...]
+            t_ref[:, count * (1 - c) : count * (1 - c) + count, :] = acc_ref[...].astype(BF16)
+
+
+def outer_input(pos_ref, gm_ref, halo_ref, l_ref, inner_ref, o_ref, h_ref):
+    def per_group(d, i, band):
+        parts = [input_part(d, l_ref, h_ref, 2 * i + h, h) for h in range(2)]
+        o_ref[band, :] = inner_ref[band, :] + jnp.concatenate(parts, axis=0)
+
+    one_side(pos_ref, gm_ref, halo_ref, h_ref, per_group, True)
 
 
 def sum_pieces(k, r1, r3, r2, keep, send):
@@ -347,26 +362,36 @@
     e = [e[0], swap(e[1], "seq", 2), swap(e[2], "seq", 6), swap(e[3], "seq", 4)]
 
     groups = rows // 8
-    prepared = call(
+    tap_rows, input_rows = call(
         prepare,
         [
             shape((groups, 2, 128, 256), BF16),
-            shape((groups, 256, tok), BF16),
-            shape((groups, 256, tok), BF16),
+            shape((groups, 2, 128, 2 * tok), BF16),
         ],
         (pos, filter_reach, filters, conv_input),
         scalars=2,
     )
-    halos = (pos, grad_conv, halo_core, halo_out)
-    shifted = pltpu.VMEM((2, 256, 3 * tok), BF16)
+    shifted = pltpu.VMEM((2, 256, 2 * tok), BF16)
+    sums = pltpu.VMEM((seq_count, groups, 256), F32)
+    grad_input, tap_sums = call(
+        inner_side,
+        [shape((rows, tok), F32), shape((seq_count, groups, 256), BF16)],
+        (pos, grad_conv, halo_core, tap_rows, input_rows),
+        scratch=[shifted, sums],
+    )
     tap_sums = call(
-        tap_grads,
-        shape((seq_count, rows // 4, 256), BF16),
-        (*halos, *prepared[1:]),
-        scratch=[shifted, pltpu.VMEM((seq_count, rows // 4, 256), F32)],
+        outer_taps,
+        shape((seq_count, 2 * groups, 256), BF16),
+        (pos, grad_conv, halo_out, input_rows, tap_sums),
+        scratch=[shifted, sums],
     )
     tap_sums = lax.all_to_all(tap_sums, "seq", 0, 0)
-    grad_input = call(input_grad, shape((rows, tok), F32), (*halos, prepared[0]), scratch=[shifted])
+    grad_input = call(
+        outer_input,
+        shape((rows, tok), F32),
+        (pos, grad_conv, halo_out, tap_rows, grad_input),
+        scratch=[shifted],
+    )
     e_keep, e_send = call(
         sum_pieces, [shape((half, feats), F32), shape((half, feats), BF16)], e, scalars=0
     )

time: 93.2 us -> 94.9 us (1.018)
  Pallas kernels: 34.8 us -> 39.1 us
  starting transfers between devices: 33.8 us -> 31.2 us
    pallas_call x11 -> x12, Pallas kernels: 34.8 us -> 39.1 us  [call(): pl.pallas_call(body, out_shape=out_shape, in_specs=[smem()] * scalars + [...]
    all_to_all x1, starting transfers between devices: 11.6 us -> 8.89 us  [on_device_0(): tap_sums = lax.all_to_all(tap_sums, 'seq', 0, 0)]
  transfers between devices with their start and end apart: 17 -> 17, of which waited for: 4 -> 4; matrix products, arithmetic and copies ran while one was open for 0% -> 0% of each run, Pallas kernels for 37% -> 41%
where the time goes in v5:
time: 94.9 us; the launch traced here: 93.9 us
  Pallas kernels  39.1 us (41%)
  starting transfers between devices  31.2 us (33%)
  waiting for transfers between devices  21 us (22%)
  local copies, waits for them, and re-layouts  1.77 us (2%)
    pallas_call x12, Pallas kernels, call(): pl.pallas_call(body, out_shape=out_shape, in_specs=[smem()] * scalars + [...  39.1 us
    ppermute x15, starting transfers between devices, swap(): lax.ppermute(v, axis, [(i, i ^ mask) for i in range(lax.axis_size(axis))])  21.6 us
    ppermute x15, waiting for transfers between devices, swap(): lax.ppermute(v, axis, [(i, i ^ mask) for i in range(lax.axis_size(axis))])  21 us
    all_to_all x1, starting transfers between devices, on_device_0(): tap_sums = lax.all_to_all(tap_sums, 'seq', 0, 0)  8.89 us
  transfers between devices with their start and end apart: 17, of which 4 were waited for; matrix products, arithmetic and copies ran while one was open for 0% of the time, Pallas kernels for 41%

profile of v5, /device:TPU:0, one launch (start us, length us, event | category | flops | bytes accessed | tf_op | source)
XLA Modules:
  0.0 93.9 jit_solution(9616798986342155033)
XLA Ops:
  0.8 3.9 %shard_map.102 = (bf16[512,512]{1,0:T(8,128)(2,1)S(1)}, bf16[512,512]{1,0:T(8,128)(2,1)S(1)}) custom-call(s32[5]{0:T(128)S(1)} %stack.32.pos_ref, bf16[1024,1024]{1,0:T(8,128)(2,1)} %w_hbm.1, bf16[512,1024]{1,0:T(8,128)(2,1)} %og_ref.1), custom_call_target="tpu_custom_call" | custom-call | tf_op jit(solution)/shard_map/pallas_call | solution.py:292
  4.7 1.7 %collective-permute-start = (bf16[512,512]{1,0:T(8,128)(2,1)S(1)}, bf16[512,512]{1,0:T(8,128)(2,1)S(1)}, u32[]{:S(2)}, u32[]{:S(2)}) collective-permute-start(bf16[512,512]{1,0:T(8,128)(2,1)S(1)} %get-tuple-element.25), channel_id=1, source_target_pairs={{0,1},{1,0},{2,3},{3,2},{4,5},{5,4},{6,7},{7,6},{8,9},{9,8},{10,11... | collective-permute-start | bytes 1572872 | tf_op jit(solution)/shard_map/ppermute | solution.py:281
  6.4 1.6 %shard_map.108 = (bf16[64,512]{1,0:T(8,128)(2,1)S(1)}, bf16[64,512]{1,0:T(8,128)(2,1)S(1)}) custom-call(s32[5]{0:T(128)S(1)} %stack.32.pos_ref, bf16[128,512]{1,0:T(8,128)(2,1)} %v_hbm.1, bf16[128,512]{1,0:T(8,128)(2,1)} %g_hbm.1), custom_call_target="tpu_custom_call" | custom-call | tf_op jit(solution)/shard_map/pallas_call | solution.py:292
  8.2 1.1 %collective-permute-done.6 = bf16[64,512]{1,0:T(8,128)(2,1)S(1)} collective-permute-done((bf16[64,512]{1,0:T(8,128)(2,1)S(1)}, bf16[64,512]{1,0:T(8,128)(2,1)S(1)}, u32[]{:S(2)}, u32[]{:S(2)}) %collective-permute-start.6) | collective-permute-done | bytes 65568 | tf_op jit(solution)/shard_map/ppermute | solution.py:281
  9.7 12.2 %collective-permute-done.7 = bf16[64,1024]{1,0:T(8,128)(2,1)S(1)} collective-permute-done((bf16[64,1024]{1,0:T(8,128)(2,1)S(1)}, bf16[64,1024]{1,0:T(8,128)(2,1)S(1)}, u32[]{:S(2)}, u32[]{:S(2)}) %collective-permute-start.7) | collective-permute-done | bytes 131104 | tf_op jit(solution)/shard_map/ppermute | solution.py:281
  21.9 4.1 %collective-permute-start.10 = (bf16[2,64,1024]{2,1,0:T(8,128)(2,1)S(1)}, bf16[2,64,1024]{2,1,0:T(8,128)(2,1)S(1)}, u32[]{:S(2)}, u32[]{:S(2)}) collective-permute-start(bf16[2,64,1024]{2,1,0:T(8,128)(2,1)S(1)} %pad_maximum_fusion.b0), channel_id=1, source_target_pairs={{0,4},{1,5},{2,6},{3,7},{4,0},{5,1},{6,2},{7,3},{8,12},{9,13},{10,... | collective-permute-start | bytes 786440 | tf_op jit(solution)/shard_map/ppermute | solution.py:281
  26.0 1.0 %collective-permute-start.8 = (bf16[2,64,1024]{2,1,0:T(8,128)(2,1)S(1)}, bf16[2,64,1024]{2,1,0:T(8,128)(2,1)S(1)}, u32[]{:S(2)}, u32[]{:S(2)}) collective-permute-start(bf16[2,64,1024]{2,1,0:T(8,128)(2,1)S(1)} %pad_maximum_fusion.b0), channel_id=1, source_target_pairs={{0,2},{1,3},{2,0},{3,1},{4,6},{5,7},{6,4},{7,5},{8,10},{9,11},{10,... | collective-permute-start | bytes 786440 | tf_op jit(solution)/shard_map/ppermute | solution.py:281
  27.2 1.2 %collective-permute-start.1 = (bf16[128,512]{1,0:T(8,128)(2,1)S(1)}, bf16[128,512]{1,0:T(8,128)(2,1)S(1)}, u32[]{:S(2)}, u32[]{:S(2)}) collective-permute-start(bf16[128,512]{1,0:T(8,128)(2,1)S(1)} %get-tuple-element.27), channel_id=1, source_target_pairs={{0,2},{1,3},{2,0},{3,1},{4,6},{5,7},{6,4},{7,5},{8,10},{9,11},{10,... | collective-permute-start | bytes 393224 | tf_op jit(solution)/shard_map/ppermute | solution.py:281
  28.4 4.8 %collective-permute-done.10.b2 = bf16[2,64,1024]{2,1,0:T(8,128)(2,1)S(1)} collective-permute-done((bf16[2,64,1024]{2,1,0:T(8,128)(2,1)S(1)}, bf16[2,64,1024]{2,1,0:T(8,128)(2,1)S(1)}, u32[]{:S(2)}, u32[]{:S(2)}) %collective-permute-start.10) | collective-permute-done | bytes 262176 | tf_op jit(solution)/shard_map/ppermute | solution.py:281
  33.1 3.7 %collective-permute-start.2 = (bf16[128,512]{1,0:T(8,128)(2,1)S(1)}, bf16[128,512]{1,0:T(8,128)(2,1)S(1)}, u32[]{:S(2)}, u32[]{:S(2)}) collective-permute-start(bf16[128,512]{1,0:T(8,128)(2,1)S(1)} %get-tuple-element.28), channel_id=1, source_target_pairs={{0,6},{1,7},{2,4},{3,5},{4,2},{5,3},{6,0},{7,1},{8,14},{9,15},{10,... | collective-permute-start | bytes 393224 | tf_op jit(solution)/shard_map/ppermute | solution.py:281
  36.9 2.9 %collective-permute-done.8.b1 = bf16[2,64,1024]{2,1,0:T(8,128)(2,1)S(1)} collective-permute-done((bf16[2,64,1024]{2,1,0:T(8,128)(2,1)S(1)}, bf16[2,64,1024]{2,1,0:T(8,128)(2,1)S(1)}, u32[]{:S(2)}, u32[]{:S(2)}) %collective-permute-start.8) | collective-permute-done | bytes 262176 | tf_op jit(solution)/shard_map/ppermute | solution.py:281
  39.8 1.2 %collective-permute-start.3 = (bf16[128,512]{1,0:T(8,128)(2,1)S(1)}, bf16[128,512]{1,0:T(8,128)(2,1)S(1)}, u32[]{:S(2)}, u32[]{:S(2)}) collective-permute-start(bf16[128,512]{1,0:T(8,128)(2,1)S(1)} %get-tuple-element.29), channel_id=1, source_target_pairs={{0,4},{1,5},{2,6},{3,7},{4,0},{5,1},{6,2},{7,3},{8,12},{9,13},{10,... | collective-permute-start | bytes 393224 | tf_op jit(solution)/shard_map/ppermute | solution.py:281
  41.0 4.3 %shard_map.109 = (bf16[2,64,1024]{2,1,0:T(8,128)(2,1)S(1)}, bf16[2,64,1024]{2,1,0:T(8,128)(2,1)}, bf16[2,64,1024]{2,1,0:T(8,128)(2,1)}, bf16[2,64,1024]{2,1,0:T(8,128)(2,1)}) custom-call(s32[5]{0:T(128)S(1)} %stack.32.pos_ref, bf16[2,64,1024]{2,1,0:T(8,128)(2,1)S(1)} %pad_maximum_fusion.b0, bf16[2,64,1024]{2,1,0:T(8,128)(2,1)S(1)} %collective-permute-done.8.b1, ...), custom_call_target="tpu_custom_call" | custom-call | tf_op jit(solution)/shard_map/pallas_call | solution.py:292
  45.3 1.6 %collective-permute-start.12 = (bf16[2,64,1024]{2,1,0:T(8,128)(2,1)}, bf16[2,64,1024]{2,1,0:T(8,128)(2,1)S(1)}, u32[]{:S(2)}, u32[]{:S(2)}) collective-permute-start(bf16[2,64,1024]{2,1,0:T(8,128)(2,1)} %get-tuple-element.38), channel_id=1, source_target_pairs={{0,16},{8,24},{16,0},{24,8},{32,48},{40,56},{48,32},{56,40},{64,80... | collective-permute-start | bytes 786440 | tf_op jit(solution)/shard_map/ppermute | solution.py:281
  46.9 2.2 %collective-permute-start.13 = (bf16[2,64,1024]{2,1,0:T(8,128)(2,1)}, bf16[2,64,1024]{2,1,0:T(8,128)(2,1)}, u32[]{:S(2)}, u32[]{:S(2)}) collective-permute-start(bf16[2,64,1024]{2,1,0:T(8,128)(2,1)} %get-tuple-element.39), channel_id=1, source_target_pairs={{0,48},{8,56},{16,32},{24,40},{32,16},{40,24},{48,0},{56,8},{64,11... | collective-permute-start | bytes 786440 | tf_op jit(solution)/shard_map/ppermute | solution.py:281
  51.3 3.0 %shard_map.105 = (bf16[16,2,128,256]{3,2,1,0:T(8,128)(2,1)S(1)}, bf16[16,2,128,1024]{3,2,1,0:T(8,128)(2,1)S(1)}) custom-call(s32[5]{0:T(128)S(1)} %stack.32.pos_ref, s32[16]{0:T(128)S(1)} %copy-done.7, bf16[2,128,512]{2,1,0:T(8,128)(2,1)S(1)} %copy-done.3, bf16[128,512]{1,0:T(8,128)(2,1)S(1)} %copy-done.6), custom_call_target="tpu_custom_call" | custom-call | tf_op jit(solution)/shard_map/pallas_call | solution.py:292
  54.3 8.6 %shard_map.106 = (f32[128,512]{1,0:T(8,128)S(1)}, bf16[16,16,256]{2,1,0:T(8,128)(2,1)S(1)}) custom-call(s32[5]{0:T(128)S(1)} %stack.32.pos_ref, bf16[128,512]{1,0:T(8,128)(2,1)S(1)} %get-tuple-element.30.gm_ref, bf16[128,512]{1,0:T(8,128)(2,1)S(1)} %collective-permute-done.5.halo_ref, bf16[16,2,128,256]{3,2,1,0:T(8,128)(2,1)S(1)} %get-tuple-element.31.l_ref, ...), custom_call_target="tpu_custom_call" | custom-call | tf_op jit(solution)/shard_map/pallas_call | solution.py:292
  63.0 7.1 %shard_map.112 = bf16[16,32,256]{2,1,0:T(8,128)(2,1)} custom-call(s32[5]{0:T(128)S(1)} %stack.32.pos_ref, bf16[128,512]{1,0:T(8,128)(2,1)S(1)} %get-tuple-element.30.gm_ref, bf16[128,512]{1,0:T(8,128)(2,1)S(1)} %collective-permute-done.4.halo_ref, bf16[16,2,128,1024]{3,2,1,0:T(8,128)(2,1)S(1)} %get-tuple-element.32.u_ref, ...), custom_call_target="tpu_custom_call" | custom-call | tf_op jit(solution)/shard_map/pallas_call | solution.py:292
  70.1 8.9 %all-to-all-start = ((bf16[16,32,256]{2,1,0:T(8,128)(2,1)}), bf16[16,32,256]{2,1,0:T(8,128)(2,1)S(1)}, u32[]{:S(2)}, u32[]{:S(2)}) async-start(bf16[16,32,256]{2,1,0:T(8,128)(2,1)} %shard_map.112), calls=%async_computation | async-start | bytes 524288 | tf_op jit(solution)/shard_map/all_to_all | solution.py:388
  79.7 0.9 %copy-done.5 = bf16[2,64,1024]{2,1,0:T(8,128)(2,1)S(1)} copy-done((bf16[2,64,1024]{2,1,0:T(8,128)(2,1)S(1)}, bf16[2,64,1024]{2,1,0:T(8,128)(2,1)}, u32[]{:S(2)}) %copy-start.5) | copy-done | bytes 262168
  80.7 1.2 %shard_map.110 = (f32[64,1024]{1,0:T(8,128)S(1)}, bf16[64,1024]{1,0:T(8,128)(2,1)S(1)}) custom-call(bf16[2,64,1024]{2,1,0:T(8,128)(2,1)S(1)} %get-tuple-element.37.k, bf16[2,64,1024]{2,1,0:T(8,128)(2,1)S(1)} %copy-done.5, bf16[2,64,1024]{2,1,0:T(8,128)(2,1)} %collective-permute-done.13.r3, bf16[2,64,1024]{2,1,0:T(8,128)(2,1)} %collective-permute-done.14.r2), custom_call_target="tpu_custom_call" | custom-call | tf_op jit(solution)/shard_map/pallas_call | solution.py:292
  81.9 3.5 %collective-permute-start.15 = (bf16[64,1024]{1,0:T(8,128)(2,1)S(1)}, bf16[64,1024]{1,0:T(8,128)(2,1)S(1)}, u32[]{:S(2)}, u32[]{:S(2)}) collective-permute-start(bf16[64,1024]{1,0:T(8,128)(2,1)S(1)} %get-tuple-element.42), channel_id=1, source_target_pairs={{0,64},{8,72},{16,80},{24,88},{32,96},{40,104},{48,112},{56,120},{... | collective-permute-start | bytes 393224 | tf_op jit(solution)/shard_map/ppermute | solution.py:281
  85.4 6.4 %shard_map.107 = f32[128,512]{1,0:T(8,128)} custom-call(s32[5]{0:T(128)S(1)} %stack.32.pos_ref, bf16[128,512]{1,0:T(8,128)(2,1)S(1)} %get-tuple-element.30.gm_ref, bf16[128,512]{1,0:T(8,128)(2,1)S(1)} %collective-permute-done.4.halo_ref, bf16[16,2,128,256]{3,2,1,0:T(8,128)(2,1)S(1)} %get-tuple-element.31.l_ref, f32[128,512]{1,0:T(8,128)S(1)} %get-tuple-element.33.inner_ref), custom_call_target="tpu_custom_call" | custom-call | tf_op jit(solution)/shard_map/pallas_call | solution.py:292
  91.7 1.4 %shard_map.113 = f32[2,32,128]{2,1,0:T(8,128)} custom-call(s32[5]{0:T(128)S(1)} %stack.32.pos_ref, s32[16]{0:T(128)S(1)} %copy-done.7, bf16[16,32,256]{2,1,0:T(8,128)(2,1)S(1)} %all-to-all-done.got), custom_call_target="tpu_custom_call" | custom-call | tf_op jit(solution)/shard_map/pallas_call | solution.py:292
  (42 shorter events, 4.7 us)
Async XLA Ops:
  0.6 40.3 %collective-permute-start.11 = (bf16[512,1024]{1,0:T(8,128)(2,1)}, bf16[512,1024]{1,0:T(8,128)(2,1)S(1)}, u32[]{:S(2)}, u32[]{:S(2)}) collective-permute-start(bf16[512,1024]{1,0:T(8,128)(2,1)} %og_ref.1), channel_id=1, source_target_pairs={{0,8},{8,0},{16,24},{24,16},{32,40},{40,32},{48,56},{56,48},{64,72... | collective-permute-start | bytes 3145736 | tf_op jit(solution)/shard_map/ppermute | solution.py:281
  0.8 40.2 %copy-start = (bf16[512,1024]{1,0:T(8,128)(2,1)S(1)}, bf16[512,1024]{1,0:T(8,128)(2,1)}, u32[]{:S(2)}) copy-start(bf16[512,1024]{1,0:T(8,128)(2,1)} %og_ref.1) | copy-start | bytes 3145732
  4.7 22.3 %collective-permute-start = (bf16[512,512]{1,0:T(8,128)(2,1)S(1)}, bf16[512,512]{1,0:T(8,128)(2,1)S(1)}, u32[]{:S(2)}, u32[]{:S(2)}) collective-permute-start(bf16[512,512]{1,0:T(8,128)(2,1)S(1)} %get-tuple-element.25), channel_id=1, source_target_pairs={{0,1},{1,0},{2,3},{3,2},{4,5},{5,4},{6,7},{7,6},{8,9},{9,8},{10,11... | collective-permute-start | bytes 1572872 | tf_op jit(solution)/shard_map/ppermute | solution.py:281
  7.9 1.3 %collective-permute-start.6 = (bf16[64,512]{1,0:T(8,128)(2,1)S(1)}, bf16[64,512]{1,0:T(8,128)(2,1)S(1)}, u32[]{:S(2)}, u32[]{:S(2)}) collective-permute-start(bf16[64,512]{1,0:T(8,128)(2,1)S(1)} %get-tuple-element.36), channel_id=1, source_target_pairs={{0,8},{8,0},{16,24},{24,16},{32,40},{40,32},{48,56},{56,48},{64,72... | collective-permute-start | bytes 196616 | tf_op jit(solution)/shard_map/ppermute | solution.py:281
  9.3 12.6 %collective-permute-start.7 = (bf16[64,1024]{1,0:T(8,128)(2,1)S(1)}, bf16[64,1024]{1,0:T(8,128)(2,1)S(1)}, u32[]{:S(2)}, u32[]{:S(2)}) collective-permute-start(bf16[64,1024]{1,0:T(8,128)(2,1)S(1)} %constant_dynamic-update-slice_fusion), channel_id=1, source_target_pairs={{0,1},{1,0},{2,3},{3,2},{4,5},{5,4},{6,7},{7,6},{8,9},{9,8},{10,11... | collective-permute-start | bytes 393224 | tf_op jit(solution)/shard_map/ppermute | solution.py:281
  21.9 11.2 %collective-permute-start.10 = (bf16[2,64,1024]{2,1,0:T(8,128)(2,1)S(1)}, bf16[2,64,1024]{2,1,0:T(8,128)(2,1)S(1)}, u32[]{:S(2)}, u32[]{:S(2)}) collective-permute-start(bf16[2,64,1024]{2,1,0:T(8,128)(2,1)S(1)} %pad_maximum_fusion.b0), channel_id=1, source_target_pairs={{0,4},{1,5},{2,6},{3,7},{4,0},{5,1},{6,2},{7,3},{8,12},{9,13},{10,... | collective-permute-start | bytes 786440 | tf_op jit(solution)/shard_map/ppermute | solution.py:281
  26.0 13.8 %collective-permute-start.8 = (bf16[2,64,1024]{2,1,0:T(8,128)(2,1)S(1)}, bf16[2,64,1024]{2,1,0:T(8,128)(2,1)S(1)}, u32[]{:S(2)}, u32[]{:S(2)}) collective-permute-start(bf16[2,64,1024]{2,1,0:T(8,128)(2,1)S(1)} %pad_maximum_fusion.b0), channel_id=1, source_target_pairs={{0,2},{1,3},{2,0},{3,1},{4,6},{5,7},{6,4},{7,5},{8,10},{9,11},{10,... | collective-permute-start | bytes 786440 | tf_op jit(solution)/shard_map/ppermute | solution.py:281
  27.0 14.0 %collective-permute-start.9 = (bf16[2,64,1024]{2,1,0:T(8,128)(2,1)S(1)}, bf16[2,64,1024]{2,1,0:T(8,128)(2,1)S(1)}, u32[]{:S(2)}, u32[]{:S(2)}) collective-permute-start(bf16[2,64,1024]{2,1,0:T(8,128)(2,1)S(1)} %pad_maximum_fusion.b0), channel_id=1, source_target_pairs={{0,6},{1,7},{2,4},{3,5},{4,2},{5,3},{6,0},{7,1},{8,14},{9,15},{10,... | collective-permute-start | bytes 786440 | tf_op jit(solution)/shard_map/ppermute | solution.py:281
  27.0 22.8 %copy-start.1 = (bf16[128,512]{1,0:T(8,128)(2,1)S(1)}, bf16[128,512]{1,0:T(8,128)(2,1)}, u32[]{:S(2)}) copy-start(bf16[128,512]{1,0:T(8,128)(2,1)} %v_hbm.1) | copy-start | bytes 393220
  27.0 22.8 %copy-start.2 = (bf16[128,512]{1,0:T(8,128)(2,1)S(1)}, bf16[128,512]{1,0:T(8,128)(2,1)}, u32[]{:S(2)}) copy-start(bf16[128,512]{1,0:T(8,128)(2,1)} %g_hbm.1) | copy-start | bytes 393220
  27.2 24.1 %copy-start.3 = (bf16[2,128,512]{2,1,0:T(8,128)(2,1)S(1)}, bf16[2,128,512]{2,1,0:T(8,128)(2,1)}, u32[]{:S(2)}) copy-start(bf16[2,128,512]{2,1,0:T(8,128)(2,1)} %f_ref.1) | copy-start | bytes 786436
  27.2 24.1 %copy-start.6 = (bf16[128,512]{1,0:T(8,128)(2,1)S(1)}, bf16[128,512]{1,0:T(8,128)(2,1)}, u32[]{:S(2)}) copy-start(bf16[128,512]{1,0:T(8,128)(2,1)} %x_ref.1) | copy-start | bytes 393220
  27.2 24.1 %copy-start.7 = (s32[16]{0:T(128)S(1)}, s32[16]{0:T(128)}, u32[]{:S(2)}) copy-start(s32[16]{0:T(128)} %reach_ref.3) | copy-start | bytes 196
  27.2 21.9 %collective-permute-start.1 = (bf16[128,512]{1,0:T(8,128)(2,1)S(1)}, bf16[128,512]{1,0:T(8,128)(2,1)S(1)}, u32[]{:S(2)}, u32[]{:S(2)}) collective-permute-start(bf16[128,512]{1,0:T(8,128)(2,1)S(1)} %get-tuple-element.27), channel_id=1, source_target_pairs={{0,2},{1,3},{2,0},{3,1},{4,6},{5,7},{6,4},{7,5},{8,10},{9,11},{10,... | collective-permute-start | bytes 393224 | tf_op jit(solution)/shard_map/ppermute | solution.py:281
  33.1 16.7 %collective-permute-start.2 = (bf16[128,512]{1,0:T(8,128)(2,1)S(1)}, bf16[128,512]{1,0:T(8,128)(2,1)S(1)}, u32[]{:S(2)}, u32[]{:S(2)}) collective-permute-start(bf16[128,512]{1,0:T(8,128)(2,1)S(1)} %get-tuple-element.28), channel_id=1, source_target_pairs={{0,6},{1,7},{2,4},{3,5},{4,2},{5,3},{6,0},{7,1},{8,14},{9,15},{10,... | collective-permute-start | bytes 393224 | tf_op jit(solution)/shard_map/ppermute | solution.py:281
  39.8 10.0 %collective-permute-start.3 = (bf16[128,512]{1,0:T(8,128)(2,1)S(1)}, bf16[128,512]{1,0:T(8,128)(2,1)S(1)}, u32[]{:S(2)}, u32[]{:S(2)}) collective-permute-start(bf16[128,512]{1,0:T(8,128)(2,1)S(1)} %get-tuple-element.29), channel_id=1, source_target_pairs={{0,4},{1,5},{2,6},{3,7},{4,0},{5,1},{6,2},{7,3},{8,12},{9,13},{10,... | collective-permute-start | bytes 393224 | tf_op jit(solution)/shard_map/ppermute | solution.py:281
  45.3 33.7 %collective-permute-start.12 = (bf16[2,64,1024]{2,1,0:T(8,128)(2,1)}, bf16[2,64,1024]{2,1,0:T(8,128)(2,1)S(1)}, u32[]{:S(2)}, u32[]{:S(2)}) collective-permute-start(bf16[2,64,1024]{2,1,0:T(8,128)(2,1)} %get-tuple-element.38), channel_id=1, source_target_pairs={{0,16},{8,24},{16,0},{24,8},{32,48},{40,56},{48,32},{56,40},{64,80... | collective-permute-start | bytes 786440 | tf_op jit(solution)/shard_map/ppermute | solution.py:281
  46.9 32.8 %collective-permute-start.13 = (bf16[2,64,1024]{2,1,0:T(8,128)(2,1)}, bf16[2,64,1024]{2,1,0:T(8,128)(2,1)}, u32[]{:S(2)}, u32[]{:S(2)}) collective-permute-start(bf16[2,64,1024]{2,1,0:T(8,128)(2,1)} %get-tuple-element.39), channel_id=1, source_target_pairs={{0,48},{8,56},{16,32},{24,40},{32,16},{40,24},{48,0},{56,8},{64,11... | collective-permute-start | bytes 786440 | tf_op jit(solution)/shard_map/ppermute | solution.py:281
  49.1 30.7 %collective-permute-start.14 = (bf16[2,64,1024]{2,1,0:T(8,128)(2,1)}, bf16[2,64,1024]{2,1,0:T(8,128)(2,1)}, u32[]{:S(2)}, u32[]{:S(2)}) collective-permute-start(bf16[2,64,1024]{2,1,0:T(8,128)(2,1)} %get-tuple-element.40), channel_id=1, source_target_pairs={{0,32},{8,40},{16,48},{24,56},{32,0},{40,8},{48,16},{56,24},{64,96... | collective-permute-start | bytes 786440 | tf_op jit(solution)/shard_map/ppermute | solution.py:281
  50.6 3.7 %collective-permute-start.5 = (bf16[128,512]{1,0:T(8,128)(2,1)S(1)}, bf16[128,512]{1,0:T(8,128)(2,1)S(1)}, u32[]{:S(2)}, u32[]{:S(2)}) collective-permute-start(bf16[128,512]{1,0:T(8,128)(2,1)S(1)} %get-tuple-element.30.gm_ref), channel_id=1, source_target_pairs={{0,8},{8,0},{16,24},{24,16},{32,40},{40,32},{48,56},{56,48},{64,72... | collective-permute-start | bytes 393224 | tf_op jit(solution)/shard_map/ppermute | solution.py:281
  50.6 12.4 %collective-permute-start.4 = (bf16[128,512]{1,0:T(8,128)(2,1)S(1)}, bf16[128,512]{1,0:T(8,128)(2,1)S(1)}, u32[]{:S(2)}, u32[]{:S(2)}) collective-permute-start(bf16[128,512]{1,0:T(8,128)(2,1)S(1)} %get-tuple-element.30.gm_ref), channel_id=1, source_target_pairs={{8,16},{24,32},{40,48},{56,64},{72,80},{88,96},{104,112},{16,8},{3... | collective-permute-start | bytes 393224 | tf_op jit(solution)/shard_map/ppermute | solution.py:354
  70.1 21.6 %all-to-all-start = ((bf16[16,32,256]{2,1,0:T(8,128)(2,1)}), bf16[16,32,256]{2,1,0:T(8,128)(2,1)S(1)}, u32[]{:S(2)}, u32[]{:S(2)}) async-start(bf16[16,32,256]{2,1,0:T(8,128)(2,1)} %shard_map.112), calls=%async_computation | async-start | bytes 524288 | tf_op jit(solution)/shard_map/all_to_all | solution.py:388
  79.7 1.0 %copy-start.5 = (bf16[2,64,1024]{2,1,0:T(8,128)(2,1)S(1)}, bf16[2,64,1024]{2,1,0:T(8,128)(2,1)}, u32[]{:S(2)}) copy-start(bf16[2,64,1024]{2,1,0:T(8,128)(2,1)} %copy-done.4) | copy-start | bytes 786436
  81.9 11.3 %collective-permute-start.15 = (bf16[64,1024]{1,0:T(8,128)(2,1)S(1)}, bf16[64,1024]{1,0:T(8,128)(2,1)S(1)}, u32[]{:S(2)}, u32[]{:S(2)}) collective-permute-start(bf16[64,1024]{1,0:T(8,128)(2,1)S(1)} %get-tuple-element.42), channel_id=1, source_target_pairs={{0,64},{8,72},{16,80},{24,88},{32,96},{40,104},{48,112},{56,120},{... | collective-permute-start | bytes 393224 | tf_op jit(solution)/shard_map/ppermute | solution.py:281
  (1 other events, 0.7 us)

commit v6 on v2

--- a/solution.py
+++ b/solution.py
@@ -145,12 +145,11 @@
 
 
 def conv_grads(pos_ref, gm_ref, gs_ref, gp_ref, l_ref, ui_ref, uo_ref,
-               o_ref, keep_ref, send_ref, h_ref, t_ref):
+               o_ref, t_ref, h_ref, acc_ref):
     rows, n = gm_ref.shape
     width = 3 * n
     lanes = n // 128
-    place = pos_ref[4]
-    core0 = (place & 1) == 0
+    core0 = (pos_ref[4] & 1) == 0
     own_cols = iota((16, 8, 256), 1) == (iota((16, 8, 256), 2) & 7)
 
     def step(i, carry):
@@ -202,21 +201,12 @@
                 sums = jnp.sum(jnp.where(own_cols, cross.reshape(16, 8, 256), 0.0), axis=1)
                 row = d * (rows // 8) + group
                 for u in range(16):
-                    r = u ^ place
-                    slot = (r & 1) * 8 + ((r >> 1) & 3) * 2 + (r >> 3)
-                    t_ref[slot, pl.ds(row, 1), :] = sums[u : u + 1]
+                    acc_ref[u, pl.ds(row, 1), :] = sums[u : u + 1]
         o_ref[band, :] = jnp.concatenate(outs, axis=0)
         return carry
 
     lax.fori_loop(0, rows // 16, step, 0)
-    keep_ref[...] = t_ref[0:8]
-    send_ref[...] = t_ref[8:16].astype(BF16)
-
-
-def split_taps(t_ref, got_ref, k, s1, s3, s2):
-    for rel, ref in ((0, k), (1, s1), (3, s3), (2, s2)):
-        both = t_ref[2 * rel : 2 * rel + 2] + got_ref[2 * rel : 2 * rel + 2].astype(F32)
-        ref[...] = both.astype(ref.dtype)
+    t_ref[...] = acc_ref[...].astype(BF16)
 
 
 def sum_pieces(k, r1, r3, r2, keep, send):
@@ -231,8 +221,10 @@
     o_ref[...] = (keep[...] + got[...].astype(F32)) * scale
 
 
-def finish_taps(pos_ref, reach_ref, part_ref, got, t_ref, *, scale):
-    f = part_ref[...] + got[...].astype(F32)
+def finish_taps(pos_ref, reach_ref, got, t_ref, *, scale):
+    f = got[0].astype(F32)
+    for i in range(1, got.shape[0]):
+        f = f + got[i].astype(F32)
     chan = pos_ref[0] * 2 + pos_ref[1]
     place = pos_ref[4]
     own_cols = iota((16, 8, 256), 1) == (iota((16, 8, 256), 2) & 7)
@@ -345,32 +337,20 @@
         (pos, filter_reach, filters, conv_input),
         scalars=2,
     )
-    grad_input, tap_keep, tap_send = call(
+    grad_input, tap_sums = call(
         conv_grads,
-        [
-            shape((rows, tok), F32),
-            shape((8, rows // 4, 256), F32),
-            shape((8, rows // 4, 256), BF16),
-        ],
+        [shape((rows, tok), F32), shape((seq_count, rows // 4, 256), BF16)],
         (pos, grad_conv, halo_core, halo_out, *prepared),
         scratch=[
             pltpu.VMEM((2, 256, 3 * tok), BF16),
-            pltpu.VMEM((16, rows // 4, 256), F32),
+            pltpu.VMEM((seq_count, rows // 4, 256), F32),
         ],
     )
-    f_got = swap(tap_send, "seq", 1)
-    piece = (2, rows // 4, 256)
-    f = call(
-        split_taps, [shape(piece, F32)] + [shape(piece, BF16)] * 3,
-        (tap_keep, f_got), scalars=0,
-    )
-    f = [f[0], swap(f[1], "seq", 2), swap(f[2], "seq", 6), swap(f[3], "seq", 4)]
+    tap_sums = lax.all_to_all(tap_sums, "seq", 0, 0)
     e_keep, e_send = call(
         sum_pieces, [shape((half, feats), F32), shape((half, feats), BF16)], e, scalars=0
     )
     e_got = swap(e_send, "seq", 8)
-    f_keep, f_send = call(sum_pieces, [shape(piece[1:], F32), shape(piece[1:], BF16)], f, scalars=0)
-    f_got = swap(f_send, "seq", 8)
     grad_weight = call(
         functools.partial(finish_rows, scale=scale),
         shape((half, feats), F32),
@@ -380,7 +360,7 @@
     grad_filters = call(
         functools.partial(finish_taps, scale=scale),
         shape((2, VN, rows), F32),
-        (pos, filter_reach, f_keep, f_got),
+        (pos, filter_reach, tap_sums),
         scalars=2,
     )
     return (grad_input, grad_gate, grad_weight, jnp.transpose(grad_filters, (0, 2, 1)))

time: 89.8 us -> 90.7 us (1.010)
  starting transfers between devices: 34.6 us -> 36.7 us
  waiting for transfers between devices: 27.3 us -> 25.8 us
    all_to_all x0 -> x1, starting transfers between devices: none -> 11.6 us  [on_device_0(): tap_sums = lax.all_to_all(tap_sums, 'seq', 0, 0)]
    ppermute x20 -> x15, starting transfers between devices: 33.9 us -> 24.5 us  [swap(): lax.ppermute(v, axis, [(i, i ^ mask) for i in range(lax.axis_size(axis))])]
    ppermute x20 -> x15, waiting for transfers between devices: 27.3 us -> 19.4 us  [swap(): lax.ppermute(v, axis, [(i, i ^ mask) for i in range(lax.axis_size(axis))])]
    all_to_all x0 -> x1, waiting for transfers between devices: none -> 6.42 us  [on_device_0(): tap_sums = lax.all_to_all(tap_sums, 'seq', 0, 0)]
    pallas_call x12 -> x10, Pallas kernels: 26.8 us -> 26.9 us  [call(): pl.pallas_call(body, out_shape=out_shape, in_specs=[smem()] * scalars + [...]
  transfers between devices with their start and end apart: 21 -> 17, of which waited for: 7 -> 5; matrix products, arithmetic and copies ran while one was open for 0% -> 0% of each run, Pallas kernels for 29% -> 29%
where the time goes in v6:
time: 90.7 us; the launch traced here: 90.4 us
  starting transfers between devices  36.7 us (40%)
  Pallas kernels  26.9 us (30%)
  waiting for transfers between devices  25.8 us (28%)
    pallas_call x10, Pallas kernels, call(): pl.pallas_call(body, out_shape=out_shape, in_specs=[smem()] * scalars + [...  26.9 us
    ppermute x15, starting transfers between devices, swap(): lax.ppermute(v, axis, [(i, i ^ mask) for i in range(lax.axis_size(axis))])  24.5 us
    ppermute x15, waiting for transfers between devices, swap(): lax.ppermute(v, axis, [(i, i ^ mask) for i in range(lax.axis_size(axis))])  19.4 us
    all_to_all x1, starting transfers between devices, on_device_0(): tap_sums = lax.all_to_all(tap_sums, 'seq', 0, 0)  11.6 us
    all_to_all x1, waiting for transfers between devices, on_device_0(): tap_sums = lax.all_to_all(tap_sums, 'seq', 0, 0)  6.42 us
  transfers between devices with their start and end apart: 17, of which 5 were waited for; matrix products, arithmetic and copies ran while one was open for 0% of the time, Pallas kernels for 29%

profile of v6, /device:TPU:0, one launch (start us, length us, event | category | flops | bytes accessed | tf_op | source)
XLA Modules:
  0.0 90.4 jit_solution(13948999885691492882)
XLA Ops:
  0.9 3.9 %shard_map.102 = (bf16[512,512]{1,0:T(8,128)(2,1)S(1)}, bf16[512,512]{1,0:T(8,128)(2,1)S(1)}) custom-call(s32[5]{0:T(128)S(1)} %stack.32.pos_ref, bf16[1024,1024]{1,0:T(8,128)(2,1)} %w_hbm.1, bf16[512,1024]{1,0:T(8,128)(2,1)} %og_ref.1), custom_call_target="tpu_custom_call" | custom-call | tf_op jit(solution)/shard_map/pallas_call | solution.py:257
  4.7 1.7 %collective-permute-start = (bf16[512,512]{1,0:T(8,128)(2,1)S(1)}, bf16[512,512]{1,0:T(8,128)(2,1)S(1)}, u32[]{:S(2)}, u32[]{:S(2)}) collective-permute-start(bf16[512,512]{1,0:T(8,128)(2,1)S(1)} %get-tuple-element.26), channel_id=1, source_target_pairs={{0,1},{1,0},{2,3},{3,2},{4,5},{5,4},{6,7},{7,6},{8,9},{9,8},{10,11... | collective-permute-start | bytes 1572872 | tf_op jit(solution)/shard_map/ppermute | solution.py:246
  6.4 1.6 %shard_map.107 = (bf16[64,512]{1,0:T(8,128)(2,1)S(1)}, bf16[64,512]{1,0:T(8,128)(2,1)S(1)}) custom-call(s32[5]{0:T(128)S(1)} %stack.32.pos_ref, bf16[128,512]{1,0:T(8,128)(2,1)} %v_hbm.1, bf16[128,512]{1,0:T(8,128)(2,1)} %g_hbm.1), custom_call_target="tpu_custom_call" | custom-call | tf_op jit(solution)/shard_map/pallas_call | solution.py:257
  8.3 1.0 %collective-permute-done.6 = bf16[64,512]{1,0:T(8,128)(2,1)S(1)} collective-permute-done((bf16[64,512]{1,0:T(8,128)(2,1)S(1)}, bf16[64,512]{1,0:T(8,128)(2,1)S(1)}, u32[]{:S(2)}, u32[]{:S(2)}) %collective-permute-start.6) | collective-permute-done | bytes 65568 | tf_op jit(solution)/shard_map/ppermute | solution.py:246
  9.8 12.2 %collective-permute-done.7 = bf16[64,1024]{1,0:T(8,128)(2,1)S(1)} collective-permute-done((bf16[64,1024]{1,0:T(8,128)(2,1)S(1)}, bf16[64,1024]{1,0:T(8,128)(2,1)S(1)}, u32[]{:S(2)}, u32[]{:S(2)}) %collective-permute-start.7) | collective-permute-done | bytes 131104 | tf_op jit(solution)/shard_map/ppermute | solution.py:246
  22.0 2.1 %collective-permute-start.8 = (bf16[2,64,1024]{2,1,0:T(8,128)(2,1)S(1)}, bf16[2,64,1024]{2,1,0:T(8,128)(2,1)S(1)}, u32[]{:S(2)}, u32[]{:S(2)}) collective-permute-start(bf16[2,64,1024]{2,1,0:T(8,128)(2,1)S(1)} %pad_maximum_fusion.b0), channel_id=1, source_target_pairs={{0,2},{1,3},{2,0},{3,1},{4,6},{5,7},{6,4},{7,5},{8,10},{9,11},{10,... | collective-permute-start | bytes 786440 | tf_op jit(solution)/shard_map/ppermute | solution.py:246
  24.1 2.5 %collective-permute-start.9 = (bf16[2,64,1024]{2,1,0:T(8,128)(2,1)S(1)}, bf16[2,64,1024]{2,1,0:T(8,128)(2,1)S(1)}, u32[]{:S(2)}, u32[]{:S(2)}) collective-permute-start(bf16[2,64,1024]{2,1,0:T(8,128)(2,1)S(1)} %pad_maximum_fusion.b0), channel_id=1, source_target_pairs={{0,6},{1,7},{2,4},{3,5},{4,2},{5,3},{6,0},{7,1},{8,14},{9,15},{10,... | collective-permute-start | bytes 786440 | tf_op jit(solution)/shard_map/ppermute | solution.py:246
  26.6 1.1 %collective-permute-start.10 = (bf16[2,64,1024]{2,1,0:T(8,128)(2,1)S(1)}, bf16[2,64,1024]{2,1,0:T(8,128)(2,1)S(1)}, u32[]{:S(2)}, u32[]{:S(2)}) collective-permute-start(bf16[2,64,1024]{2,1,0:T(8,128)(2,1)S(1)} %pad_maximum_fusion.b0), channel_id=1, source_target_pairs={{0,4},{1,5},{2,6},{3,7},{4,0},{5,1},{6,2},{7,3},{8,12},{9,13},{10,... | collective-permute-start | bytes 786440 | tf_op jit(solution)/shard_map/ppermute | solution.py:246
  28.4 2.9 %collective-permute-done.8.b1 = bf16[2,64,1024]{2,1,0:T(8,128)(2,1)S(1)} collective-permute-done((bf16[2,64,1024]{2,1,0:T(8,128)(2,1)S(1)}, bf16[2,64,1024]{2,1,0:T(8,128)(2,1)S(1)}, u32[]{:S(2)}, u32[]{:S(2)}) %collective-permute-start.8) | collective-permute-done | bytes 262176 | tf_op jit(solution)/shard_map/ppermute | solution.py:246
  31.2 4.1 %collective-permute-start.2 = (bf16[128,512]{1,0:T(8,128)(2,1)S(1)}, bf16[128,512]{1,0:T(8,128)(2,1)S(1)}, u32[]{:S(2)}, u32[]{:S(2)}) collective-permute-start(bf16[128,512]{1,0:T(8,128)(2,1)S(1)} %get-tuple-element.29), channel_id=1, source_target_pairs={{0,6},{1,7},{2,4},{3,5},{4,2},{5,3},{6,0},{7,1},{8,14},{9,15},{10,... | collective-permute-start | bytes 393224 | tf_op jit(solution)/shard_map/ppermute | solution.py:246
  35.4 3.3 %collective-permute-done.9.b3 = bf16[2,64,1024]{2,1,0:T(8,128)(2,1)S(1)} collective-permute-done((bf16[2,64,1024]{2,1,0:T(8,128)(2,1)S(1)}, bf16[2,64,1024]{2,1,0:T(8,128)(2,1)S(1)}, u32[]{:S(2)}, u32[]{:S(2)}) %collective-permute-start.9) | collective-permute-done | bytes 262176 | tf_op jit(solution)/shard_map/ppermute | solution.py:246
  38.7 3.6 %collective-permute-start.3 = (bf16[128,512]{1,0:T(8,128)(2,1)S(1)}, bf16[128,512]{1,0:T(8,128)(2,1)S(1)}, u32[]{:S(2)}, u32[]{:S(2)}) collective-permute-start(bf16[128,512]{1,0:T(8,128)(2,1)S(1)} %get-tuple-element.30), channel_id=1, source_target_pairs={{0,4},{1,5},{2,6},{3,7},{4,0},{5,1},{6,2},{7,3},{8,12},{9,13},{10,... | collective-permute-start | bytes 393224 | tf_op jit(solution)/shard_map/ppermute | solution.py:246
  42.3 3.6 %shard_map.108 = (bf16[2,64,1024]{2,1,0:T(8,128)(2,1)S(1)}, bf16[2,64,1024]{2,1,0:T(8,128)(2,1)S(1)}, bf16[2,64,1024]{2,1,0:T(8,128)(2,1)S(1)}, bf16[2,64,1024]{2,1,0:T(8,128)(2,1)S(1)}) custom-call(s32[5]{0:T(128)S(1)} %stack.32.pos_ref, bf16[2,64,1024]{2,1,0:T(8,128)(2,1)S(1)} %pad_maximum_fusion.b0, bf16[2,64,1024]{2,1,0:T(8,128)(2,1)S(1)} %collective-permute-done.8.b1, ...), custom_call_target="tpu_custom_call" | custom-call | tf_op jit(solution)/shard_map/pallas_call | solution.py:257
  45.9 1.6 %collective-permute-start.12 = (bf16[2,64,1024]{2,1,0:T(8,128)(2,1)S(1)}, bf16[2,64,1024]{2,1,0:T(8,128)(2,1)S(1)}, u32[]{:S(2)}, u32[]{:S(2)}) collective-permute-start(bf16[2,64,1024]{2,1,0:T(8,128)(2,1)S(1)} %get-tuple-element.40), channel_id=1, source_target_pairs={{0,16},{8,24},{16,0},{24,8},{32,48},{40,56},{48,32},{56,40},{64,80... | collective-permute-start | bytes 786440 | tf_op jit(solution)/shard_map/ppermute | solution.py:246
  47.5 2.2 %collective-permute-start.13 = (bf16[2,64,1024]{2,1,0:T(8,128)(2,1)S(1)}, bf16[2,64,1024]{2,1,0:T(8,128)(2,1)S(1)}, u32[]{:S(2)}, u32[]{:S(2)}) collective-permute-start(bf16[2,64,1024]{2,1,0:T(8,128)(2,1)S(1)} %get-tuple-element.41), channel_id=1, source_target_pairs={{0,48},{8,56},{16,32},{24,40},{32,16},{40,24},{48,0},{56,8},{64,11... | collective-permute-start | bytes 786440 | tf_op jit(solution)/shard_map/ppermute | solution.py:246
  49.7 0.7 collective-permute-start.14
  50.5 0.8 shard_map.104
  51.9 3.0 %shard_map.105 = (bf16[16,2,128,256]{3,2,1,0:T(8,128)(2,1)S(1)}, bf16[16,256,512]{2,1,0:T(8,128)(2,1)S(1)}, bf16[16,256,512]{2,1,0:T(8,128)(2,1)S(1)}) custom-call(s32[5]{0:T(128)S(1)} %stack.32.pos_ref, s32[16]{0:T(128)S(1)} %copy-done.5, bf16[2,128,512]{2,1,0:T(8,128)(2,1)S(1)} %copy-done.3, bf16[128,512]{1,0:T(8,128)(2,1)S(1)} %copy-done.4), custom_call_target="tpu_custom_call" | custom-call | tf_op jit(solution)/shard_map/pallas_call | solution.py:257
  55.0 11.6 %shard_map.106 = (f32[128,512]{1,0:T(8,128)}, bf16[16,32,256]{2,1,0:T(8,128)(2,1)}) custom-call(s32[5]{0:T(128)S(1)} %stack.32.pos_ref, bf16[128,512]{1,0:T(8,128)(2,1)S(1)} %get-tuple-element.31.gm_ref, bf16[128,512]{1,0:T(8,128)(2,1)S(1)} %collective-permute-done.4.gs_ref, bf16[128,512]{1,0:T(8,128)(2,1)S(1)} %collective-permute-done.5.gp_ref, ...), custom_call_target="tpu_custom_call" | custom-call | tf_op jit(solution)/shard_map/pallas_call | solution.py:257
  66.6 11.6 %all-to-all-start = ((bf16[16,32,256]{2,1,0:T(8,128)(2,1)}), bf16[16,32,256]{2,1,0:T(8,128)(2,1)S(1)}, u32[]{:S(2)}, u32[]{:S(2)}) async-start(bf16[16,32,256]{2,1,0:T(8,128)(2,1)} %get-tuple-element.45), calls=%async_computation | async-start | bytes 524288 | tf_op jit(solution)/shard_map/all_to_all | solution.py:349
  78.4 3.5 %collective-permute-start.15 = (bf16[64,1024]{1,0:T(8,128)(2,1)S(1)}, bf16[64,1024]{1,0:T(8,128)(2,1)S(1)}, u32[]{:S(2)}, u32[]{:S(2)}) collective-permute-start(bf16[64,1024]{1,0:T(8,128)(2,1)S(1)} %get-tuple-element.44), channel_id=1, source_target_pairs={{0,64},{8,72},{16,80},{24,88},{32,96},{40,104},{48,112},{56,120},{... | collective-permute-start | bytes 393224 | tf_op jit(solution)/shard_map/ppermute | solution.py:246
  81.9 6.4 %all-to-all-done.got = bf16[16,32,256]{2,1,0:T(8,128)(2,1)S(1)} async-done(((bf16[16,32,256]{2,1,0:T(8,128)(2,1)}), bf16[16,32,256]{2,1,0:T(8,128)(2,1)S(1)}, u32[]{:S(2)}, u32[]{:S(2)}) %all-to-all-start) | async-done | bytes 262176 | tf_op jit(solution)/shard_map/all_to_all | solution.py:349
  88.3 1.4 %shard_map.111 = f32[2,32,128]{2,1,0:T(8,128)} custom-call(s32[5]{0:T(128)S(1)} %stack.32.pos_ref, s32[16]{0:T(128)S(1)} %copy-done.5, bf16[16,32,256]{2,1,0:T(8,128)(2,1)S(1)} %all-to-all-done.got), custom_call_target="tpu_custom_call" | custom-call | tf_op jit(solution)/shard_map/pallas_call | solution.py:257
  89.7 0.7 shard_map.110
  (36 shorter events, 2.5 us)
Async XLA Ops:
  0.6 41.6 %copy-start = (bf16[512,1024]{1,0:T(8,128)(2,1)S(1)}, bf16[512,1024]{1,0:T(8,128)(2,1)}, u32[]{:S(2)}) copy-start(bf16[512,1024]{1,0:T(8,128)(2,1)} %og_ref.1) | copy-start | bytes 3145732
  0.6 41.6 %collective-permute-start.11 = (bf16[512,1024]{1,0:T(8,128)(2,1)}, bf16[512,1024]{1,0:T(8,128)(2,1)S(1)}, u32[]{:S(2)}, u32[]{:S(2)}) collective-permute-start(bf16[512,1024]{1,0:T(8,128)(2,1)} %og_ref.1), channel_id=1, source_target_pairs={{0,8},{8,0},{16,24},{24,16},{32,40},{40,32},{48,56},{56,48},{64,72... | collective-permute-start | bytes 3145736 | tf_op jit(solution)/shard_map/ppermute | solution.py:246
  0.8 49.6 %copy-start.1 = (bf16[128,512]{1,0:T(8,128)(2,1)S(1)}, bf16[128,512]{1,0:T(8,128)(2,1)}, u32[]{:S(2)}) copy-start(bf16[128,512]{1,0:T(8,128)(2,1)} %v_hbm.1) | copy-start | bytes 393220
  0.8 49.6 %copy-start.2 = (bf16[128,512]{1,0:T(8,128)(2,1)S(1)}, bf16[128,512]{1,0:T(8,128)(2,1)}, u32[]{:S(2)}) copy-start(bf16[128,512]{1,0:T(8,128)(2,1)} %g_hbm.1) | copy-start | bytes 393220
  0.8 51.1 %copy-start.3 = (bf16[2,128,512]{2,1,0:T(8,128)(2,1)S(1)}, bf16[2,128,512]{2,1,0:T(8,128)(2,1)}, u32[]{:S(2)}) copy-start(bf16[2,128,512]{2,1,0:T(8,128)(2,1)} %f_ref.1) | copy-start | bytes 786436
  0.8 51.1 %copy-start.4 = (bf16[128,512]{1,0:T(8,128)(2,1)S(1)}, bf16[128,512]{1,0:T(8,128)(2,1)}, u32[]{:S(2)}) copy-start(bf16[128,512]{1,0:T(8,128)(2,1)} %x_ref.1) | copy-start | bytes 393220
  0.8 51.1 %copy-start.5 = (s32[16]{0:T(128)S(1)}, s32[16]{0:T(128)}, u32[]{:S(2)}) copy-start(s32[16]{0:T(128)} %reach_ref.3) | copy-start | bytes 196
  4.7 22.9 %collective-permute-start = (bf16[512,512]{1,0:T(8,128)(2,1)S(1)}, bf16[512,512]{1,0:T(8,128)(2,1)S(1)}, u32[]{:S(2)}, u32[]{:S(2)}) collective-permute-start(bf16[512,512]{1,0:T(8,128)(2,1)S(1)} %get-tuple-element.26), channel_id=1, source_target_pairs={{0,1},{1,0},{2,3},{3,2},{4,5},{5,4},{6,7},{7,6},{8,9},{9,8},{10,11... | collective-permute-start | bytes 1572872 | tf_op jit(solution)/shard_map/ppermute | solution.py:246
  8.0 1.3 %collective-permute-start.6 = (bf16[64,512]{1,0:T(8,128)(2,1)S(1)}, bf16[64,512]{1,0:T(8,128)(2,1)S(1)}, u32[]{:S(2)}, u32[]{:S(2)}) collective-permute-start(bf16[64,512]{1,0:T(8,128)(2,1)S(1)} %get-tuple-element.38), channel_id=1, source_target_pairs={{0,8},{8,0},{16,24},{24,16},{32,40},{40,32},{48,56},{56,48},{64,72... | collective-permute-start | bytes 196616 | tf_op jit(solution)/shard_map/ppermute | solution.py:246
  9.3 12.6 %collective-permute-start.7 = (bf16[64,1024]{1,0:T(8,128)(2,1)S(1)}, bf16[64,1024]{1,0:T(8,128)(2,1)S(1)}, u32[]{:S(2)}, u32[]{:S(2)}) collective-permute-start(bf16[64,1024]{1,0:T(8,128)(2,1)S(1)} %constant_dynamic-update-slice_fusion), channel_id=1, source_target_pairs={{0,1},{1,0},{2,3},{3,2},{4,5},{5,4},{6,7},{7,6},{8,9},{9,8},{10,11... | collective-permute-start | bytes 393224 | tf_op jit(solution)/shard_map/ppermute | solution.py:246
  22.0 9.3 %collective-permute-start.8 = (bf16[2,64,1024]{2,1,0:T(8,128)(2,1)S(1)}, bf16[2,64,1024]{2,1,0:T(8,128)(2,1)S(1)}, u32[]{:S(2)}, u32[]{:S(2)}) collective-permute-start(bf16[2,64,1024]{2,1,0:T(8,128)(2,1)S(1)} %pad_maximum_fusion.b0), channel_id=1, source_target_pairs={{0,2},{1,3},{2,0},{3,1},{4,6},{5,7},{6,4},{7,5},{8,10},{9,11},{10,... | collective-permute-start | bytes 786440 | tf_op jit(solution)/shard_map/ppermute | solution.py:246
  24.1 14.6 %collective-permute-start.9 = (bf16[2,64,1024]{2,1,0:T(8,128)(2,1)S(1)}, bf16[2,64,1024]{2,1,0:T(8,128)(2,1)S(1)}, u32[]{:S(2)}, u32[]{:S(2)}) collective-permute-start(bf16[2,64,1024]{2,1,0:T(8,128)(2,1)S(1)} %pad_maximum_fusion.b0), channel_id=1, source_target_pairs={{0,6},{1,7},{2,4},{3,5},{4,2},{5,3},{6,0},{7,1},{8,14},{9,15},{10,... | collective-permute-start | bytes 786440 | tf_op jit(solution)/shard_map/ppermute | solution.py:246
  26.6 15.7 %collective-permute-start.10 = (bf16[2,64,1024]{2,1,0:T(8,128)(2,1)S(1)}, bf16[2,64,1024]{2,1,0:T(8,128)(2,1)S(1)}, u32[]{:S(2)}, u32[]{:S(2)}) collective-permute-start(bf16[2,64,1024]{2,1,0:T(8,128)(2,1)S(1)} %pad_maximum_fusion.b0), channel_id=1, source_target_pairs={{0,4},{1,5},{2,6},{3,7},{4,0},{5,1},{6,2},{7,3},{8,12},{9,13},{10,... | collective-permute-start | bytes 786440 | tf_op jit(solution)/shard_map/ppermute | solution.py:246
  27.8 21.9 %collective-permute-start.1 = (bf16[128,512]{1,0:T(8,128)(2,1)S(1)}, bf16[128,512]{1,0:T(8,128)(2,1)S(1)}, u32[]{:S(2)}, u32[]{:S(2)}) collective-permute-start(bf16[128,512]{1,0:T(8,128)(2,1)S(1)} %get-tuple-element.28), channel_id=1, source_target_pairs={{0,2},{1,3},{2,0},{3,1},{4,6},{5,7},{6,4},{7,5},{8,10},{9,11},{10,... | collective-permute-start | bytes 393224 | tf_op jit(solution)/shard_map/ppermute | solution.py:246
  31.2 19.2 %collective-permute-start.2 = (bf16[128,512]{1,0:T(8,128)(2,1)S(1)}, bf16[128,512]{1,0:T(8,128)(2,1)S(1)}, u32[]{:S(2)}, u32[]{:S(2)}) collective-permute-start(bf16[128,512]{1,0:T(8,128)(2,1)S(1)} %get-tuple-element.29), channel_id=1, source_target_pairs={{0,6},{1,7},{2,4},{3,5},{4,2},{5,3},{6,0},{7,1},{8,14},{9,15},{10,... | collective-permute-start | bytes 393224 | tf_op jit(solution)/shard_map/ppermute | solution.py:246
  38.7 11.8 %collective-permute-start.3 = (bf16[128,512]{1,0:T(8,128)(2,1)S(1)}, bf16[128,512]{1,0:T(8,128)(2,1)S(1)}, u32[]{:S(2)}, u32[]{:S(2)}) collective-permute-start(bf16[128,512]{1,0:T(8,128)(2,1)S(1)} %get-tuple-element.30), channel_id=1, source_target_pairs={{0,4},{1,5},{2,6},{3,7},{4,0},{5,1},{6,2},{7,3},{8,12},{9,13},{10,... | collective-permute-start | bytes 393224 | tf_op jit(solution)/shard_map/ppermute | solution.py:246
  45.9 32.3 %collective-permute-start.12 = (bf16[2,64,1024]{2,1,0:T(8,128)(2,1)S(1)}, bf16[2,64,1024]{2,1,0:T(8,128)(2,1)S(1)}, u32[]{:S(2)}, u32[]{:S(2)}) collective-permute-start(bf16[2,64,1024]{2,1,0:T(8,128)(2,1)S(1)} %get-tuple-element.40), channel_id=1, source_target_pairs={{0,16},{8,24},{16,0},{24,8},{32,48},{40,56},{48,32},{56,40},{64,80... | collective-permute-start | bytes 786440 | tf_op jit(solution)/shard_map/ppermute | solution.py:246
  47.5 30.7 %collective-permute-start.13 = (bf16[2,64,1024]{2,1,0:T(8,128)(2,1)S(1)}, bf16[2,64,1024]{2,1,0:T(8,128)(2,1)S(1)}, u32[]{:S(2)}, u32[]{:S(2)}) collective-permute-start(bf16[2,64,1024]{2,1,0:T(8,128)(2,1)S(1)} %get-tuple-element.41), channel_id=1, source_target_pairs={{0,48},{8,56},{16,32},{24,40},{32,16},{40,24},{48,0},{56,8},{64,11... | collective-permute-start | bytes 786440 | tf_op jit(solution)/shard_map/ppermute | solution.py:246
  49.7 28.5 %collective-permute-start.14 = (bf16[2,64,1024]{2,1,0:T(8,128)(2,1)S(1)}, bf16[2,64,1024]{2,1,0:T(8,128)(2,1)S(1)}, u32[]{:S(2)}, u32[]{:S(2)}) collective-permute-start(bf16[2,64,1024]{2,1,0:T(8,128)(2,1)S(1)} %get-tuple-element.42), channel_id=1, source_target_pairs={{0,32},{8,40},{16,48},{24,56},{32,0},{40,8},{48,16},{56,24},{64,96... | collective-permute-start | bytes 786440 | tf_op jit(solution)/shard_map/ppermute | solution.py:246
  51.2 3.7 %collective-permute-start.4 = (bf16[128,512]{1,0:T(8,128)(2,1)S(1)}, bf16[128,512]{1,0:T(8,128)(2,1)S(1)}, u32[]{:S(2)}, u32[]{:S(2)}) collective-permute-start(bf16[128,512]{1,0:T(8,128)(2,1)S(1)} %get-tuple-element.31.gm_ref), channel_id=1, source_target_pairs={{0,8},{8,0},{16,24},{24,16},{32,40},{40,32},{48,56},{56,48},{64,72... | collective-permute-start | bytes 393224 | tf_op jit(solution)/shard_map/ppermute | solution.py:246
  51.2 3.7 %collective-permute-start.5 = (bf16[128,512]{1,0:T(8,128)(2,1)S(1)}, bf16[128,512]{1,0:T(8,128)(2,1)S(1)}, u32[]{:S(2)}, u32[]{:S(2)}) collective-permute-start(bf16[128,512]{1,0:T(8,128)(2,1)S(1)} %get-tuple-element.31.gm_ref), channel_id=1, source_target_pairs={{8,16},{24,32},{40,48},{56,64},{72,80},{88,96},{104,112},{16,8},{3... | collective-permute-start | bytes 393224 | tf_op jit(solution)/shard_map/ppermute | solution.py:319
  66.6 21.7 %all-to-all-start = ((bf16[16,32,256]{2,1,0:T(8,128)(2,1)}), bf16[16,32,256]{2,1,0:T(8,128)(2,1)S(1)}, u32[]{:S(2)}, u32[]{:S(2)}) async-start(bf16[16,32,256]{2,1,0:T(8,128)(2,1)} %get-tuple-element.45), calls=%async_computation | async-start | bytes 524288 | tf_op jit(solution)/shard_map/all_to_all | solution.py:349
  78.4 11.3 %collective-permute-start.15 = (bf16[64,1024]{1,0:T(8,128)(2,1)S(1)}, bf16[64,1024]{1,0:T(8,128)(2,1)S(1)}, u32[]{:S(2)}, u32[]{:S(2)}) collective-permute-start(bf16[64,1024]{1,0:T(8,128)(2,1)S(1)} %get-tuple-element.44), channel_id=1, source_target_pairs={{0,64},{8,72},{16,80},{24,88},{32,96},{40,104},{48,112},{56,120},{... | collective-permute-start | bytes 393224 | tf_op jit(solution)/shard_map/ppermute | solution.py:246

commit v7 on v2

--- a/solution.py
+++ b/solution.py
@@ -10,6 +10,7 @@
 
 GROUP = 64
 VN = 32
+JOINT = 8
 F32 = jnp.float32
 BF16 = jnp.bfloat16
 
@@ -154,14 +155,14 @@
     own_cols = iota((16, 8, 256), 1) == (iota((16, 8, 256), 2) & 7)
 
     def step(i, carry):
-        band = pl.ds(pl.multiple_of(i * 16, 16), 16)
+        band = pl.ds(pl.multiple_of(i * 8 * JOINT, 8 * JOINT), 8 * JOINT)
         gm = gm_ref[band, :].astype(F32)
         gs = gs_ref[band, :].astype(F32)
         gp = gp_ref[band, :].astype(F32)
         ext16 = jnp.concatenate([jnp.where(core0, gp, gs), gm, jnp.where(core0, gs, gp)], axis=1)
         outs = []
-        for h in range(2):
-            group = 2 * i + h
+        for h in range(JOINT):
+            group = JOINT * i + h
             ext = ext16[8 * h : 8 * h + 8]
             two = jnp.concatenate([ext, pltpu.roll(ext, width - 1, 1)], axis=0).astype(BF16)
             for k in range(VN // 2):
@@ -208,7 +209,7 @@
         o_ref[band, :] = jnp.concatenate(outs, axis=0)
         return carry
 
-    lax.fori_loop(0, rows // 16, step, 0)
+    lax.fori_loop(0, rows // (8 * JOINT), step, 0)
     keep_ref[...] = t_ref[0:8]
     send_ref[...] = t_ref[8:16].astype(BF16)
 
@@ -354,7 +355,7 @@
         ],
         (pos, grad_conv, halo_core, halo_out, *prepared),
         scratch=[
-            pltpu.VMEM((2, 256, 3 * tok), BF16),
+            pltpu.VMEM((JOINT, 256, 3 * tok), BF16),
             pltpu.VMEM((16, rows // 4, 256), F32),
         ],
     )

time: 89.8 us -> 86.8 us (0.967)
  Pallas kernels: 26.8 us -> 23.8 us
    pallas_call x12, Pallas kernels: 26.8 us -> 23.8 us  [call(): pl.pallas_call(body, out_shape=out_shape, in_specs=[smem()] * scalars + [...]
  transfers between devices with their start and end apart: 21 -> 21, of which waited for: 7 -> 7; matrix products, arithmetic and copies ran while one was open for 0% -> 0% of each run, Pallas kernels for 29% -> 27%
where the time goes in v7:
time: 86.8 us; the launch traced here: 86.7 us
  starting transfers between devices  34.6 us (40%)
  waiting for transfers between devices  27.3 us (31%)
  Pallas kernels  23.8 us (27%)
    ppermute x20, starting transfers between devices, swap(): lax.ppermute(v, axis, [(i, i ^ mask) for i in range(lax.axis_size(axis))])  34 us
    ppermute x20, waiting for transfers between devices, swap(): lax.ppermute(v, axis, [(i, i ^ mask) for i in range(lax.axis_size(axis))])  27.3 us
    pallas_call x12, Pallas kernels, call(): pl.pallas_call(body, out_shape=out_shape, in_specs=[smem()] * scalars + [...  23.8 us
  transfers between devices with their start and end apart: 21, of which 7 were waited for; matrix products, arithmetic and copies ran while one was open for 0% of the time, Pallas kernels for 27%

profile of v7, /device:TPU:0, one launch (start us, length us, event | category | flops | bytes accessed | tf_op | source)
XLA Modules:
  0.0 86.7 jit_solution(1856366212408760670)
XLA Ops:
  0.9 3.9 %shard_map.102 = (bf16[512,512]{1,0:T(8,128)(2,1)S(1)}, bf16[512,512]{1,0:T(8,128)(2,1)S(1)}) custom-call(s32[5]{0:T(128)S(1)} %stack.32.pos_ref, bf16[1024,1024]{1,0:T(8,128)(2,1)} %w_hbm.1, bf16[512,1024]{1,0:T(8,128)(2,1)} %og_ref.1), custom_call_target="tpu_custom_call" | custom-call | tf_op jit(solution)/shard_map/pallas_call | solution.py:266
  4.7 1.7 %collective-permute-start = (bf16[512,512]{1,0:T(8,128)(2,1)S(1)}, bf16[512,512]{1,0:T(8,128)(2,1)S(1)}, u32[]{:S(2)}, u32[]{:S(2)}) collective-permute-start(bf16[512,512]{1,0:T(8,128)(2,1)S(1)} %get-tuple-element.33), channel_id=1, source_target_pairs={{0,1},{1,0},{2,3},{3,2},{4,5},{5,4},{6,7},{7,6},{8,9},{9,8},{10,11... | collective-permute-start | bytes 1572872 | tf_op jit(solution)/shard_map/ppermute | solution.py:255
  6.4 1.6 %shard_map.107 = (bf16[64,512]{1,0:T(8,128)(2,1)S(1)}, bf16[64,512]{1,0:T(8,128)(2,1)S(1)}) custom-call(s32[5]{0:T(128)S(1)} %stack.32.pos_ref, bf16[128,512]{1,0:T(8,128)(2,1)} %v_hbm.1, bf16[128,512]{1,0:T(8,128)(2,1)} %g_hbm.1), custom_call_target="tpu_custom_call" | custom-call | tf_op jit(solution)/shard_map/pallas_call | solution.py:266
  9.8 12.2 %collective-permute-done.7 = bf16[64,1024]{1,0:T(8,128)(2,1)S(1)} collective-permute-done((bf16[64,1024]{1,0:T(8,128)(2,1)S(1)}, bf16[64,1024]{1,0:T(8,128)(2,1)S(1)}, u32[]{:S(2)}, u32[]{:S(2)}) %collective-permute-start.7) | collective-permute-done | bytes 131104 | tf_op jit(solution)/shard_map/ppermute | solution.py:255
  22.0 4.1 %collective-permute-start.10 = (bf16[2,64,1024]{2,1,0:T(8,128)(2,1)S(1)}, bf16[2,64,1024]{2,1,0:T(8,128)(2,1)S(1)}, u32[]{:S(2)}, u32[]{:S(2)}) collective-permute-start(bf16[2,64,1024]{2,1,0:T(8,128)(2,1)S(1)} %pad_maximum_fusion.b0), channel_id=1, source_target_pairs={{0,4},{1,5},{2,6},{3,7},{4,0},{5,1},{6,2},{7,3},{8,12},{9,13},{10,... | collective-permute-start | bytes 786440 | tf_op jit(solution)/shard_map/ppermute | solution.py:255
  27.2 1.2 %collective-permute-start.1 = (bf16[128,512]{1,0:T(8,128)(2,1)S(1)}, bf16[128,512]{1,0:T(8,128)(2,1)S(1)}, u32[]{:S(2)}, u32[]{:S(2)}) collective-permute-start(bf16[128,512]{1,0:T(8,128)(2,1)S(1)} %get-tuple-element.35), channel_id=1, source_target_pairs={{0,2},{1,3},{2,0},{3,1},{4,6},{5,7},{6,4},{7,5},{8,10},{9,11},{10,... | collective-permute-start | bytes 393224 | tf_op jit(solution)/shard_map/ppermute | solution.py:255
  28.4 4.8 %collective-permute-done.10.b2 = bf16[2,64,1024]{2,1,0:T(8,128)(2,1)S(1)} collective-permute-done((bf16[2,64,1024]{2,1,0:T(8,128)(2,1)S(1)}, bf16[2,64,1024]{2,1,0:T(8,128)(2,1)S(1)}, u32[]{:S(2)}, u32[]{:S(2)}) %collective-permute-start.10) | collective-permute-done | bytes 262176 | tf_op jit(solution)/shard_map/ppermute | solution.py:255
  33.2 3.7 %collective-permute-start.2 = (bf16[128,512]{1,0:T(8,128)(2,1)S(1)}, bf16[128,512]{1,0:T(8,128)(2,1)S(1)}, u32[]{:S(2)}, u32[]{:S(2)}) collective-permute-start(bf16[128,512]{1,0:T(8,128)(2,1)S(1)} %get-tuple-element.36), channel_id=1, source_target_pairs={{0,6},{1,7},{2,4},{3,5},{4,2},{5,3},{6,0},{7,1},{8,14},{9,15},{10,... | collective-permute-start | bytes 393224 | tf_op jit(solution)/shard_map/ppermute | solution.py:255
  36.9 2.9 %collective-permute-done.8.b1 = bf16[2,64,1024]{2,1,0:T(8,128)(2,1)S(1)} collective-permute-done((bf16[2,64,1024]{2,1,0:T(8,128)(2,1)S(1)}, bf16[2,64,1024]{2,1,0:T(8,128)(2,1)S(1)}, u32[]{:S(2)}, u32[]{:S(2)}) %collective-permute-start.8) | collective-permute-done | bytes 262176 | tf_op jit(solution)/shard_map/ppermute | solution.py:255
  39.9 1.2 %collective-permute-start.3 = (bf16[128,512]{1,0:T(8,128)(2,1)S(1)}, bf16[128,512]{1,0:T(8,128)(2,1)S(1)}, u32[]{:S(2)}, u32[]{:S(2)}) collective-permute-start(bf16[128,512]{1,0:T(8,128)(2,1)S(1)} %get-tuple-element.37), channel_id=1, source_target_pairs={{0,4},{1,5},{2,6},{3,7},{4,0},{5,1},{6,2},{7,3},{8,12},{9,13},{10,... | collective-permute-start | bytes 393224 | tf_op jit(solution)/shard_map/ppermute | solution.py:255
  41.0 3.6 %shard_map.108 = (bf16[2,64,1024]{2,1,0:T(8,128)(2,1)S(1)}, bf16[2,64,1024]{2,1,0:T(8,128)(2,1)S(1)}, bf16[2,64,1024]{2,1,0:T(8,128)(2,1)S(1)}, bf16[2,64,1024]{2,1,0:T(8,128)(2,1)S(1)}) custom-call(s32[5]{0:T(128)S(1)} %stack.32.pos_ref, bf16[2,64,1024]{2,1,0:T(8,128)(2,1)S(1)} %pad_maximum_fusion.b0, bf16[2,64,1024]{2,1,0:T(8,128)(2,1)S(1)} %collective-permute-done.8.b1, ...), custom_call_target="tpu_custom_call" | custom-call | tf_op jit(solution)/shard_map/pallas_call | solution.py:266
  44.7 1.7 %collective-permute-start.12 = (bf16[2,64,1024]{2,1,0:T(8,128)(2,1)S(1)}, bf16[2,64,1024]{2,1,0:T(8,128)(2,1)S(1)}, u32[]{:S(2)}, u32[]{:S(2)}) collective-permute-start(bf16[2,64,1024]{2,1,0:T(8,128)(2,1)S(1)} %get-tuple-element.47), channel_id=1, source_target_pairs={{0,16},{8,24},{16,0},{24,8},{32,48},{40,56},{48,32},{56,40},{64,80... | collective-permute-start | bytes 786440 | tf_op jit(solution)/shard_map/ppermute | solution.py:255
  46.3 2.2 %collective-permute-start.13 = (bf16[2,64,1024]{2,1,0:T(8,128)(2,1)S(1)}, bf16[2,64,1024]{2,1,0:T(8,128)(2,1)S(1)}, u32[]{:S(2)}, u32[]{:S(2)}) collective-permute-start(bf16[2,64,1024]{2,1,0:T(8,128)(2,1)S(1)} %get-tuple-element.48), channel_id=1, source_target_pairs={{0,48},{8,56},{16,32},{24,40},{32,16},{40,24},{48,0},{56,8},{64,11... | collective-permute-start | bytes 786440 | tf_op jit(solution)/shard_map/ppermute | solution.py:255
  50.7 3.0 %shard_map.105 = (bf16[16,2,128,256]{3,2,1,0:T(8,128)(2,1)S(1)}, bf16[16,256,512]{2,1,0:T(8,128)(2,1)S(1)}, bf16[16,256,512]{2,1,0:T(8,128)(2,1)S(1)}) custom-call(s32[5]{0:T(128)S(1)} %stack.32.pos_ref, s32[16]{0:T(128)S(1)} %copy-done.5, bf16[2,128,512]{2,1,0:T(8,128)(2,1)S(1)} %copy-done.3, bf16[128,512]{1,0:T(8,128)(2,1)S(1)} %copy-done.4), custom_call_target="tpu_custom_call" | custom-call | tf_op jit(solution)/shard_map/pallas_call | solution.py:266
  53.7 8.5 %shard_map.106 = (f32[128,512]{1,0:T(8,128)}, f32[8,32,256]{2,1,0:T(8,128)S(1)}, bf16[8,32,256]{2,1,0:T(8,128)(2,1)S(1)}) custom-call(s32[5]{0:T(128)S(1)} %stack.32.pos_ref, bf16[128,512]{1,0:T(8,128)(2,1)S(1)} %get-tuple-element.38.gm_ref, bf16[128,512]{1,0:T(8,128)(2,1)S(1)} %collective-permute-done.4.gs_ref, ...), custom_call_target="tpu_custom_call" | custom-call | tf_op jit(solution)/shard_map/pallas_call | solution.py:266
  62.3 3.8 %collective-permute-start.16 = (bf16[8,32,256]{2,1,0:T(8,128)(2,1)S(1)}, bf16[8,32,256]{2,1,0:T(8,128)(2,1)S(1)}, u32[]{:S(2)}, u32[]{:S(2)}) collective-permute-start(bf16[8,32,256]{2,1,0:T(8,128)(2,1)S(1)} %get-tuple-element.53), channel_id=1, source_target_pairs={{0,8},{8,0},{16,24},{24,16},{32,40},{40,32},{48,56},{56,48},{64,72... | collective-permute-start | bytes 393224 | tf_op jit(solution)/shard_map/ppermute | solution.py:255
  66.2 6.0 %collective-permute-start.15 = (bf16[64,1024]{1,0:T(8,128)(2,1)S(1)}, bf16[64,1024]{1,0:T(8,128)(2,1)S(1)}, u32[]{:S(2)}, u32[]{:S(2)}) collective-permute-start(bf16[64,1024]{1,0:T(8,128)(2,1)S(1)} %get-tuple-element.51), channel_id=1, source_target_pairs={{0,64},{8,72},{16,80},{24,88},{32,96},{40,104},{48,112},{56,120},{... | collective-permute-start | bytes 393224 | tf_op jit(solution)/shard_map/ppermute | solution.py:255
  72.3 1.5 %collective-permute-start.18 = (bf16[2,32,256]{2,1,0:T(8,128)(2,1)S(1)}, bf16[2,32,256]{2,1,0:T(8,128)(2,1)S(1)}, u32[]{:S(2)}, u32[]{:S(2)}) collective-permute-start(bf16[2,32,256]{2,1,0:T(8,128)(2,1)S(1)} %get-tuple-element.56), channel_id=1, source_target_pairs={{0,48},{8,56},{16,32},{24,40},{32,16},{40,24},{48,0},{56,8},{64,11... | collective-permute-start | bytes 98312 | tf_op jit(solution)/shard_map/ppermute | solution.py:255
  73.8 2.6 %collective-permute-start.19 = (bf16[2,32,256]{2,1,0:T(8,128)(2,1)S(1)}, bf16[2,32,256]{2,1,0:T(8,128)(2,1)S(1)}, u32[]{:S(2)}, u32[]{:S(2)}) collective-permute-start(bf16[2,32,256]{2,1,0:T(8,128)(2,1)S(1)} %get-tuple-element.57), channel_id=1, source_target_pairs={{0,32},{8,40},{16,48},{24,56},{32,0},{40,8},{48,16},{56,24},{64,96... | collective-permute-start | bytes 98312 | tf_op jit(solution)/shard_map/ppermute | solution.py:255
  76.4 1.1 %collective-permute-done.18.r3 = bf16[2,32,256]{2,1,0:T(8,128)(2,1)S(1)} collective-permute-done((bf16[2,32,256]{2,1,0:T(8,128)(2,1)S(1)}, bf16[2,32,256]{2,1,0:T(8,128)(2,1)S(1)}, u32[]{:S(2)}, u32[]{:S(2)}) %collective-permute-start.18) | collective-permute-done | bytes 32800 | tf_op jit(solution)/shard_map/ppermute | solution.py:255
  77.5 1.7 %collective-permute-done.19.r2 = bf16[2,32,256]{2,1,0:T(8,128)(2,1)S(1)} collective-permute-done((bf16[2,32,256]{2,1,0:T(8,128)(2,1)S(1)}, bf16[2,32,256]{2,1,0:T(8,128)(2,1)S(1)}, u32[]{:S(2)}, u32[]{:S(2)}) %collective-permute-start.19) | collective-permute-done | bytes 32800 | tf_op jit(solution)/shard_map/ppermute | solution.py:255
  79.2 1.8 %collective-permute-start.20 = (bf16[32,256]{1,0:T(8,128)(2,1)S(1)}, bf16[32,256]{1,0:T(8,128)(2,1)S(1)}, u32[]{:S(2)}, u32[]{:S(2)}) collective-permute-start(bf16[32,256]{1,0:T(8,128)(2,1)S(1)} %get-tuple-element.59), channel_id=1, source_target_pairs={{0,64},{8,72},{16,80},{24,88},{32,96},{40,104},{48,112},{56,120},{... | collective-permute-start | bytes 49160 | tf_op jit(solution)/shard_map/ppermute | solution.py:255
  81.1 3.5 %collective-permute-done.20.got = bf16[32,256]{1,0:T(8,128)(2,1)S(1)} collective-permute-done((bf16[32,256]{1,0:T(8,128)(2,1)S(1)}, bf16[32,256]{1,0:T(8,128)(2,1)S(1)}, u32[]{:S(2)}, u32[]{:S(2)}) %collective-permute-start.20) | collective-permute-done | bytes 16416 | tf_op jit(solution)/shard_map/ppermute | solution.py:255
  84.5 1.4 %shard_map.113 = f32[2,32,128]{2,1,0:T(8,128)} custom-call(s32[5]{0:T(128)S(1)} %stack.32.pos_ref, s32[16]{0:T(128)S(1)} %copy-done.5, f32[32,256]{1,0:T(8,128)S(1)} %get-tuple-element.58.part_ref, bf16[32,256]{1,0:T(8,128)(2,1)S(1)} %collective-permute-done.20.got), custom_call_target="tpu_custom_call" | custom-call | tf_op jit(solution)/shard_map/pallas_call | solution.py:266
  (46 shorter events, 6.4 us)
Async XLA Ops:
  0.6 40.4 %collective-permute-start.11 = (bf16[512,1024]{1,0:T(8,128)(2,1)}, bf16[512,1024]{1,0:T(8,128)(2,1)S(1)}, u32[]{:S(2)}, u32[]{:S(2)}) collective-permute-start(bf16[512,1024]{1,0:T(8,128)(2,1)} %og_ref.1), channel_id=1, source_target_pairs={{0,8},{8,0},{16,24},{24,16},{32,40},{40,32},{48,56},{56,48},{64,72... | collective-permute-start | bytes 3145736 | tf_op jit(solution)/shard_map/ppermute | solution.py:255
  0.8 49.9 %copy-start.3 = (bf16[2,128,512]{2,1,0:T(8,128)(2,1)S(1)}, bf16[2,128,512]{2,1,0:T(8,128)(2,1)}, u32[]{:S(2)}) copy-start(bf16[2,128,512]{2,1,0:T(8,128)(2,1)} %f_ref.1) | copy-start | bytes 786436
  0.8 49.9 %copy-start.4 = (bf16[128,512]{1,0:T(8,128)(2,1)S(1)}, bf16[128,512]{1,0:T(8,128)(2,1)}, u32[]{:S(2)}) copy-start(bf16[128,512]{1,0:T(8,128)(2,1)} %x_ref.1) | copy-start | bytes 393220
  0.8 49.9 %copy-start.5 = (s32[16]{0:T(128)S(1)}, s32[16]{0:T(128)}, u32[]{:S(2)}) copy-start(s32[16]{0:T(128)} %reach_ref.3) | copy-start | bytes 196
  4.7 22.3 %collective-permute-start = (bf16[512,512]{1,0:T(8,128)(2,1)S(1)}, bf16[512,512]{1,0:T(8,128)(2,1)S(1)}, u32[]{:S(2)}, u32[]{:S(2)}) collective-permute-start(bf16[512,512]{1,0:T(8,128)(2,1)S(1)} %get-tuple-element.33), channel_id=1, source_target_pairs={{0,1},{1,0},{2,3},{3,2},{4,5},{5,4},{6,7},{7,6},{8,9},{9,8},{10,11... | collective-permute-start | bytes 1572872 | tf_op jit(solution)/shard_map/ppermute | solution.py:255
  8.0 1.3 %collective-permute-start.6 = (bf16[64,512]{1,0:T(8,128)(2,1)S(1)}, bf16[64,512]{1,0:T(8,128)(2,1)S(1)}, u32[]{:S(2)}, u32[]{:S(2)}) collective-permute-start(bf16[64,512]{1,0:T(8,128)(2,1)S(1)} %get-tuple-element.45), channel_id=1, source_target_pairs={{0,8},{8,0},{16,24},{24,16},{32,40},{40,32},{48,56},{56,48},{64,72... | collective-permute-start | bytes 196616 | tf_op jit(solution)/shard_map/ppermute | solution.py:255
  9.3 12.6 %collective-permute-start.7 = (bf16[64,1024]{1,0:T(8,128)(2,1)S(1)}, bf16[64,1024]{1,0:T(8,128)(2,1)S(1)}, u32[]{:S(2)}, u32[]{:S(2)}) collective-permute-start(bf16[64,1024]{1,0:T(8,128)(2,1)S(1)} %constant_dynamic-update-slice_fusion), channel_id=1, source_target_pairs={{0,1},{1,0},{2,3},{3,2},{4,5},{5,4},{6,7},{7,6},{8,9},{9,8},{10,11... | collective-permute-start | bytes 393224 | tf_op jit(solution)/shard_map/ppermute | solution.py:255
  22.0 11.2 %collective-permute-start.10 = (bf16[2,64,1024]{2,1,0:T(8,128)(2,1)S(1)}, bf16[2,64,1024]{2,1,0:T(8,128)(2,1)S(1)}, u32[]{:S(2)}, u32[]{:S(2)}) collective-permute-start(bf16[2,64,1024]{2,1,0:T(8,128)(2,1)S(1)} %pad_maximum_fusion.b0), channel_id=1, source_target_pairs={{0,4},{1,5},{2,6},{3,7},{4,0},{5,1},{6,2},{7,3},{8,12},{9,13},{10,... | collective-permute-start | bytes 786440 | tf_op jit(solution)/shard_map/ppermute | solution.py:255
  26.0 13.8 %collective-permute-start.8 = (bf16[2,64,1024]{2,1,0:T(8,128)(2,1)S(1)}, bf16[2,64,1024]{2,1,0:T(8,128)(2,1)S(1)}, u32[]{:S(2)}, u32[]{:S(2)}) collective-permute-start(bf16[2,64,1024]{2,1,0:T(8,128)(2,1)S(1)} %pad_maximum_fusion.b0), channel_id=1, source_target_pairs={{0,2},{1,3},{2,0},{3,1},{4,6},{5,7},{6,4},{7,5},{8,10},{9,11},{10,... | collective-permute-start | bytes 786440 | tf_op jit(solution)/shard_map/ppermute | solution.py:255
  27.0 14.0 %collective-permute-start.9 = (bf16[2,64,1024]{2,1,0:T(8,128)(2,1)S(1)}, bf16[2,64,1024]{2,1,0:T(8,128)(2,1)S(1)}, u32[]{:S(2)}, u32[]{:S(2)}) collective-permute-start(bf16[2,64,1024]{2,1,0:T(8,128)(2,1)S(1)} %pad_maximum_fusion.b0), channel_id=1, source_target_pairs={{0,6},{1,7},{2,4},{3,5},{4,2},{5,3},{6,0},{7,1},{8,14},{9,15},{10,... | collective-permute-start | bytes 786440 | tf_op jit(solution)/shard_map/ppermute | solution.py:255
  27.2 21.3 %collective-permute-start.1 = (bf16[128,512]{1,0:T(8,128)(2,1)S(1)}, bf16[128,512]{1,0:T(8,128)(2,1)S(1)}, u32[]{:S(2)}, u32[]{:S(2)}) collective-permute-start(bf16[128,512]{1,0:T(8,128)(2,1)S(1)} %get-tuple-element.35), channel_id=1, source_target_pairs={{0,2},{1,3},{2,0},{3,1},{4,6},{5,7},{6,4},{7,5},{8,10},{9,11},{10,... | collective-permute-start | bytes 393224 | tf_op jit(solution)/shard_map/ppermute | solution.py:255
  33.2 16.0 %collective-permute-start.2 = (bf16[128,512]{1,0:T(8,128)(2,1)S(1)}, bf16[128,512]{1,0:T(8,128)(2,1)S(1)}, u32[]{:S(2)}, u32[]{:S(2)}) collective-permute-start(bf16[128,512]{1,0:T(8,128)(2,1)S(1)} %get-tuple-element.36), channel_id=1, source_target_pairs={{0,6},{1,7},{2,4},{3,5},{4,2},{5,3},{6,0},{7,1},{8,14},{9,15},{10,... | collective-permute-start | bytes 393224 | tf_op jit(solution)/shard_map/ppermute | solution.py:255
  39.9 9.4 %collective-permute-start.3 = (bf16[128,512]{1,0:T(8,128)(2,1)S(1)}, bf16[128,512]{1,0:T(8,128)(2,1)S(1)}, u32[]{:S(2)}, u32[]{:S(2)}) collective-permute-start(bf16[128,512]{1,0:T(8,128)(2,1)S(1)} %get-tuple-element.37), channel_id=1, source_target_pairs={{0,4},{1,5},{2,6},{3,7},{4,0},{5,1},{6,2},{7,3},{8,12},{9,13},{10,... | collective-permute-start | bytes 393224 | tf_op jit(solution)/shard_map/ppermute | solution.py:255
  44.7 21.4 %collective-permute-start.12 = (bf16[2,64,1024]{2,1,0:T(8,128)(2,1)S(1)}, bf16[2,64,1024]{2,1,0:T(8,128)(2,1)S(1)}, u32[]{:S(2)}, u32[]{:S(2)}) collective-permute-start(bf16[2,64,1024]{2,1,0:T(8,128)(2,1)S(1)} %get-tuple-element.47), channel_id=1, source_target_pairs={{0,16},{8,24},{16,0},{24,8},{32,48},{40,56},{48,32},{56,40},{64,80... | collective-permute-start | bytes 786440 | tf_op jit(solution)/shard_map/ppermute | solution.py:255
  46.3 19.7 %collective-permute-start.13 = (bf16[2,64,1024]{2,1,0:T(8,128)(2,1)S(1)}, bf16[2,64,1024]{2,1,0:T(8,128)(2,1)S(1)}, u32[]{:S(2)}, u32[]{:S(2)}) collective-permute-start(bf16[2,64,1024]{2,1,0:T(8,128)(2,1)S(1)} %get-tuple-element.48), channel_id=1, source_target_pairs={{0,48},{8,56},{16,32},{24,40},{32,16},{40,24},{48,0},{56,8},{64,11... | collective-permute-start | bytes 786440 | tf_op jit(solution)/shard_map/ppermute | solution.py:255
  48.5 17.6 %collective-permute-start.14 = (bf16[2,64,1024]{2,1,0:T(8,128)(2,1)S(1)}, bf16[2,64,1024]{2,1,0:T(8,128)(2,1)S(1)}, u32[]{:S(2)}, u32[]{:S(2)}) collective-permute-start(bf16[2,64,1024]{2,1,0:T(8,128)(2,1)S(1)} %get-tuple-element.49), channel_id=1, source_target_pairs={{0,32},{8,40},{16,48},{24,56},{32,0},{40,8},{48,16},{56,24},{64,96... | collective-permute-start | bytes 786440 | tf_op jit(solution)/shard_map/ppermute | solution.py:255
  50.0 3.7 %collective-permute-start.4 = (bf16[128,512]{1,0:T(8,128)(2,1)S(1)}, bf16[128,512]{1,0:T(8,128)(2,1)S(1)}, u32[]{:S(2)}, u32[]{:S(2)}) collective-permute-start(bf16[128,512]{1,0:T(8,128)(2,1)S(1)} %get-tuple-element.38.gm_ref), channel_id=1, source_target_pairs={{0,8},{8,0},{16,24},{24,16},{32,40},{40,32},{48,56},{56,48},{64,72... | collective-permute-start | bytes 393224 | tf_op jit(solution)/shard_map/ppermute | solution.py:255
  50.0 3.7 %collective-permute-start.5 = (bf16[128,512]{1,0:T(8,128)(2,1)S(1)}, bf16[128,512]{1,0:T(8,128)(2,1)S(1)}, u32[]{:S(2)}, u32[]{:S(2)}) collective-permute-start(bf16[128,512]{1,0:T(8,128)(2,1)S(1)} %get-tuple-element.38.gm_ref), channel_id=1, source_target_pairs={{8,16},{24,32},{40,48},{56,64},{72,80},{88,96},{104,112},{16,8},{3... | collective-permute-start | bytes 393224 | tf_op jit(solution)/shard_map/ppermute | solution.py:328
  62.3 9.9 %collective-permute-start.16 = (bf16[8,32,256]{2,1,0:T(8,128)(2,1)S(1)}, bf16[8,32,256]{2,1,0:T(8,128)(2,1)S(1)}, u32[]{:S(2)}, u32[]{:S(2)}) collective-permute-start(bf16[8,32,256]{2,1,0:T(8,128)(2,1)S(1)} %get-tuple-element.53), channel_id=1, source_target_pairs={{0,8},{8,0},{16,24},{24,16},{32,40},{40,32},{48,56},{56,48},{64,72... | collective-permute-start | bytes 393224 | tf_op jit(solution)/shard_map/ppermute | solution.py:255
  66.2 19.7 %collective-permute-start.15 = (bf16[64,1024]{1,0:T(8,128)(2,1)S(1)}, bf16[64,1024]{1,0:T(8,128)(2,1)S(1)}, u32[]{:S(2)}, u32[]{:S(2)}) collective-permute-start(bf16[64,1024]{1,0:T(8,128)(2,1)S(1)} %get-tuple-element.51), channel_id=1, source_target_pairs={{0,64},{8,72},{16,80},{24,88},{32,96},{40,104},{48,112},{56,120},{... | collective-permute-start | bytes 393224 | tf_op jit(solution)/shard_map/ppermute | solution.py:255
  72.2 4.2 %collective-permute-start.17 = (bf16[2,32,256]{2,1,0:T(8,128)(2,1)S(1)}, bf16[2,32,256]{2,1,0:T(8,128)(2,1)S(1)}, u32[]{:S(2)}, u32[]{:S(2)}) collective-permute-start(bf16[2,32,256]{2,1,0:T(8,128)(2,1)S(1)} %get-tuple-element.55), channel_id=1, source_target_pairs={{0,16},{8,24},{16,0},{24,8},{32,48},{40,56},{48,32},{56,40},{64,80... | collective-permute-start | bytes 98312 | tf_op jit(solution)/shard_map/ppermute | solution.py:255
  72.3 5.2 %collective-permute-start.18 = (bf16[2,32,256]{2,1,0:T(8,128)(2,1)S(1)}, bf16[2,32,256]{2,1,0:T(8,128)(2,1)S(1)}, u32[]{:S(2)}, u32[]{:S(2)}) collective-permute-start(bf16[2,32,256]{2,1,0:T(8,128)(2,1)S(1)} %get-tuple-element.56), channel_id=1, source_target_pairs={{0,48},{8,56},{16,32},{24,40},{32,16},{40,24},{48,0},{56,8},{64,11... | collective-permute-start | bytes 98312 | tf_op jit(solution)/shard_map/ppermute | solution.py:255
  73.8 5.4 %collective-permute-start.19 = (bf16[2,32,256]{2,1,0:T(8,128)(2,1)S(1)}, bf16[2,32,256]{2,1,0:T(8,128)(2,1)S(1)}, u32[]{:S(2)}, u32[]{:S(2)}) collective-permute-start(bf16[2,32,256]{2,1,0:T(8,128)(2,1)S(1)} %get-tuple-element.57), channel_id=1, source_target_pairs={{0,32},{8,40},{16,48},{24,56},{32,0},{40,8},{48,16},{56,24},{64,96... | collective-permute-start | bytes 98312 | tf_op jit(solution)/shard_map/ppermute | solution.py:255
  79.2 5.3 %collective-permute-start.20 = (bf16[32,256]{1,0:T(8,128)(2,1)S(1)}, bf16[32,256]{1,0:T(8,128)(2,1)S(1)}, u32[]{:S(2)}, u32[]{:S(2)}) collective-permute-start(bf16[32,256]{1,0:T(8,128)(2,1)S(1)} %get-tuple-element.59), channel_id=1, source_target_pairs={{0,64},{8,72},{16,80},{24,88},{32,96},{40,104},{48,112},{56,120},{... | collective-permute-start | bytes 49160 | tf_op jit(solution)/shard_map/ppermute | solution.py:255
  (3 other events, 137.2 us)

commit v8 on v7

--- a/solution.py
+++ b/solution.py
@@ -45,7 +45,7 @@
         ref[...] = (v_ref[band, :].astype(F32) * g_ref[band, :].astype(F32)).astype(BF16)
 
 
-def first_product(pos_ref, w_hbm, og_hbm, keep, send, w_ref, og_ref, sems):
+def first_product(pos_ref, w_hbm, og_hbm, keep, send, og_ref, w_ref, sems):
     z = pos_ref[0]
     x = pos_ref[1]
     og_load = pltpu.make_async_copy(og_hbm, og_ref, sems.at[8])
@@ -74,10 +74,14 @@
         ref[...] = (k_ref[band, :].astype(F32) + r_ref[band, :].astype(F32)).astype(ref.dtype)
 
 
-def gate_grads(k_ref, r1, r3, r2, v_ref, g_ref, gate_ref, conv_ref):
+def gate_grads(k_ref, r1, r3, r2, g_ref, conv_ref, total_ref):
     total = k_ref[...] + r1[...].astype(F32) + r3[...].astype(F32) + r2[...].astype(F32)
-    gate_ref[...] = total * v_ref[...].astype(F32)
     conv_ref[...] = (total * g_ref[...].astype(F32)).astype(BF16)
+    total_ref[...] = total
+
+
+def gate_output(total_ref, v_ref, gate_ref):
+    gate_ref[...] = total_ref[...] * v_ref[...].astype(F32)
 
 
 def second_product(pos_ref, b0, b1, b3, b2, og_ref, ogs_ref, *refs):
@@ -298,13 +302,12 @@
     b3 = swap(pair, "chan", 6)
     b2 = swap(pair, "chan", 4)
 
-    keep, send = call(
+    keep, send, og_local = call(
         first_product,
-        [shape((rows * 4, tok), BF16)] * 2,
+        [shape((rows * 4, tok), BF16)] * 2 + [shape((tok, feats), BF16)],
         (pos, out_weight, out_grad),
         scratch=[
             pltpu.VMEM((4, 2 * rows, feats), BF16),
-            pltpu.VMEM((tok, feats), BF16),
             pltpu.SemaphoreType.DMA((9,)),
         ],
         held_in=pltpu.HBM,
@@ -316,12 +319,13 @@
         scalars=0,
     )
     s1, s3, s2 = swap(s1, "chan", 2), swap(s3, "chan", 6), swap(s2, "chan", 4)
-    grad_gate, grad_conv = call(
+    grad_conv, total = call(
         gate_grads,
-        [shape((rows, tok), F32), shape((rows, tok), BF16)],
-        (keep, s1, s3, s2, conv_output, gate_values),
+        [shape((rows, tok), BF16), shape((rows, tok), F32)],
+        (keep, s1, s3, s2, gate_values),
         scalars=0,
     )
+    grad_gate = call(gate_output, shape((rows, tok), F32), (total, conv_output), scalars=0)
 
     halo_core = swap(grad_conv, "seq", 1)
     pairs = [(i, i + 1) for i in range(1, seq_count - 1, 2)]
@@ -330,7 +334,7 @@
     e = call(
         second_product,
         [shape((2, half, feats), BF16)] * 4,
-        (pos, pair, b1, b3, b2, out_grad, og_core),
+        (pos, pair, b1, b3, b2, og_local, og_core),
         scratch=[pltpu.VMEM((8, half, 2 * tok), BF16)],
     )
     e = [e[0], swap(e[1], "seq", 2), swap(e[2], "seq", 6), swap(e[3], "seq", 4)]

time: 86.8 us -> 89.7 us (1.033)
  starting transfers between devices: 34.6 us -> 37.4 us
    ppermute x20, starting transfers between devices: 34 us -> 36.7 us  [swap(): lax.ppermute(v, axis, [(i, i ^ mask) for i in range(lax.axis_size(axis))])]
    pallas_call x12 -> x13, Pallas kernels: 23.8 us -> 23.8 us  [call(): pl.pallas_call(body, out_shape=out_shape, in_specs=[smem()] * scalars + [...]
  transfers between devices with their start and end apart: 21 -> 21, of which waited for: 7 -> 6; matrix products, arithmetic and copies ran while one was open for 0% -> 0% of each run, Pallas kernels for 27% -> 26%
where the time goes in v8:
time: 89.7 us; the launch traced here: 89.6 us
  starting transfers between devices  37.4 us (42%)
  waiting for transfers between devices  27.4 us (31%)
  Pallas kernels  23.8 us (27%)
    ppermute x20, starting transfers between devices, swap(): lax.ppermute(v, axis, [(i, i ^ mask) for i in range(lax.axis_size(axis))])  36.7 us
    ppermute x20, waiting for transfers between devices, swap(): lax.ppermute(v, axis, [(i, i ^ mask) for i in range(lax.axis_size(axis))])  27.4 us
    pallas_call x13, Pallas kernels, call(): pl.pallas_call(body, out_shape=out_shape, in_specs=[smem()] * scalars + [...  23.8 us
  transfers between devices with their start and end apart: 21, of which 6 were waited for; matrix products, arithmetic and copies ran while one was open for 0% of the time, Pallas kernels for 26%

profile of v8, /device:TPU:0, one launch (start us, length us, event | category | flops | bytes accessed | tf_op | source)
XLA Modules:
  0.0 89.6 jit_solution(16558018007600609283)
XLA Ops:
  0.8 1.6 %shard_map.108 = (bf16[64,512]{1,0:T(8,128)(2,1)S(1)}, bf16[64,512]{1,0:T(8,128)(2,1)S(1)}) custom-call(s32[5]{0:T(128)S(1)} %stack.32.pos_ref, bf16[128,512]{1,0:T(8,128)(2,1)} %v_hbm.1, bf16[128,512]{1,0:T(8,128)(2,1)} %g_hbm.1), custom_call_target="tpu_custom_call" | custom-call | tf_op jit(solution)/shard_map/pallas_call | solution.py:270
  3.0 3.9 %shard_map.102 = (bf16[512,512]{1,0:T(8,128)(2,1)S(1)}, bf16[512,512]{1,0:T(8,128)(2,1)S(1)}, bf16[512,1024]{1,0:T(8,128)(2,1)S(1)}) custom-call(s32[5]{0:T(128)S(1)} %stack.32.pos_ref, bf16[1024,1024]{1,0:T(8,128)(2,1)} %w_hbm.1, bf16[512,1024]{1,0:T(8,128)(2,1)} %og_hbm.1), custom_call_target="tpu_custom_call" | custom-call | tf_op jit(solution)/shard_map/pallas_call | solution.py:270
  6.9 1.6 %collective-permute-start = (bf16[512,512]{1,0:T(8,128)(2,1)S(1)}, bf16[512,512]{1,0:T(8,128)(2,1)S(1)}, u32[]{:S(2)}, u32[]{:S(2)}) collective-permute-start(bf16[512,512]{1,0:T(8,128)(2,1)S(1)} %get-tuple-element.34), channel_id=1, source_target_pairs={{0,1},{1,0},{2,3},{3,2},{4,5},{5,4},{6,7},{7,6},{8,9},{9,8},{10,11... | collective-permute-start | bytes 1572872 | tf_op jit(solution)/shard_map/ppermute | solution.py:259
  9.1 14.5 %collective-permute-done.7 = bf16[64,1024]{1,0:T(8,128)(2,1)S(1)} collective-permute-done((bf16[64,1024]{1,0:T(8,128)(2,1)S(1)}, bf16[64,1024]{1,0:T(8,128)(2,1)S(1)}, u32[]{:S(2)}, u32[]{:S(2)}) %collective-permute-start.7) | collective-permute-done | bytes 131104 | tf_op jit(solution)/shard_map/ppermute | solution.py:259
  23.6 4.1 %collective-permute-start.10 = (bf16[2,64,1024]{2,1,0:T(8,128)(2,1)S(1)}, bf16[2,64,1024]{2,1,0:T(8,128)(2,1)S(1)}, u32[]{:S(2)}, u32[]{:S(2)}) collective-permute-start(bf16[2,64,1024]{2,1,0:T(8,128)(2,1)S(1)} %pad_maximum_fusion.b0), channel_id=1, source_target_pairs={{0,4},{1,5},{2,6},{3,7},{4,0},{5,1},{6,2},{7,3},{8,12},{9,13},{10,... | collective-permute-start | bytes 786440 | tf_op jit(solution)/shard_map/ppermute | solution.py:259
  28.9 1.8 %collective-permute-start.1 = (bf16[128,512]{1,0:T(8,128)(2,1)S(1)}, bf16[128,512]{1,0:T(8,128)(2,1)S(1)}, u32[]{:S(2)}, u32[]{:S(2)}) collective-permute-start(bf16[128,512]{1,0:T(8,128)(2,1)S(1)} %get-tuple-element.36), channel_id=1, source_target_pairs={{0,2},{1,3},{2,0},{3,1},{4,6},{5,7},{6,4},{7,5},{8,10},{9,11},{10,... | collective-permute-start | bytes 393224 | tf_op jit(solution)/shard_map/ppermute | solution.py:259
  30.7 4.2 %collective-permute-done.10.b2 = bf16[2,64,1024]{2,1,0:T(8,128)(2,1)S(1)} collective-permute-done((bf16[2,64,1024]{2,1,0:T(8,128)(2,1)S(1)}, bf16[2,64,1024]{2,1,0:T(8,128)(2,1)S(1)}, u32[]{:S(2)}, u32[]{:S(2)}) %collective-permute-start.10) | collective-permute-done | bytes 262176 | tf_op jit(solution)/shard_map/ppermute | solution.py:259
  34.8 3.7 %collective-permute-start.2 = (bf16[128,512]{1,0:T(8,128)(2,1)S(1)}, bf16[128,512]{1,0:T(8,128)(2,1)S(1)}, u32[]{:S(2)}, u32[]{:S(2)}) collective-permute-start(bf16[128,512]{1,0:T(8,128)(2,1)S(1)} %get-tuple-element.37), channel_id=1, source_target_pairs={{0,6},{1,7},{2,4},{3,5},{4,2},{5,3},{6,0},{7,1},{8,14},{9,15},{10,... | collective-permute-start | bytes 393224 | tf_op jit(solution)/shard_map/ppermute | solution.py:259
  39.3 2.9 %collective-permute-start.3 = (bf16[128,512]{1,0:T(8,128)(2,1)S(1)}, bf16[128,512]{1,0:T(8,128)(2,1)S(1)}, u32[]{:S(2)}, u32[]{:S(2)}) collective-permute-start(bf16[128,512]{1,0:T(8,128)(2,1)S(1)} %get-tuple-element.38), channel_id=1, source_target_pairs={{0,4},{1,5},{2,6},{3,7},{4,0},{5,1},{6,2},{7,3},{8,12},{9,13},{10,... | collective-permute-start | bytes 393224 | tf_op jit(solution)/shard_map/ppermute | solution.py:259
  42.2 3.6 %shard_map.109 = (bf16[2,64,1024]{2,1,0:T(8,128)(2,1)S(1)}, bf16[2,64,1024]{2,1,0:T(8,128)(2,1)S(1)}, bf16[2,64,1024]{2,1,0:T(8,128)(2,1)S(1)}, bf16[2,64,1024]{2,1,0:T(8,128)(2,1)S(1)}) custom-call(s32[5]{0:T(128)S(1)} %stack.32.pos_ref, bf16[2,64,1024]{2,1,0:T(8,128)(2,1)S(1)} %pad_maximum_fusion.b0, bf16[2,64,1024]{2,1,0:T(8,128)(2,1)S(1)} %collective-permute-done.8.b1, ...), custom_call_target="tpu_custom_call" | custom-call | tf_op jit(solution)/shard_map/pallas_call | solution.py:270
  45.9 1.7 %collective-permute-start.12 = (bf16[2,64,1024]{2,1,0:T(8,128)(2,1)S(1)}, bf16[2,64,1024]{2,1,0:T(8,128)(2,1)S(1)}, u32[]{:S(2)}, u32[]{:S(2)}) collective-permute-start(bf16[2,64,1024]{2,1,0:T(8,128)(2,1)S(1)} %get-tuple-element.49), channel_id=1, source_target_pairs={{0,16},{8,24},{16,0},{24,8},{32,48},{40,56},{48,32},{56,40},{64,80... | collective-permute-start | bytes 786440 | tf_op jit(solution)/shard_map/ppermute | solution.py:259
  47.5 2.2 %collective-permute-start.13 = (bf16[2,64,1024]{2,1,0:T(8,128)(2,1)S(1)}, bf16[2,64,1024]{2,1,0:T(8,128)(2,1)S(1)}, u32[]{:S(2)}, u32[]{:S(2)}) collective-permute-start(bf16[2,64,1024]{2,1,0:T(8,128)(2,1)S(1)} %get-tuple-element.50), channel_id=1, source_target_pairs={{0,48},{8,56},{16,32},{24,40},{32,16},{40,24},{48,0},{56,8},{64,11... | collective-permute-start | bytes 786440 | tf_op jit(solution)/shard_map/ppermute | solution.py:259
  51.2 2.6 %collective-permute-start.4 = (bf16[128,512]{1,0:T(8,128)(2,1)S(1)}, bf16[128,512]{1,0:T(8,128)(2,1)S(1)}, u32[]{:S(2)}, u32[]{:S(2)}) collective-permute-start(bf16[128,512]{1,0:T(8,128)(2,1)S(1)} %get-tuple-element.39.gm_ref), channel_id=1, source_target_pairs={{0,8},{8,0},{16,24},{24,16},{32,40},{40,32},{48,56},{56,48},{64,72... | collective-permute-start | bytes 393224 | tf_op jit(solution)/shard_map/ppermute | solution.py:259
  53.9 3.0 %shard_map.105 = (bf16[16,2,128,256]{3,2,1,0:T(8,128)(2,1)S(1)}, bf16[16,256,512]{2,1,0:T(8,128)(2,1)S(1)}, bf16[16,256,512]{2,1,0:T(8,128)(2,1)S(1)}) custom-call(s32[5]{0:T(128)S(1)} %stack.32.pos_ref, s32[16]{0:T(128)S(1)} %copy-done.4, bf16[2,128,512]{2,1,0:T(8,128)(2,1)S(1)} %copy-done.2, bf16[128,512]{1,0:T(8,128)(2,1)S(1)} %copy-done.3), custom_call_target="tpu_custom_call" | custom-call | tf_op jit(solution)/shard_map/pallas_call | solution.py:270
  56.9 8.5 %shard_map.106 = (f32[128,512]{1,0:T(8,128)}, f32[8,32,256]{2,1,0:T(8,128)S(1)}, bf16[8,32,256]{2,1,0:T(8,128)(2,1)S(1)}) custom-call(s32[5]{0:T(128)S(1)} %stack.32.pos_ref, bf16[128,512]{1,0:T(8,128)(2,1)S(1)} %get-tuple-element.39.gm_ref, bf16[128,512]{1,0:T(8,128)(2,1)S(1)} %collective-permute-done.4.gs_ref, ...), custom_call_target="tpu_custom_call" | custom-call | tf_op jit(solution)/shard_map/pallas_call | solution.py:270
  65.4 4.5 %collective-permute-start.16 = (bf16[8,32,256]{2,1,0:T(8,128)(2,1)S(1)}, bf16[8,32,256]{2,1,0:T(8,128)(2,1)S(1)}, u32[]{:S(2)}, u32[]{:S(2)}) collective-permute-start(bf16[8,32,256]{2,1,0:T(8,128)(2,1)S(1)} %get-tuple-element.55), channel_id=1, source_target_pairs={{0,8},{8,0},{16,24},{24,16},{32,40},{40,32},{48,56},{56,48},{64,72... | collective-permute-start | bytes 393224 | tf_op jit(solution)/shard_map/ppermute | solution.py:259
  70.0 3.2 %collective-permute-start.15 = (bf16[64,1024]{1,0:T(8,128)(2,1)S(1)}, bf16[64,1024]{1,0:T(8,128)(2,1)S(1)}, u32[]{:S(2)}, u32[]{:S(2)}) collective-permute-start(bf16[64,1024]{1,0:T(8,128)(2,1)S(1)} %get-tuple-element.53), channel_id=1, source_target_pairs={{0,64},{8,72},{16,80},{24,88},{32,96},{40,104},{48,112},{56,120},{... | collective-permute-start | bytes 393224 | tf_op jit(solution)/shard_map/ppermute | solution.py:259
  73.3 1.2 %collective-permute-start.17 = (bf16[2,32,256]{2,1,0:T(8,128)(2,1)S(1)}, bf16[2,32,256]{2,1,0:T(8,128)(2,1)S(1)}, u32[]{:S(2)}, u32[]{:S(2)}) collective-permute-start(bf16[2,32,256]{2,1,0:T(8,128)(2,1)S(1)} %get-tuple-element.57), channel_id=1, source_target_pairs={{0,16},{8,24},{16,0},{24,8},{32,48},{40,56},{48,32},{56,40},{64,80... | collective-permute-start | bytes 98312 | tf_op jit(solution)/shard_map/ppermute | solution.py:259
  74.4 2.3 %collective-permute-start.18 = (bf16[2,32,256]{2,1,0:T(8,128)(2,1)S(1)}, bf16[2,32,256]{2,1,0:T(8,128)(2,1)S(1)}, u32[]{:S(2)}, u32[]{:S(2)}) collective-permute-start(bf16[2,32,256]{2,1,0:T(8,128)(2,1)S(1)} %get-tuple-element.58), channel_id=1, source_target_pairs={{0,48},{8,56},{16,32},{24,40},{32,16},{40,24},{48,0},{56,8},{64,11... | collective-permute-start | bytes 98312 | tf_op jit(solution)/shard_map/ppermute | solution.py:259
  77.4 2.1 %collective-permute-done.18.r3 = bf16[2,32,256]{2,1,0:T(8,128)(2,1)S(1)} collective-permute-done((bf16[2,32,256]{2,1,0:T(8,128)(2,1)S(1)}, bf16[2,32,256]{2,1,0:T(8,128)(2,1)S(1)}, u32[]{:S(2)}, u32[]{:S(2)}) %collective-permute-start.18) | collective-permute-done | bytes 32800 | tf_op jit(solution)/shard_map/ppermute | solution.py:259
  79.5 2.6 %collective-permute-done.19.r2 = bf16[2,32,256]{2,1,0:T(8,128)(2,1)S(1)} collective-permute-done((bf16[2,32,256]{2,1,0:T(8,128)(2,1)S(1)}, bf16[2,32,256]{2,1,0:T(8,128)(2,1)S(1)}, u32[]{:S(2)}, u32[]{:S(2)}) %collective-permute-start.19) | collective-permute-done | bytes 32800 | tf_op jit(solution)/shard_map/ppermute | solution.py:259
  82.2 1.2 %collective-permute-start.20 = (bf16[32,256]{1,0:T(8,128)(2,1)S(1)}, bf16[32,256]{1,0:T(8,128)(2,1)S(1)}, u32[]{:S(2)}, u32[]{:S(2)}) collective-permute-start(bf16[32,256]{1,0:T(8,128)(2,1)S(1)} %get-tuple-element.61), channel_id=1, source_target_pairs={{0,64},{8,72},{16,80},{24,88},{32,96},{40,104},{48,112},{56,120},{... | collective-permute-start | bytes 49160 | tf_op jit(solution)/shard_map/ppermute | solution.py:259
  84.1 3.4 %collective-permute-done.20.got = bf16[32,256]{1,0:T(8,128)(2,1)S(1)} collective-permute-done((bf16[32,256]{1,0:T(8,128)(2,1)S(1)}, bf16[32,256]{1,0:T(8,128)(2,1)S(1)}, u32[]{:S(2)}, u32[]{:S(2)}) %collective-permute-start.20) | collective-permute-done | bytes 16416 | tf_op jit(solution)/shard_map/ppermute | solution.py:259
  87.5 1.4 %shard_map.114 = f32[2,32,128]{2,1,0:T(8,128)} custom-call(s32[5]{0:T(128)S(1)} %stack.32.pos_ref, s32[16]{0:T(128)S(1)} %copy-done.4, f32[32,256]{1,0:T(8,128)S(1)} %get-tuple-element.60.part_ref, bf16[32,256]{1,0:T(8,128)(2,1)S(1)} %collective-permute-done.20.got), custom_call_target="tpu_custom_call" | custom-call | tf_op jit(solution)/shard_map/pallas_call | solution.py:270
  (45 shorter events, 7.1 us)
Async XLA Ops:
  0.6 41.6 %collective-permute-start.11 = (bf16[512,1024]{1,0:T(8,128)(2,1)}, bf16[512,1024]{1,0:T(8,128)(2,1)S(1)}, u32[]{:S(2)}, u32[]{:S(2)}) collective-permute-start(bf16[512,1024]{1,0:T(8,128)(2,1)} %og_hbm.1), channel_id=1, source_target_pairs={{0,8},{8,0},{16,24},{24,16},{32,40},{40,32},{48,56},{56,48},{64,72... | collective-permute-start | bytes 3145736 | tf_op jit(solution)/shard_map/ppermute | solution.py:259
  2.4 51.5 %copy-start.2 = (bf16[2,128,512]{2,1,0:T(8,128)(2,1)S(1)}, bf16[2,128,512]{2,1,0:T(8,128)(2,1)}, u32[]{:S(2)}) copy-start(bf16[2,128,512]{2,1,0:T(8,128)(2,1)} %f_ref.1) | copy-start | bytes 786436
  2.4 51.5 %copy-start.3 = (bf16[128,512]{1,0:T(8,128)(2,1)S(1)}, bf16[128,512]{1,0:T(8,128)(2,1)}, u32[]{:S(2)}) copy-start(bf16[128,512]{1,0:T(8,128)(2,1)} %x_ref.1) | copy-start | bytes 393220
  2.4 51.4 %copy-start.4 = (s32[16]{0:T(128)S(1)}, s32[16]{0:T(128)}, u32[]{:S(2)}) copy-start(s32[16]{0:T(128)} %reach_ref.3) | copy-start | bytes 196
  2.4 6.1 %collective-permute-start.6 = (bf16[64,512]{1,0:T(8,128)(2,1)S(1)}, bf16[64,512]{1,0:T(8,128)(2,1)S(1)}, u32[]{:S(2)}, u32[]{:S(2)}) collective-permute-start(bf16[64,512]{1,0:T(8,128)(2,1)S(1)} %get-tuple-element.46), channel_id=1, source_target_pairs={{0,8},{8,0},{16,24},{24,16},{32,40},{40,32},{48,56},{56,48},{64,72... | collective-permute-start | bytes 196616 | tf_op jit(solution)/shard_map/ppermute | solution.py:259
  6.9 21.9 %collective-permute-start = (bf16[512,512]{1,0:T(8,128)(2,1)S(1)}, bf16[512,512]{1,0:T(8,128)(2,1)S(1)}, u32[]{:S(2)}, u32[]{:S(2)}) collective-permute-start(bf16[512,512]{1,0:T(8,128)(2,1)S(1)} %get-tuple-element.34), channel_id=1, source_target_pairs={{0,1},{1,0},{2,3},{3,2},{4,5},{5,4},{6,7},{7,6},{8,9},{9,8},{10,11... | collective-permute-start | bytes 1572872 | tf_op jit(solution)/shard_map/ppermute | solution.py:259
  8.6 15.0 %collective-permute-start.7 = (bf16[64,1024]{1,0:T(8,128)(2,1)S(1)}, bf16[64,1024]{1,0:T(8,128)(2,1)S(1)}, u32[]{:S(2)}, u32[]{:S(2)}) collective-permute-start(bf16[64,1024]{1,0:T(8,128)(2,1)S(1)} %constant_dynamic-update-slice_fusion), channel_id=1, source_target_pairs={{0,1},{1,0},{2,3},{3,2},{4,5},{5,4},{6,7},{7,6},{8,9},{9,8},{10,11... | collective-permute-start | bytes 393224 | tf_op jit(solution)/shard_map/ppermute | solution.py:259
  23.6 11.2 %collective-permute-start.10 = (bf16[2,64,1024]{2,1,0:T(8,128)(2,1)S(1)}, bf16[2,64,1024]{2,1,0:T(8,128)(2,1)S(1)}, u32[]{:S(2)}, u32[]{:S(2)}) collective-permute-start(bf16[2,64,1024]{2,1,0:T(8,128)(2,1)S(1)} %pad_maximum_fusion.b0), channel_id=1, source_target_pairs={{0,4},{1,5},{2,6},{3,7},{4,0},{5,1},{6,2},{7,3},{8,12},{9,13},{10,... | collective-permute-start | bytes 786440 | tf_op jit(solution)/shard_map/ppermute | solution.py:259
  27.7 11.6 %collective-permute-start.9 = (bf16[2,64,1024]{2,1,0:T(8,128)(2,1)S(1)}, bf16[2,64,1024]{2,1,0:T(8,128)(2,1)S(1)}, u32[]{:S(2)}, u32[]{:S(2)}) collective-permute-start(bf16[2,64,1024]{2,1,0:T(8,128)(2,1)S(1)} %pad_maximum_fusion.b0), channel_id=1, source_target_pairs={{0,6},{1,7},{2,4},{3,5},{4,2},{5,3},{6,0},{7,1},{8,14},{9,15},{10,... | collective-permute-start | bytes 786440 | tf_op jit(solution)/shard_map/ppermute | solution.py:259
  28.5 13.8 %collective-permute-start.8 = (bf16[2,64,1024]{2,1,0:T(8,128)(2,1)S(1)}, bf16[2,64,1024]{2,1,0:T(8,128)(2,1)S(1)}, u32[]{:S(2)}, u32[]{:S(2)}) collective-permute-start(bf16[2,64,1024]{2,1,0:T(8,128)(2,1)S(1)} %pad_maximum_fusion.b0), channel_id=1, source_target_pairs={{0,2},{1,3},{2,0},{3,1},{4,6},{5,7},{6,4},{7,5},{8,10},{9,11},{10,... | collective-permute-start | bytes 786440 | tf_op jit(solution)/shard_map/ppermute | solution.py:259
  28.9 20.8 %collective-permute-start.1 = (bf16[128,512]{1,0:T(8,128)(2,1)S(1)}, bf16[128,512]{1,0:T(8,128)(2,1)S(1)}, u32[]{:S(2)}, u32[]{:S(2)}) collective-permute-start(bf16[128,512]{1,0:T(8,128)(2,1)S(1)} %get-tuple-element.36), channel_id=1, source_target_pairs={{0,2},{1,3},{2,0},{3,1},{4,6},{5,7},{6,4},{7,5},{8,10},{9,11},{10,... | collective-permute-start | bytes 393224 | tf_op jit(solution)/shard_map/ppermute | solution.py:259
  34.8 15.6 %collective-permute-start.2 = (bf16[128,512]{1,0:T(8,128)(2,1)S(1)}, bf16[128,512]{1,0:T(8,128)(2,1)S(1)}, u32[]{:S(2)}, u32[]{:S(2)}) collective-permute-start(bf16[128,512]{1,0:T(8,128)(2,1)S(1)} %get-tuple-element.37), channel_id=1, source_target_pairs={{0,6},{1,7},{2,4},{3,5},{4,2},{5,3},{6,0},{7,1},{8,14},{9,15},{10,... | collective-permute-start | bytes 393224 | tf_op jit(solution)/shard_map/ppermute | solution.py:259
  39.3 11.2 %collective-permute-start.3 = (bf16[128,512]{1,0:T(8,128)(2,1)S(1)}, bf16[128,512]{1,0:T(8,128)(2,1)S(1)}, u32[]{:S(2)}, u32[]{:S(2)}) collective-permute-start(bf16[128,512]{1,0:T(8,128)(2,1)S(1)} %get-tuple-element.38), channel_id=1, source_target_pairs={{0,4},{1,5},{2,6},{3,7},{4,0},{5,1},{6,2},{7,3},{8,12},{9,13},{10,... | collective-permute-start | bytes 393224 | tf_op jit(solution)/shard_map/ppermute | solution.py:259
  45.9 24.0 %collective-permute-start.12 = (bf16[2,64,1024]{2,1,0:T(8,128)(2,1)S(1)}, bf16[2,64,1024]{2,1,0:T(8,128)(2,1)S(1)}, u32[]{:S(2)}, u32[]{:S(2)}) collective-permute-start(bf16[2,64,1024]{2,1,0:T(8,128)(2,1)S(1)} %get-tuple-element.49), channel_id=1, source_target_pairs={{0,16},{8,24},{16,0},{24,8},{32,48},{40,56},{48,32},{56,40},{64,80... | collective-permute-start | bytes 786440 | tf_op jit(solution)/shard_map/ppermute | solution.py:259
  47.5 22.3 %collective-permute-start.13 = (bf16[2,64,1024]{2,1,0:T(8,128)(2,1)S(1)}, bf16[2,64,1024]{2,1,0:T(8,128)(2,1)S(1)}, u32[]{:S(2)}, u32[]{:S(2)}) collective-permute-start(bf16[2,64,1024]{2,1,0:T(8,128)(2,1)S(1)} %get-tuple-element.50), channel_id=1, source_target_pairs={{0,48},{8,56},{16,32},{24,40},{32,16},{40,24},{48,0},{56,8},{64,11... | collective-permute-start | bytes 786440 | tf_op jit(solution)/shard_map/ppermute | solution.py:259
  49.7 20.1 %collective-permute-start.14 = (bf16[2,64,1024]{2,1,0:T(8,128)(2,1)S(1)}, bf16[2,64,1024]{2,1,0:T(8,128)(2,1)S(1)}, u32[]{:S(2)}, u32[]{:S(2)}) collective-permute-start(bf16[2,64,1024]{2,1,0:T(8,128)(2,1)S(1)} %get-tuple-element.51), channel_id=1, source_target_pairs={{0,32},{8,40},{16,48},{24,56},{32,0},{40,8},{48,16},{56,24},{64,96... | collective-permute-start | bytes 786440 | tf_op jit(solution)/shard_map/ppermute | solution.py:259
  50.6 6.3 %collective-permute-start.5 = (bf16[128,512]{1,0:T(8,128)(2,1)S(1)}, bf16[128,512]{1,0:T(8,128)(2,1)S(1)}, u32[]{:S(2)}, u32[]{:S(2)}) collective-permute-start(bf16[128,512]{1,0:T(8,128)(2,1)S(1)} %get-tuple-element.39.gm_ref), channel_id=1, source_target_pairs={{8,16},{24,32},{40,48},{56,64},{72,80},{88,96},{104,112},{16,8},{3... | collective-permute-start | bytes 393224 | tf_op jit(solution)/shard_map/ppermute | solution.py:332
  51.2 5.6 %collective-permute-start.4 = (bf16[128,512]{1,0:T(8,128)(2,1)S(1)}, bf16[128,512]{1,0:T(8,128)(2,1)S(1)}, u32[]{:S(2)}, u32[]{:S(2)}) collective-permute-start(bf16[128,512]{1,0:T(8,128)(2,1)S(1)} %get-tuple-element.39.gm_ref), channel_id=1, source_target_pairs={{0,8},{8,0},{16,24},{24,16},{32,40},{40,32},{48,56},{56,48},{64,72... | collective-permute-start | bytes 393224 | tf_op jit(solution)/shard_map/ppermute | solution.py:259
  65.4 7.8 %collective-permute-start.16 = (bf16[8,32,256]{2,1,0:T(8,128)(2,1)S(1)}, bf16[8,32,256]{2,1,0:T(8,128)(2,1)S(1)}, u32[]{:S(2)}, u32[]{:S(2)}) collective-permute-start(bf16[8,32,256]{2,1,0:T(8,128)(2,1)S(1)} %get-tuple-element.55), channel_id=1, source_target_pairs={{0,8},{8,0},{16,24},{24,16},{32,40},{40,32},{48,56},{56,48},{64,72... | collective-permute-start | bytes 393224 | tf_op jit(solution)/shard_map/ppermute | solution.py:259
  70.0 18.9 %collective-permute-start.15 = (bf16[64,1024]{1,0:T(8,128)(2,1)S(1)}, bf16[64,1024]{1,0:T(8,128)(2,1)S(1)}, u32[]{:S(2)}, u32[]{:S(2)}) collective-permute-start(bf16[64,1024]{1,0:T(8,128)(2,1)S(1)} %get-tuple-element.53), channel_id=1, source_target_pairs={{0,64},{8,72},{16,80},{24,88},{32,96},{40,104},{48,112},{56,120},{... | collective-permute-start | bytes 393224 | tf_op jit(solution)/shard_map/ppermute | solution.py:259
  73.3 4.2 %collective-permute-start.17 = (bf16[2,32,256]{2,1,0:T(8,128)(2,1)S(1)}, bf16[2,32,256]{2,1,0:T(8,128)(2,1)S(1)}, u32[]{:S(2)}, u32[]{:S(2)}) collective-permute-start(bf16[2,32,256]{2,1,0:T(8,128)(2,1)S(1)} %get-tuple-element.57), channel_id=1, source_target_pairs={{0,16},{8,24},{16,0},{24,8},{32,48},{40,56},{48,32},{56,40},{64,80... | collective-permute-start | bytes 98312 | tf_op jit(solution)/shard_map/ppermute | solution.py:259
  74.4 5.1 %collective-permute-start.18 = (bf16[2,32,256]{2,1,0:T(8,128)(2,1)S(1)}, bf16[2,32,256]{2,1,0:T(8,128)(2,1)S(1)}, u32[]{:S(2)}, u32[]{:S(2)}) collective-permute-start(bf16[2,32,256]{2,1,0:T(8,128)(2,1)S(1)} %get-tuple-element.58), channel_id=1, source_target_pairs={{0,48},{8,56},{16,32},{24,40},{32,16},{40,24},{48,0},{56,8},{64,11... | collective-permute-start | bytes 98312 | tf_op jit(solution)/shard_map/ppermute | solution.py:259
  76.7 5.4 %collective-permute-start.19 = (bf16[2,32,256]{2,1,0:T(8,128)(2,1)S(1)}, bf16[2,32,256]{2,1,0:T(8,128)(2,1)S(1)}, u32[]{:S(2)}, u32[]{:S(2)}) collective-permute-start(bf16[2,32,256]{2,1,0:T(8,128)(2,1)S(1)} %get-tuple-element.59), channel_id=1, source_target_pairs={{0,32},{8,40},{16,48},{24,56},{32,0},{40,8},{48,16},{56,24},{64,96... | collective-permute-start | bytes 98312 | tf_op jit(solution)/shard_map/ppermute | solution.py:259
  82.2 5.3 %collective-permute-start.20 = (bf16[32,256]{1,0:T(8,128)(2,1)S(1)}, bf16[32,256]{1,0:T(8,128)(2,1)S(1)}, u32[]{:S(2)}, u32[]{:S(2)}) collective-permute-start(bf16[32,256]{1,0:T(8,128)(2,1)S(1)} %get-tuple-element.61), channel_id=1, source_target_pairs={{0,64},{8,72},{16,80},{24,88},{32,96},{40,104},{48,112},{56,120},{... | collective-permute-start | bytes 49160 | tf_op jit(solution)/shard_map/ppermute | solution.py:259
  (2 other events, 76.1 us)

commit v9 on v8

--- a/solution.py
+++ b/solution.py
@@ -10,7 +10,7 @@
 
 GROUP = 64
 VN = 32
-JOINT = 8
+JOINT = 16
 F32 = jnp.float32
 BF16 = jnp.bfloat16
 
@@ -29,39 +29,31 @@
 RELS = (0, 1, 3, 2)
 
 
-def gate_rows(pos_ref, v_hbm, g_hbm, mine, other, v_ref, g_ref, sems):
-    loads = [
-        pltpu.make_async_copy(v_hbm, v_ref, sems.at[0]),
-        pltpu.make_async_copy(g_hbm, g_ref, sems.at[1]),
-    ]
+def gate_rows(pos_ref, v_hbm, g_hbm, w_hbm, og_hbm, mine, other, w_ref, og_ref, v_ref, g_ref, sems):
+    z = pos_ref[0]
+    x = pos_ref[1]
+    loads = [(v_hbm, v_ref), (g_hbm, g_ref), (og_hbm, og_ref)]
+    for i, rel in enumerate(RELS):
+        for a in range(2):
+            rows = pl.ds(pl.multiple_of(((z ^ rel) * 2 + (x ^ a)) * 128, 128), 128)
+            loads.append((w_hbm.at[rows], w_ref.at[i, 128 * a : 128 * (a + 1)]))
+    loads = [pltpu.make_async_copy(src, dst, sems.at[i]) for i, (src, dst) in enumerate(loads)]
     for load in loads:
         load.start()
-    for load in loads:
-        load.wait()
+    loads[0].wait()
+    loads[1].wait()
     half = mine.shape[0]
     core = pos_ref[4] & 1
     for ref, part in ((mine, core), (other, 1 - core)):
         band = pl.ds(pl.multiple_of(part * half, half), half)
         ref[...] = (v_ref[band, :].astype(F32) * g_ref[band, :].astype(F32)).astype(BF16)
-
-
-def first_product(pos_ref, w_hbm, og_hbm, keep, send, og_ref, w_ref, sems):
-    z = pos_ref[0]
-    x = pos_ref[1]
-    og_load = pltpu.make_async_copy(og_hbm, og_ref, sems.at[8])
-    og_load.start()
-    loads = []
-    for i, rel in enumerate(RELS):
-        for a in range(2):
-            rows = pl.ds(pl.multiple_of(((z ^ rel) * 2 + (x ^ a)) * 128, 128), 128)
-            part = w_ref.at[i, 128 * a : 128 * (a + 1)]
-            loads.append(pltpu.make_async_copy(w_hbm.at[rows], part, sems.at[2 * i + a]))
-            loads[-1].start()
-    og_load.wait()
+    for load in loads[2:]:
+        load.wait()
+
+
+def first_product(w_ref, og_ref, keep, send):
     og = og_ref[...]
     for i in range(4):
-        loads[2 * i].wait()
-        loads[2 * i + 1].wait()
         p = dot(w_ref[i], og, NT).astype(BF16)
         keep[128 * i : 128 * (i + 1), :] = p[:128]
         send[128 * i : 128 * (i + 1), :] = p[128:]
@@ -288,29 +280,23 @@
     half = rows // 2
     scale = 1.0 / float(tok * seq_count) ** 0.5
 
-    mine, other = call(
+    mine, other, weight, grad_local = call(
         gate_rows,
-        [shape((half, tok), BF16)] * 2,
-        (pos, conv_output, gate_values),
-        scratch=[pltpu.VMEM((rows, tok), BF16)] * 2 + [pltpu.SemaphoreType.DMA((2,))],
+        [shape((half, tok), BF16)] * 2
+        + [shape((4, 2 * rows, feats), BF16), shape((tok, feats), BF16)],
+        (pos, conv_output, gate_values, out_weight, out_grad),
+        scratch=[pltpu.VMEM((rows, tok), BF16)] * 2 + [pltpu.SemaphoreType.DMA((11,))],
         held_in=pltpu.HBM,
     )
     own = jnp.concatenate([mine, swap(other, "seq", 1)], axis=1)
-    og_core = swap(out_grad, "seq", 1)
+    og_core = swap(grad_local, "seq", 1)
     pair = jnp.stack([own, swap(own, "chan", 1)])
     b1 = swap(pair, "chan", 2)
     b3 = swap(pair, "chan", 6)
     b2 = swap(pair, "chan", 4)
 
-    keep, send, og_local = call(
-        first_product,
-        [shape((rows * 4, tok), BF16)] * 2 + [shape((tok, feats), BF16)],
-        (pos, out_weight, out_grad),
-        scratch=[
-            pltpu.VMEM((4, 2 * rows, feats), BF16),
-            pltpu.SemaphoreType.DMA((9,)),
-        ],
-        held_in=pltpu.HBM,
+    keep, send = call(
+        first_product, [shape((rows * 4, tok), BF16)] * 2, (weight, grad_local), scalars=0
     )
     keep, s1, s3, s2 = call(
         middle_sums,
@@ -334,7 +320,7 @@
     e = call(
         second_product,
         [shape((2, half, feats), BF16)] * 4,
-        (pos, pair, b1, b3, b2, og_local, og_core),
+        (pos, pair, b1, b3, b2, grad_local, og_core),
         scratch=[pltpu.VMEM((8, half, 2 * tok), BF16)],
     )
     e = [e[0], swap(e[1], "seq", 2), swap(e[2], "seq", 6), swap(e[3], "seq", 4)]

time: 89.7 us -> 87.6 us (0.977)
  Pallas kernels: 23.8 us -> 21.7 us
    pallas_call x13, Pallas kernels: 23.8 us -> 21.7 us  [call(): pl.pallas_call(body, out_shape=out_shape, in_specs=[smem()] * scalars + [...]
  transfers between devices with their start and end apart: 21 -> 21, of which waited for: 6 -> 6; matrix products, arithmetic and copies ran while one was open for 0% -> 0% of each run, Pallas kernels for 26% -> 21%
where the time goes in v9:
time: 87.6 us; the launch traced here: 87.5 us
  starting transfers between devices  37.4 us (43%)
  waiting for transfers between devices  27.4 us (31%)
  Pallas kernels  21.7 us (25%)
    ppermute x20, starting transfers between devices, swap(): lax.ppermute(v, axis, [(i, i ^ mask) for i in range(lax.axis_size(axis))])  36.7 us
    ppermute x20, waiting for transfers between devices, swap(): lax.ppermute(v, axis, [(i, i ^ mask) for i in range(lax.axis_size(axis))])  27.4 us
    pallas_call x13, Pallas kernels, call(): pl.pallas_call(body, out_shape=out_shape, in_specs=[smem()] * scalars + [...  21.7 us
  transfers between devices with their start and end apart: 21, of which 6 were waited for; matrix products, arithmetic and copies ran while one was open for 0% of the time, Pallas kernels for 21%

profile of v9, /device:TPU:0, one launch (start us, length us, event | category | flops | bytes accessed | tf_op | source)
XLA Modules:
  0.0 87.5 jit_solution(12004938484609388696)
XLA Ops:
  0.7 2.6 %shard_map.102 = (bf16[64,512]{1,0:T(8,128)(2,1)S(1)}, bf16[64,512]{1,0:T(8,128)(2,1)S(1)}, bf16[4,256,1024]{2,1,0:T(8,128)(2,1)S(1)}, bf16[512,1024]{1,0:T(8,128)(2,1)S(1)}) custom-call(s32[5]{0:T(128)S(1)} %stack.32.pos_ref, bf16[128,512]{1,0:T(8,128)(2,1)} %v_ref.1, bf16[128,512]{1,0:T(8,128)(2,1)} %g_ref.1, bf16[1024,1024]{1,0:T(8,128)(2,1)} %w_hbm.1, ...), custom_call_target="tpu_custom_call" | custom-call | tf_op jit(solution)/shard_map/pallas_call | solution.py:262
  3.9 1.3 %shard_map.103 = (bf16[512,512]{1,0:T(8,128)(2,1)S(1)}, bf16[512,512]{1,0:T(8,128)(2,1)S(1)}) custom-call(bf16[4,256,1024]{2,1,0:T(8,128)(2,1)S(1)} %get-tuple-element.34.w_ref, bf16[512,1024]{1,0:T(8,128)(2,1)S(1)} %get-tuple-element.35.og_ref), custom_call_target="tpu_custom_call" | custom-call | tf_op jit(solution)/shard_map/pallas_call | solution.py:262
  5.2 1.7 %collective-permute-start = (bf16[512,512]{1,0:T(8,128)(2,1)S(1)}, bf16[512,512]{1,0:T(8,128)(2,1)S(1)}, u32[]{:S(2)}, u32[]{:S(2)}) collective-permute-start(bf16[512,512]{1,0:T(8,128)(2,1)S(1)} %get-tuple-element.37), channel_id=1, source_target_pairs={{0,1},{1,0},{2,3},{3,2},{4,5},{5,4},{6,7},{7,6},{8,9},{9,8},{10,11... | collective-permute-start | bytes 1572872 | tf_op jit(solution)/shard_map/ppermute | solution.py:251
  7.8 14.3 %collective-permute-done.7 = bf16[64,1024]{1,0:T(8,128)(2,1)S(1)} collective-permute-done((bf16[64,1024]{1,0:T(8,128)(2,1)S(1)}, bf16[64,1024]{1,0:T(8,128)(2,1)S(1)}, u32[]{:S(2)}, u32[]{:S(2)}) %collective-permute-start.7) | collective-permute-done | bytes 131104 | tf_op jit(solution)/shard_map/ppermute | solution.py:251
  22.0 4.1 %collective-permute-start.10 = (bf16[2,64,1024]{2,1,0:T(8,128)(2,1)S(1)}, bf16[2,64,1024]{2,1,0:T(8,128)(2,1)S(1)}, u32[]{:S(2)}, u32[]{:S(2)}) collective-permute-start(bf16[2,64,1024]{2,1,0:T(8,128)(2,1)S(1)} %pad_maximum_fusion.b0), channel_id=1, source_target_pairs={{0,4},{1,5},{2,6},{3,7},{4,0},{5,1},{6,2},{7,3},{8,12},{9,13},{10,... | collective-permute-start | bytes 786440 | tf_op jit(solution)/shard_map/ppermute | solution.py:251
  27.3 1.8 %collective-permute-start.1 = (bf16[128,512]{1,0:T(8,128)(2,1)S(1)}, bf16[128,512]{1,0:T(8,128)(2,1)S(1)}, u32[]{:S(2)}, u32[]{:S(2)}) collective-permute-start(bf16[128,512]{1,0:T(8,128)(2,1)S(1)} %get-tuple-element.39), channel_id=1, source_target_pairs={{0,2},{1,3},{2,0},{3,1},{4,6},{5,7},{6,4},{7,5},{8,10},{9,11},{10,... | collective-permute-start | bytes 393224 | tf_op jit(solution)/shard_map/ppermute | solution.py:251
  29.1 4.2 %collective-permute-done.10.b2 = bf16[2,64,1024]{2,1,0:T(8,128)(2,1)S(1)} collective-permute-done((bf16[2,64,1024]{2,1,0:T(8,128)(2,1)S(1)}, bf16[2,64,1024]{2,1,0:T(8,128)(2,1)S(1)}, u32[]{:S(2)}, u32[]{:S(2)}) %collective-permute-start.10) | collective-permute-done | bytes 262176 | tf_op jit(solution)/shard_map/ppermute | solution.py:251
  33.3 3.7 %collective-permute-start.2 = (bf16[128,512]{1,0:T(8,128)(2,1)S(1)}, bf16[128,512]{1,0:T(8,128)(2,1)S(1)}, u32[]{:S(2)}, u32[]{:S(2)}) collective-permute-start(bf16[128,512]{1,0:T(8,128)(2,1)S(1)} %get-tuple-element.40), channel_id=1, source_target_pairs={{0,6},{1,7},{2,4},{3,5},{4,2},{5,3},{6,0},{7,1},{8,14},{9,15},{10,... | collective-permute-start | bytes 393224 | tf_op jit(solution)/shard_map/ppermute | solution.py:251
  37.7 3.1 %collective-permute-start.3 = (bf16[128,512]{1,0:T(8,128)(2,1)S(1)}, bf16[128,512]{1,0:T(8,128)(2,1)S(1)}, u32[]{:S(2)}, u32[]{:S(2)}) collective-permute-start(bf16[128,512]{1,0:T(8,128)(2,1)S(1)} %get-tuple-element.41), channel_id=1, source_target_pairs={{0,4},{1,5},{2,6},{3,7},{4,0},{5,1},{6,2},{7,3},{8,12},{9,13},{10,... | collective-permute-start | bytes 393224 | tf_op jit(solution)/shard_map/ppermute | solution.py:251
  40.8 3.7 %shard_map.109 = (bf16[2,64,1024]{2,1,0:T(8,128)(2,1)S(1)}, bf16[2,64,1024]{2,1,0:T(8,128)(2,1)S(1)}, bf16[2,64,1024]{2,1,0:T(8,128)(2,1)S(1)}, bf16[2,64,1024]{2,1,0:T(8,128)(2,1)S(1)}) custom-call(s32[5]{0:T(128)S(1)} %stack.32.pos_ref, bf16[2,64,1024]{2,1,0:T(8,128)(2,1)S(1)} %pad_maximum_fusion.b0, bf16[2,64,1024]{2,1,0:T(8,128)(2,1)S(1)} %collective-permute-done.8.b1, ...), custom_call_target="tpu_custom_call" | custom-call | tf_op jit(solution)/shard_map/pallas_call | solution.py:262
  44.5 1.7 %collective-permute-start.12 = (bf16[2,64,1024]{2,1,0:T(8,128)(2,1)S(1)}, bf16[2,64,1024]{2,1,0:T(8,128)(2,1)S(1)}, u32[]{:S(2)}, u32[]{:S(2)}) collective-permute-start(bf16[2,64,1024]{2,1,0:T(8,128)(2,1)S(1)} %get-tuple-element.51), channel_id=1, source_target_pairs={{0,16},{8,24},{16,0},{24,8},{32,48},{40,56},{48,32},{56,40},{64,80... | collective-permute-start | bytes 786440 | tf_op jit(solution)/shard_map/ppermute | solution.py:251
  46.1 2.2 %collective-permute-start.13 = (bf16[2,64,1024]{2,1,0:T(8,128)(2,1)S(1)}, bf16[2,64,1024]{2,1,0:T(8,128)(2,1)S(1)}, u32[]{:S(2)}, u32[]{:S(2)}) collective-permute-start(bf16[2,64,1024]{2,1,0:T(8,128)(2,1)S(1)} %get-tuple-element.52), channel_id=1, source_target_pairs={{0,48},{8,56},{16,32},{24,40},{32,16},{40,24},{48,0},{56,8},{64,11... | collective-permute-start | bytes 786440 | tf_op jit(solution)/shard_map/ppermute | solution.py:251
  49.8 2.8 %collective-permute-start.4 = (bf16[128,512]{1,0:T(8,128)(2,1)S(1)}, bf16[128,512]{1,0:T(8,128)(2,1)S(1)}, u32[]{:S(2)}, u32[]{:S(2)}) collective-permute-start(bf16[128,512]{1,0:T(8,128)(2,1)S(1)} %get-tuple-element.42.gm_ref), channel_id=1, source_target_pairs={{0,8},{8,0},{16,24},{24,16},{32,40},{40,32},{48,56},{56,48},{64,72... | collective-permute-start | bytes 393224 | tf_op jit(solution)/shard_map/ppermute | solution.py:251
  52.6 3.0 %shard_map.106 = (bf16[16,2,128,256]{3,2,1,0:T(8,128)(2,1)S(1)}, bf16[16,256,512]{2,1,0:T(8,128)(2,1)S(1)}, bf16[16,256,512]{2,1,0:T(8,128)(2,1)S(1)}) custom-call(s32[5]{0:T(128)S(1)} %stack.32.pos_ref, s32[16]{0:T(128)S(1)} %copy-done.4, bf16[2,128,512]{2,1,0:T(8,128)(2,1)S(1)} %copy-done.2, bf16[128,512]{1,0:T(8,128)(2,1)S(1)} %copy-done.3), custom_call_target="tpu_custom_call" | custom-call | tf_op jit(solution)/shard_map/pallas_call | solution.py:262
  55.7 7.9 %shard_map.107 = (f32[128,512]{1,0:T(8,128)}, f32[8,32,256]{2,1,0:T(8,128)S(1)}, bf16[8,32,256]{2,1,0:T(8,128)(2,1)S(1)}) custom-call(s32[5]{0:T(128)S(1)} %stack.32.pos_ref, bf16[128,512]{1,0:T(8,128)(2,1)S(1)} %get-tuple-element.42.gm_ref, bf16[128,512]{1,0:T(8,128)(2,1)S(1)} %collective-permute-done.4.gs_ref, ...), custom_call_target="tpu_custom_call" | custom-call | tf_op jit(solution)/shard_map/pallas_call | solution.py:262
  63.6 3.5 %collective-permute-start.16 = (bf16[8,32,256]{2,1,0:T(8,128)(2,1)S(1)}, bf16[8,32,256]{2,1,0:T(8,128)(2,1)S(1)}, u32[]{:S(2)}, u32[]{:S(2)}) collective-permute-start(bf16[8,32,256]{2,1,0:T(8,128)(2,1)S(1)} %get-tuple-element.57), channel_id=1, source_target_pairs={{0,8},{8,0},{16,24},{24,16},{32,40},{40,32},{48,56},{56,48},{64,72... | collective-permute-start | bytes 393224 | tf_op jit(solution)/shard_map/ppermute | solution.py:251
  67.3 3.7 %collective-permute-start.15 = (bf16[64,1024]{1,0:T(8,128)(2,1)S(1)}, bf16[64,1024]{1,0:T(8,128)(2,1)S(1)}, u32[]{:S(2)}, u32[]{:S(2)}) collective-permute-start(bf16[64,1024]{1,0:T(8,128)(2,1)S(1)} %get-tuple-element.55), channel_id=1, source_target_pairs={{0,64},{8,72},{16,80},{24,88},{32,96},{40,104},{48,112},{56,120},{... | collective-permute-start | bytes 393224 | tf_op jit(solution)/shard_map/ppermute | solution.py:251
  71.0 1.0 %collective-permute-start.17 = (bf16[2,32,256]{2,1,0:T(8,128)(2,1)S(1)}, bf16[2,32,256]{2,1,0:T(8,128)(2,1)S(1)}, u32[]{:S(2)}, u32[]{:S(2)}) collective-permute-start(bf16[2,32,256]{2,1,0:T(8,128)(2,1)S(1)} %get-tuple-element.59), channel_id=1, source_target_pairs={{0,16},{8,24},{16,0},{24,8},{32,48},{40,56},{48,32},{56,40},{64,80... | collective-permute-start | bytes 98312 | tf_op jit(solution)/shard_map/ppermute | solution.py:251
  72.0 2.5 %collective-permute-start.18 = (bf16[2,32,256]{2,1,0:T(8,128)(2,1)S(1)}, bf16[2,32,256]{2,1,0:T(8,128)(2,1)S(1)}, u32[]{:S(2)}, u32[]{:S(2)}) collective-permute-start(bf16[2,32,256]{2,1,0:T(8,128)(2,1)S(1)} %get-tuple-element.60), channel_id=1, source_target_pairs={{0,48},{8,56},{16,32},{24,40},{32,16},{40,24},{48,0},{56,8},{64,11... | collective-permute-start | bytes 98312 | tf_op jit(solution)/shard_map/ppermute | solution.py:251
  75.2 2.0 %collective-permute-done.18.r3 = bf16[2,32,256]{2,1,0:T(8,128)(2,1)S(1)} collective-permute-done((bf16[2,32,256]{2,1,0:T(8,128)(2,1)S(1)}, bf16[2,32,256]{2,1,0:T(8,128)(2,1)S(1)}, u32[]{:S(2)}, u32[]{:S(2)}) %collective-permute-start.18) | collective-permute-done | bytes 32800 | tf_op jit(solution)/shard_map/ppermute | solution.py:251
  77.2 2.8 %collective-permute-done.19.r2 = bf16[2,32,256]{2,1,0:T(8,128)(2,1)S(1)} collective-permute-done((bf16[2,32,256]{2,1,0:T(8,128)(2,1)S(1)}, bf16[2,32,256]{2,1,0:T(8,128)(2,1)S(1)}, u32[]{:S(2)}, u32[]{:S(2)}) %collective-permute-start.19) | collective-permute-done | bytes 32800 | tf_op jit(solution)/shard_map/ppermute | solution.py:251
  80.0 1.2 %collective-permute-start.20 = (bf16[32,256]{1,0:T(8,128)(2,1)S(1)}, bf16[32,256]{1,0:T(8,128)(2,1)S(1)}, u32[]{:S(2)}, u32[]{:S(2)}) collective-permute-start(bf16[32,256]{1,0:T(8,128)(2,1)S(1)} %get-tuple-element.63), channel_id=1, source_target_pairs={{0,64},{8,72},{16,80},{24,88},{32,96},{40,104},{48,112},{56,120},{... | collective-permute-start | bytes 49160 | tf_op jit(solution)/shard_map/ppermute | solution.py:251
  81.9 3.4 %collective-permute-done.20.got = bf16[32,256]{1,0:T(8,128)(2,1)S(1)} collective-permute-done((bf16[32,256]{1,0:T(8,128)(2,1)S(1)}, bf16[32,256]{1,0:T(8,128)(2,1)S(1)}, u32[]{:S(2)}, u32[]{:S(2)}) %collective-permute-start.20) | collective-permute-done | bytes 16416 | tf_op jit(solution)/shard_map/ppermute | solution.py:251
  85.3 1.4 %shard_map.114 = f32[2,32,128]{2,1,0:T(8,128)} custom-call(s32[5]{0:T(128)S(1)} %stack.32.pos_ref, s32[16]{0:T(128)S(1)} %copy-done.4, f32[32,256]{1,0:T(8,128)S(1)} %get-tuple-element.62.part_ref, bf16[32,256]{1,0:T(8,128)(2,1)S(1)} %collective-permute-done.20.got), custom_call_target="tpu_custom_call" | custom-call | tf_op jit(solution)/shard_map/pallas_call | solution.py:262
  (45 shorter events, 7.2 us)
Async XLA Ops:
  3.3 37.5 %collective-permute-start.11 = (bf16[512,1024]{1,0:T(8,128)(2,1)S(1)}, bf16[512,1024]{1,0:T(8,128)(2,1)S(1)}, u32[]{:S(2)}, u32[]{:S(2)}) collective-permute-start(bf16[512,1024]{1,0:T(8,128)(2,1)S(1)} %get-tuple-element.35.og_ref), channel_id=1, source_target_pairs={{0,8},{8,0},{16,24},{24,16},{32,40},{40,32},{48,56},{56,48},{64,72... | collective-permute-start | bytes 3145736 | tf_op jit(solution)/shard_map/ppermute | solution.py:251
  3.4 3.5 %collective-permute-start.6 = (bf16[64,512]{1,0:T(8,128)(2,1)S(1)}, bf16[64,512]{1,0:T(8,128)(2,1)S(1)}, u32[]{:S(2)}, u32[]{:S(2)}) collective-permute-start(bf16[64,512]{1,0:T(8,128)(2,1)S(1)} %get-tuple-element.49), channel_id=1, source_target_pairs={{0,8},{8,0},{16,24},{24,16},{32,40},{40,32},{48,56},{56,48},{64,72... | collective-permute-start | bytes 196616 | tf_op jit(solution)/shard_map/ppermute | solution.py:251
  5.2 21.9 %collective-permute-start = (bf16[512,512]{1,0:T(8,128)(2,1)S(1)}, bf16[512,512]{1,0:T(8,128)(2,1)S(1)}, u32[]{:S(2)}, u32[]{:S(2)}) collective-permute-start(bf16[512,512]{1,0:T(8,128)(2,1)S(1)} %get-tuple-element.37), channel_id=1, source_target_pairs={{0,1},{1,0},{2,3},{3,2},{4,5},{5,4},{6,7},{7,6},{8,9},{9,8},{10,11... | collective-permute-start | bytes 1572872 | tf_op jit(solution)/shard_map/ppermute | solution.py:251
  6.9 15.1 %collective-permute-start.7 = (bf16[64,1024]{1,0:T(8,128)(2,1)S(1)}, bf16[64,1024]{1,0:T(8,128)(2,1)S(1)}, u32[]{:S(2)}, u32[]{:S(2)}) collective-permute-start(bf16[64,1024]{1,0:T(8,128)(2,1)S(1)} %constant_dynamic-update-slice_fusion), channel_id=1, source_target_pairs={{0,1},{1,0},{2,3},{3,2},{4,5},{5,4},{6,7},{7,6},{8,9},{9,8},{10,11... | collective-permute-start | bytes 393224 | tf_op jit(solution)/shard_map/ppermute | solution.py:251
  22.0 11.2 %collective-permute-start.10 = (bf16[2,64,1024]{2,1,0:T(8,128)(2,1)S(1)}, bf16[2,64,1024]{2,1,0:T(8,128)(2,1)S(1)}, u32[]{:S(2)}, u32[]{:S(2)}) collective-permute-start(bf16[2,64,1024]{2,1,0:T(8,128)(2,1)S(1)} %pad_maximum_fusion.b0), channel_id=1, source_target_pairs={{0,4},{1,5},{2,6},{3,7},{4,0},{5,1},{6,2},{7,3},{8,12},{9,13},{10,... | collective-permute-start | bytes 786440 | tf_op jit(solution)/shard_map/ppermute | solution.py:251
  26.1 11.6 %collective-permute-start.9 = (bf16[2,64,1024]{2,1,0:T(8,128)(2,1)S(1)}, bf16[2,64,1024]{2,1,0:T(8,128)(2,1)S(1)}, u32[]{:S(2)}, u32[]{:S(2)}) collective-permute-start(bf16[2,64,1024]{2,1,0:T(8,128)(2,1)S(1)} %pad_maximum_fusion.b0), channel_id=1, source_target_pairs={{0,6},{1,7},{2,4},{3,5},{4,2},{5,3},{6,0},{7,1},{8,14},{9,15},{10,... | collective-permute-start | bytes 786440 | tf_op jit(solution)/shard_map/ppermute | solution.py:251
  26.8 14.0 %collective-permute-start.8 = (bf16[2,64,1024]{2,1,0:T(8,128)(2,1)S(1)}, bf16[2,64,1024]{2,1,0:T(8,128)(2,1)S(1)}, u32[]{:S(2)}, u32[]{:S(2)}) collective-permute-start(bf16[2,64,1024]{2,1,0:T(8,128)(2,1)S(1)} %pad_maximum_fusion.b0), channel_id=1, source_target_pairs={{0,2},{1,3},{2,0},{3,1},{4,6},{5,7},{6,4},{7,5},{8,10},{9,11},{10,... | collective-permute-start | bytes 786440 | tf_op jit(solution)/shard_map/ppermute | solution.py:251
  27.3 25.4 %copy-start.2 = (bf16[2,128,512]{2,1,0:T(8,128)(2,1)S(1)}, bf16[2,128,512]{2,1,0:T(8,128)(2,1)}, u32[]{:S(2)}) copy-start(bf16[2,128,512]{2,1,0:T(8,128)(2,1)} %f_ref.1) | copy-start | bytes 786436
  27.3 25.3 %copy-start.3 = (bf16[128,512]{1,0:T(8,128)(2,1)S(1)}, bf16[128,512]{1,0:T(8,128)(2,1)}, u32[]{:S(2)}) copy-start(bf16[128,512]{1,0:T(8,128)(2,1)} %x_ref.1) | copy-start | bytes 393220
  27.3 21.0 %collective-permute-start.1 = (bf16[128,512]{1,0:T(8,128)(2,1)S(1)}, bf16[128,512]{1,0:T(8,128)(2,1)S(1)}, u32[]{:S(2)}, u32[]{:S(2)}) collective-permute-start(bf16[128,512]{1,0:T(8,128)(2,1)S(1)} %get-tuple-element.39), channel_id=1, source_target_pairs={{0,2},{1,3},{2,0},{3,1},{4,6},{5,7},{6,4},{7,5},{8,10},{9,11},{10,... | collective-permute-start | bytes 393224 | tf_op jit(solution)/shard_map/ppermute | solution.py:251
  33.3 15.8 %collective-permute-start.2 = (bf16[128,512]{1,0:T(8,128)(2,1)S(1)}, bf16[128,512]{1,0:T(8,128)(2,1)S(1)}, u32[]{:S(2)}, u32[]{:S(2)}) collective-permute-start(bf16[128,512]{1,0:T(8,128)(2,1)S(1)} %get-tuple-element.40), channel_id=1, source_target_pairs={{0,6},{1,7},{2,4},{3,5},{4,2},{5,3},{6,0},{7,1},{8,14},{9,15},{10,... | collective-permute-start | bytes 393224 | tf_op jit(solution)/shard_map/ppermute | solution.py:251
  37.7 11.3 %collective-permute-start.3 = (bf16[128,512]{1,0:T(8,128)(2,1)S(1)}, bf16[128,512]{1,0:T(8,128)(2,1)S(1)}, u32[]{:S(2)}, u32[]{:S(2)}) collective-permute-start(bf16[128,512]{1,0:T(8,128)(2,1)S(1)} %get-tuple-element.41), channel_id=1, source_target_pairs={{0,4},{1,5},{2,6},{3,7},{4,0},{5,1},{6,2},{7,3},{8,12},{9,13},{10,... | collective-permute-start | bytes 393224 | tf_op jit(solution)/shard_map/ppermute | solution.py:251
  44.5 22.7 %collective-permute-start.12 = (bf16[2,64,1024]{2,1,0:T(8,128)(2,1)S(1)}, bf16[2,64,1024]{2,1,0:T(8,128)(2,1)S(1)}, u32[]{:S(2)}, u32[]{:S(2)}) collective-permute-start(bf16[2,64,1024]{2,1,0:T(8,128)(2,1)S(1)} %get-tuple-element.51), channel_id=1, source_target_pairs={{0,16},{8,24},{16,0},{24,8},{32,48},{40,56},{48,32},{56,40},{64,80... | collective-permute-start | bytes 786440 | tf_op jit(solution)/shard_map/ppermute | solution.py:251
  46.1 21.0 %collective-permute-start.13 = (bf16[2,64,1024]{2,1,0:T(8,128)(2,1)S(1)}, bf16[2,64,1024]{2,1,0:T(8,128)(2,1)S(1)}, u32[]{:S(2)}, u32[]{:S(2)}) collective-permute-start(bf16[2,64,1024]{2,1,0:T(8,128)(2,1)S(1)} %get-tuple-element.52), channel_id=1, source_target_pairs={{0,48},{8,56},{16,32},{24,40},{32,16},{40,24},{48,0},{56,8},{64,11... | collective-permute-start | bytes 786440 | tf_op jit(solution)/shard_map/ppermute | solution.py:251
  48.3 18.8 %collective-permute-start.14 = (bf16[2,64,1024]{2,1,0:T(8,128)(2,1)S(1)}, bf16[2,64,1024]{2,1,0:T(8,128)(2,1)S(1)}, u32[]{:S(2)}, u32[]{:S(2)}) collective-permute-start(bf16[2,64,1024]{2,1,0:T(8,128)(2,1)S(1)} %get-tuple-element.53), channel_id=1, source_target_pairs={{0,32},{8,40},{16,48},{24,56},{32,0},{40,8},{48,16},{56,24},{64,96... | collective-permute-start | bytes 786440 | tf_op jit(solution)/shard_map/ppermute | solution.py:251
  49.1 6.5 %collective-permute-start.5 = (bf16[128,512]{1,0:T(8,128)(2,1)S(1)}, bf16[128,512]{1,0:T(8,128)(2,1)S(1)}, u32[]{:S(2)}, u32[]{:S(2)}) collective-permute-start(bf16[128,512]{1,0:T(8,128)(2,1)S(1)} %get-tuple-element.42.gm_ref), channel_id=1, source_target_pairs={{8,16},{24,32},{40,48},{56,64},{72,80},{88,96},{104,112},{16,8},{3... | collective-permute-start | bytes 393224 | tf_op jit(solution)/shard_map/ppermute | solution.py:318
  49.8 5.8 %collective-permute-start.4 = (bf16[128,512]{1,0:T(8,128)(2,1)S(1)}, bf16[128,512]{1,0:T(8,128)(2,1)S(1)}, u32[]{:S(2)}, u32[]{:S(2)}) collective-permute-start(bf16[128,512]{1,0:T(8,128)(2,1)S(1)} %get-tuple-element.42.gm_ref), channel_id=1, source_target_pairs={{0,8},{8,0},{16,24},{24,16},{32,40},{40,32},{48,56},{56,48},{64,72... | collective-permute-start | bytes 393224 | tf_op jit(solution)/shard_map/ppermute | solution.py:251
  55.6 25.6 %copy-start = (bf16[128,512]{1,0:T(8,128)(2,1)S(1)}, bf16[128,512]{1,0:T(8,128)(2,1)}, u32[]{:S(2)}) copy-start(bf16[128,512]{1,0:T(8,128)(2,1)} %v_ref.1) | copy-start | bytes 393220
  63.6 7.4 %collective-permute-start.16 = (bf16[8,32,256]{2,1,0:T(8,128)(2,1)S(1)}, bf16[8,32,256]{2,1,0:T(8,128)(2,1)S(1)}, u32[]{:S(2)}, u32[]{:S(2)}) collective-permute-start(bf16[8,32,256]{2,1,0:T(8,128)(2,1)S(1)} %get-tuple-element.57), channel_id=1, source_target_pairs={{0,8},{8,0},{16,24},{24,16},{32,40},{40,32},{48,56},{56,48},{64,72... | collective-permute-start | bytes 393224 | tf_op jit(solution)/shard_map/ppermute | solution.py:251
  67.3 19.4 %collective-permute-start.15 = (bf16[64,1024]{1,0:T(8,128)(2,1)S(1)}, bf16[64,1024]{1,0:T(8,128)(2,1)S(1)}, u32[]{:S(2)}, u32[]{:S(2)}) collective-permute-start(bf16[64,1024]{1,0:T(8,128)(2,1)S(1)} %get-tuple-element.55), channel_id=1, source_target_pairs={{0,64},{8,72},{16,80},{24,88},{32,96},{40,104},{48,112},{56,120},{... | collective-permute-start | bytes 393224 | tf_op jit(solution)/shard_map/ppermute | solution.py:251
  71.0 4.2 %collective-permute-start.17 = (bf16[2,32,256]{2,1,0:T(8,128)(2,1)S(1)}, bf16[2,32,256]{2,1,0:T(8,128)(2,1)S(1)}, u32[]{:S(2)}, u32[]{:S(2)}) collective-permute-start(bf16[2,32,256]{2,1,0:T(8,128)(2,1)S(1)} %get-tuple-element.59), channel_id=1, source_target_pairs={{0,16},{8,24},{16,0},{24,8},{32,48},{40,56},{48,32},{56,40},{64,80... | collective-permute-start | bytes 98312 | tf_op jit(solution)/shard_map/ppermute | solution.py:251
  72.0 5.1 %collective-permute-start.18 = (bf16[2,32,256]{2,1,0:T(8,128)(2,1)S(1)}, bf16[2,32,256]{2,1,0:T(8,128)(2,1)S(1)}, u32[]{:S(2)}, u32[]{:S(2)}) collective-permute-start(bf16[2,32,256]{2,1,0:T(8,128)(2,1)S(1)} %get-tuple-element.60), channel_id=1, source_target_pairs={{0,48},{8,56},{16,32},{24,40},{32,16},{40,24},{48,0},{56,8},{64,11... | collective-permute-start | bytes 98312 | tf_op jit(solution)/shard_map/ppermute | solution.py:251
  74.6 5.4 %collective-permute-start.19 = (bf16[2,32,256]{2,1,0:T(8,128)(2,1)S(1)}, bf16[2,32,256]{2,1,0:T(8,128)(2,1)S(1)}, u32[]{:S(2)}, u32[]{:S(2)}) collective-permute-start(bf16[2,32,256]{2,1,0:T(8,128)(2,1)S(1)} %get-tuple-element.61), channel_id=1, source_target_pairs={{0,32},{8,40},{16,48},{24,56},{32,0},{40,8},{48,16},{56,24},{64,96... | collective-permute-start | bytes 98312 | tf_op jit(solution)/shard_map/ppermute | solution.py:251
  80.0 5.3 %collective-permute-start.20 = (bf16[32,256]{1,0:T(8,128)(2,1)S(1)}, bf16[32,256]{1,0:T(8,128)(2,1)S(1)}, u32[]{:S(2)}, u32[]{:S(2)}) collective-permute-start(bf16[32,256]{1,0:T(8,128)(2,1)S(1)} %get-tuple-element.63), channel_id=1, source_target_pairs={{0,64},{8,72},{16,80},{24,88},{32,96},{40,104},{48,112},{56,120},{... | collective-permute-start | bytes 49160 | tf_op jit(solution)/shard_map/ppermute | solution.py:251
  (2 other events, 47.2 us)
